TPU v7x, 32 devices: a whole 2x2x4 slice. The times are simulated.
32 devices in a mesh: stream: 4 (over x, core), frames: 8 (over z, y).
Axes of the slice: x: 2, y: 2, z: 4, core: 2. Of those that a mesh axis runs over, the one named last changes fastest.
Arguments:
- inputs: bfloat16 [4096, 4, 1024], P('frames', 'stream'), may hold values from -6 to 6
- context: bfloat16 [4096, 4096], P('frames'), may hold values from -6 to 6
- cotangent: float32 [4096, 4, 1024], P('frames', 'stream'), may hold values from -6 to 6
- live_frames: int32 [32], P('frames'), may hold values from 0 to 128, as said below
- ctx_weight: bfloat16 [4096, 1024], P(None, 'frames'), may hold values from -0.09375 to 0.09375
- norm_gains: float32 [2, 1024], replicated, may hold values from 0.5 to 1.5
- qkv_weight: bfloat16 [4, 2, 1024, 1536], P('stream', None, 'frames'), may hold values from -0.1875 to 0.1875
- out_weight: bfloat16 [4, 2, 1024, 512], P('stream', None, 'frames'), may hold values from -0.25 to 0.25
- gate_up_weight: bfloat16 [4, 2, 1024, 2816], P('stream', None, 'frames'), may hold values from -0.1875 to 0.1875
- down_weight: bfloat16 [4, 2, 1024, 1408], P('stream', None, 'frames'), may hold values from -0.109375 to 0.109375
Outputs:
- result: float32 [4096, 4, 1024], P('frames', 'stream')
- grad_input: float32 [4096, 4, 1024], P('frames', 'stream')
- grad_context: float32 [4096, 4096], P('frames', 'stream')
- grad_ctx_weight: float32 [4096, 1024], P(None, ('stream', 'frames'))
- grad_norm_gains: float32 [2, 1024], P(None, ('stream', 'frames'))
- grad_qkv_weight: float32 [4, 2, 1024, 1536], P('stream', None, 'frames')
- grad_out_weight: float32 [4, 2, 1024, 512], P('stream', None, 'frames')
- grad_gate_up_weight: float32 [4, 2, 1024, 2816], P('stream', None, 'frames')
- grad_down_weight: float32 [4, 2, 1024, 1408], P('stream', None, 'frames')
Inputs may be any that keep to these rules, and one draw needn't show every extreme that they name: `live_frames`: slots form buckets of 24 consecutive slots; each bucket holds one item that fills its first frames, so padding lies only at the end of a bucket (the last slot of all is always padding). Slot 0 is full.
All inputs are finite; a program needn't handle non-finite values.
Results may differ from a plain program's by a relative error of at most 0.015.
Values may be sent and summed in bfloat16 or wider, within the bound.
A program may use at most 256 MiB of HBM per device.

v0:
```python
import jax
import jax.numpy as jnp
from jax import lax
from jax.sharding import PartitionSpec as P

HD = 64
SLOT = 128


norm_eps = 1e-05


def swapped(value, axis, stride):
    mask = 2**stride
    pairs = [(source, source ^ mask) for source in range(lax.axis_size(axis))]
    return lax.ppermute(value, axis, pairs)


def shifted(block, axis, distance):
    devices = range(lax.axis_size(axis))
    route = [(i - distance, i) for i in devices if i - distance in devices]
    return lax.ppermute(block, axis, route)


def norm_scale(values):
    return lax.rsqrt(jnp.mean(values * values, axis=-1, keepdims=True) + norm_eps)


def norm_back(values, scale, gain, grad):
    weighted = grad * gain
    inner_mean = jnp.mean(weighted * values, axis=-1, keepdims=True)
    grad_values = scale * weighted - values * (scale * scale * scale) * inner_mean
    grad_gain = jnp.sum(grad * values * scale, axis=0)
    return (grad_values, grad_gain)


def paired(mine, half_index):
    other = swapped(mine, "stream", 0)
    first = jnp.where(half_index == 0, mine, other)
    second = jnp.where(half_index == 0, other, mine)
    return jnp.stack([first, second], axis=1)


def own_sum(partial_value, half_index):
    mine = jnp.where(half_index == 0, partial_value[:, 0], partial_value[:, 1])
    outgoing = jnp.where(half_index == 0, partial_value[:, 1], partial_value[:, 0])
    return mine + swapped(outgoing, "stream", 0)


def shards(
    inputs,
    context,
    cotangent,
    live_frames,
    ctx_weight,
    norm_gains,
    qkv_weight,
    out_weight,
    gate_up_weight,
    down_weight,
):
    f32 = jnp.float32
    bf16 = jnp.bfloat16
    stream_index = lax.axis_index("stream")
    half_index = stream_index % 2
    user_flag = stream_index // 2
    frame_count = inputs.shape[0]
    offsets = lax.broadcasted_iota(jnp.int32, (frame_count,), 0)
    valid_mask = (offsets % SLOT < jnp.repeat(live_frames, SLOT)).astype(f32)
    ctx_full = lax.all_gather(ctx_weight, "frames", axis=1, tiled=True)
    projected = jnp.dot(context, ctx_full, preferred_element_type=f32)
    resid_in = inputs[:, 0].astype(f32) + projected
    gain_one = norm_gains[0]
    gain_two = norm_gains[1]
    qkv_all, out_all, gate_up_all, down_all = (
        lax.all_gather(qkv_weight, "frames", axis=2, tiled=True),
        lax.all_gather(out_weight, "frames", axis=2, tiled=True),
        lax.all_gather(gate_up_weight, "frames", axis=2, tiled=True),
        lax.all_gather(down_weight, "frames", axis=2, tiled=True),
    )
    qkv_full = qkv_all[0]
    out_full = out_all[0]
    scale_one = norm_scale(resid_in)
    normed_one = (resid_in * scale_one * gain_one).astype(bf16)
    paired_one = paired(normed_one, half_index)
    qkv_rows = jnp.einsum("fpd,pdc->fpc", paired_one, qkv_full, preferred_element_type=f32).astype(
        bf16
    )
    head_width = out_full.shape[2]
    head_count = head_width // HD
    query = qkv_rows[..., :head_width]
    key_rows = qkv_rows[..., head_width : 2 * head_width]
    value_rows = qkv_rows[..., 2 * head_width :]
    far_key, far_value = shifted((key_rows, value_rows), "stream", 2)
    keys_all = jnp.concatenate([far_key, key_rows], axis=1)
    values_all = jnp.concatenate([far_value, value_rows], axis=1)
    query_heads = query.reshape(frame_count, 2, head_count, HD)
    key_heads = keys_all.reshape(frame_count, 4, head_count, HD)
    value_heads = values_all.reshape(frame_count, 4, head_count, HD)
    score_scale = HD ** (-0.5)
    rows = lax.broadcasted_iota(jnp.int32, (2, 4), 0)
    cols = lax.broadcasted_iota(jnp.int32, (2, 4), 1)
    allowed = jnp.where(cols < 2, user_flag == 1, cols - 2 <= rows)
    raw_scores = (
        jnp.einsum("fqhd,fkhd->fhqk", query_heads, key_heads, preferred_element_type=f32)
        * score_scale
    )
    scores = jnp.where(allowed, raw_scores, -1e30)
    top_score = jnp.max(scores, axis=-1, keepdims=True)
    expo = jnp.exp(scores - top_score)
    attn_probs = expo / jnp.sum(expo, axis=-1, keepdims=True)
    probs_low = attn_probs.astype(bf16)
    mixed = jnp.einsum(
        "fhqk,fkhd->fqhd", probs_low, value_heads, preferred_element_type=f32
    ).astype(bf16)
    mixed = mixed.reshape(frame_count, 2, head_width)
    attn_part = jnp.einsum("fpc,pdc->fpd", mixed, out_full, preferred_element_type=f32)
    resid_mid = resid_in + own_sum(attn_part, half_index)
    gate_up_full = gate_up_all[0]
    down_full = down_all[0]
    scale_two = norm_scale(resid_mid)
    normed_two = (resid_mid * scale_two * gain_two).astype(bf16)
    paired_two = paired(normed_two, half_index)
    gate_up = jnp.einsum("fpd,pdc->fpc", paired_two, gate_up_full, preferred_element_type=f32)
    ffn_half = down_full.shape[2]
    gate_part = gate_up[..., :ffn_half]
    up_part = gate_up[..., ffn_half:]
    sigmoid_gate = jax.nn.sigmoid(gate_part)
    activated = gate_part * sigmoid_gate
    hidden = (activated * up_part).astype(bf16)
    ffn_part = jnp.einsum("fpc,pdc->fpd", hidden, down_full, preferred_element_type=f32)
    result = (resid_mid + own_sum(ffn_part, half_index)) * valid_mask[:, None]
    grad_res = cotangent[:, 0] * valid_mask[:, None]
    paired_grad_ffn = paired(grad_res.astype(bf16), half_index)
    grad_hidden = jnp.einsum("fpd,pdc->fpc", paired_grad_ffn, down_full, preferred_element_type=f32)
    grad_down = jnp.einsum("fpd,fpc->pdc", paired_grad_ffn, hidden, preferred_element_type=f32)
    grad_gate = grad_hidden * up_part * (sigmoid_gate * (1.0 + gate_part * (1.0 - sigmoid_gate)))
    grad_up = grad_hidden * activated
    grad_gu_low = jnp.concatenate([grad_gate, grad_up], axis=-1).astype(bf16)
    grad_gate_up = jnp.einsum("fpd,fpc->pdc", paired_two, grad_gu_low, preferred_element_type=f32)
    grad_normed_two = own_sum(
        jnp.einsum("fpc,pdc->fpd", grad_gu_low, gate_up_full, preferred_element_type=f32),
        half_index,
    )
    back_two, grad_gain_two = norm_back(resid_mid, scale_two, gain_two, grad_normed_two)
    grad_mid = grad_res + back_two
    paired_grad_attn = paired(grad_mid.astype(bf16), half_index)
    grad_mixed = jnp.einsum(
        "fpd,pdc->fpc", paired_grad_attn, out_full, preferred_element_type=f32
    ).astype(bf16)
    grad_out = jnp.einsum("fpd,fpc->pdc", paired_grad_attn, mixed, preferred_element_type=f32)
    grad_mixed_heads = grad_mixed.reshape(frame_count, 2, head_count, HD)
    grad_probs = jnp.einsum(
        "fqhd,fkhd->fhqk", grad_mixed_heads, value_heads, preferred_element_type=f32
    )
    grad_value_heads = jnp.einsum(
        "fhqk,fqhd->fkhd", probs_low, grad_mixed_heads, preferred_element_type=f32
    )
    row_total = jnp.sum(grad_probs * attn_probs, axis=-1, keepdims=True)
    grad_scores = (attn_probs * (grad_probs - row_total)).astype(bf16)
    grad_query = (
        jnp.einsum("fhqk,fkhd->fqhd", grad_scores, key_heads, preferred_element_type=f32)
        * score_scale
    )
    grad_key_heads = (
        jnp.einsum("fhqk,fqhd->fkhd", grad_scores, query_heads, preferred_element_type=f32)
        * score_scale
    )
    grad_keys = grad_key_heads.reshape(frame_count, 4, head_width)
    grad_values = grad_value_heads.reshape(frame_count, 4, head_width)
    back_key, back_value = (
        shifted(grad_keys[:, :2].astype(jnp.bfloat16), "stream", -2).astype(jnp.float32),
        shifted(grad_values[:, :2].astype(jnp.bfloat16), "stream", -2).astype(jnp.float32),
    )
    grad_key_own = grad_keys[:, 2:] + back_key
    grad_value_own = grad_values[:, 2:] + back_value
    grad_qkv_low = jnp.concatenate(
        [grad_query.reshape(frame_count, 2, head_width), grad_key_own, grad_value_own], axis=-1
    ).astype(bf16)
    grad_qkv = jnp.einsum("fpd,fpc->pdc", paired_one, grad_qkv_low, preferred_element_type=f32)
    grad_normed_one = own_sum(
        jnp.einsum("fpc,pdc->fpd", grad_qkv_low, qkv_full, preferred_element_type=f32), half_index
    )
    back_one, grad_gain_one = norm_back(resid_in, scale_one, gain_one, grad_normed_one)
    grad_resid = grad_mid + back_one
    sum_qkv, sum_out, sum_gate_up, sum_down = (
        lax.psum_scatter(grad_qkv[None], "frames", scatter_dimension=2, tiled=True),
        lax.psum_scatter(grad_out[None], "frames", scatter_dimension=2, tiled=True),
        lax.psum_scatter(grad_gate_up[None], "frames", scatter_dimension=2, tiled=True),
        lax.psum_scatter(grad_down[None], "frames", scatter_dimension=2, tiled=True),
    )
    grad_ctx_low = grad_resid.astype(bf16)
    ctx_term = jnp.einsum("fc,fd->cd", context, grad_ctx_low, preferred_element_type=f32)
    gain_terms = jnp.stack([grad_gain_one, grad_gain_two])
    sum_ctx, sum_gains = (
        lax.psum_scatter(ctx_term, ("stream", "frames"), scatter_dimension=1, tiled=True),
        lax.psum_scatter(gain_terms, ("stream", "frames"), scatter_dimension=1, tiled=True),
    )
    context_term = jnp.einsum("fd,cd->fc", grad_ctx_low, ctx_full, preferred_element_type=f32)
    sum_context = lax.psum_scatter(
        context_term.astype(jnp.bfloat16), "stream", scatter_dimension=1, tiled=True
    ).astype(jnp.float32)
    return (
        result[:, None],
        grad_resid[:, None],
        sum_context,
        sum_ctx,
        sum_gains,
        sum_qkv,
        sum_out,
        sum_gate_up,
        sum_down,
    )


def solution(mesh):
    placed = (
        P("frames", "stream", None),
        P("frames", None),
        P("frames", "stream", None),
        P("frames"),
        P(None, "frames"),
        P(),
        P("stream", None, "frames", None),
        P("stream", None, "frames", None),
        P("stream", None, "frames", None),
        P("stream", None, "frames", None),
    )
    return jax.shard_map(
        shards,
        mesh=mesh,
        in_specs=placed,
        out_specs=(
            P("frames", "stream", None),
            P("frames", "stream", None),
            P("frames", "stream"),
            P(None, ("stream", "frames")),
            P(None, ("stream", "frames")),
            P("stream", None, "frames", None),
            P("stream", None, "frames", None),
            P("stream", None, "frames", None),
            P("stream", None, "frames", None),
        ),
        check_vma=False,
    )
```

profile of v0, /device:TPU:0, one launch (start us, length us, event | category | flops | bytes accessed | tf_op | source)
XLA Modules:
  0.0 2138.9 jit_solution(12377852825696128908)
XLA Ops:
  10.1 128.1 %all-gather.6.cloned.1.call-done = bf16[4096,1024]{1,0:T(8,128)(2,1)} async-done(((bf16[4096,128]{1,0:T(8,128)(2,1)}), bf16[4096,1024]{1,0:T(8,128)(2,1)}) %all-gather.6.cloned.1.call-update) | async-done | bytes 8388624 | tf_op jit(solution)/shard_map/all_gather | solution.py:70
  138.2 9.4 multiply_reduce_fusion.6
  148.5 2.8 collective-permute-done
  151.3 2.7 select_bitcast_fusion.11
  154.0 83.7 %all-gather.8.cloned.1.call-done = bf16[1,2,1024,1536]{3,2,1,0:T(8,128)(2,1)} async-done(((bf16[1,2,128,1536]{3,2,1,0:T(8,128)(2,1)}), bf16[1,2,1024,1536]{3,2,1,0:T(8,128)(2,1)}) %all-gather.8.cloned.1.call-update) | async-done | bytes 6291472 | tf_op jit(solution)/shard_map/all_gather | solution.py:76
  237.6 6.5 fusion.25
  245.9 4.3 collective-permute-start.2
  251.9 3.8 copy.66
  258.1 15.1 collective-permute-done.2
  273.2 3.1 pad_maximum_fusion.8
  276.2 4.1 copy.65
  280.4 7.5 copy.67
  287.9 14.0 fusion.73
  301.9 2.7 pad_maximum_fusion.7
  304.6 4.1 copy.63
  308.8 7.6 copy.68
  316.3 6.5 broadcast_divide_fusion
  324.9 5.6 fusion.28
  330.5 4.8 copy.69
  335.3 3.0 convolution_bitcast_fusion.6
  340.5 2.7 collective-permute-done.3
  348.6 102.9 %all-gather.12.cloned.1.call-done = bf16[1,2,1024,2816]{3,2,1,0:T(8,128)(2,1)} async-done(((bf16[1,2,128,2816]{3,2,1,0:T(8,128)(2,1)}), bf16[1,2,1024,2816]{3,2,1,0:T(8,128)(2,1)}) %all-gather.12.cloned.1.call-update) | async-done | bytes 11534352 | tf_op jit(solution)/shard_map/all_gather | solution.py:78
  451.5 13.4 fusion.5
  464.9 79.5 %all-gather.14.cloned.1.call-done = bf16[1,2,1024,1408]{3,2,1,0:T(8,128)(2,1)} async-done(((bf16[1,2,128,1408]{3,2,1,0:T(8,128)(2,1)}), bf16[1,2,1024,1408]{3,2,1,0:T(8,128)(2,1)}) %all-gather.14.cloned.1.call-update) | async-done | bytes 5767184 | tf_op jit(solution)/shard_map/all_gather | solution.py:79
  544.4 11.1 fusion.13
  555.6 13.5 fusion.36
  569.1 2.8 select_bitcast_fusion.1
  573.0 3.5 fusion.30
  581.3 2.8 fusion.69
  584.2 2.5 collective-permute-done.8
  589.2 6.0 copy.72
  595.3 11.3 multiply_reduce_fusion
  606.5 8.9 convolution_bitcast_fusion.4
  615.5 8.5 copy.81
  624.0 2.7 slice.100
  626.7 3.1 slice.99
  633.4 13.7 multiply_convert_fusion.2
  648.5 7.1 multiply_bitcast_fusion
  655.6 8.5 copy.77
  664.1 2.7 slice.98
  666.8 3.1 slice.97
  673.5 8.7 fusion.29
  682.2 5.9 copy.75
  690.3 2.9 copy.104
  693.2 2.9 copy.102
  702.2 6.0 fusion.33
  708.8 4.1 collective-permute-done.11
  716.5 2.7 subtract_add_fusion
  720.5 9.6 convolution_convert_fusion
  731.6 3.7 convolution_bitcast_fusion.5
  736.8 8.1 convolution_bitcast_fusion.2
  746.8 9.6 convolution_bitcast_fusion.3
  758.0 10.3 convolution_bitcast_fusion.1
  769.6 13.8 convolution_bitcast_fusion
  783.5 5.1 copy.90
  788.5 3.5 copy.91
  792.0 58.0 %reduce-scatter.22.cloned.1.call-done = f32[32,2]{1,0:T(8,128)} async-done(((f32[1024,2]{1,0:T(8,128)}), f32[32,2]{1,0:T(8,128)}) %reduce-scatter.22.cloned.1.call-update) | async-done | bytes 272
  851.3 42.2 %reduce-scatter.10.cloned.1.call-done = bf16[512,1024]{1,0:T(8,128)(2,1)} async-done(((bf16[512,4096]{1,0:T(8,128)(2,1)}), bf16[512,1024]{1,0:T(8,128)(2,1)}) %reduce-scatter.10.cloned.1.call-update) | async-done | bytes 1048592 | tf_op jit(solution)/shard_map/reduce_scatter | solution.py:200
  893.5 2.8 convert_element_type.91
  896.3 89.6 %reduce-scatter.16.cloned.1.call-done = f32[1,2,128,512]{3,2,1,0:T(8,128)} async-done(((f32[1,2,1024,512]{3,2,1,0:T(8,128)}), f32[1,2,128,512]{3,2,1,0:T(8,128)}) %reduce-scatter.16.cloned.1.call-update) | async-done | bytes 524304 | tf_op jit(solution)/shard_map/reduce_scatter | solution.py:188
  985.9 197.1 %reduce-scatter.20.cloned.1.call-done = f32[1,2,128,1408]{3,2,1,0:T(8,128)} async-done(((f32[1,2,1024,1408]{3,2,1,0:T(8,128)}), f32[1,2,128,1408]{3,2,1,0:T(8,128)}) %reduce-scatter.20.cloned.1.call-update) | async-done | bytes 1441808 | tf_op jit(solution)/shard_map/reduce_scatter | solution.py:190
  1183.0 210.8 %reduce-scatter.14.cloned.1.call-done = f32[1,2,128,1536]{3,2,1,0:T(8,128)} async-done(((f32[1,2,1024,1536]{3,2,1,0:T(8,128)}), f32[1,2,128,1536]{3,2,1,0:T(8,128)}) %reduce-scatter.14.cloned.1.call-update) | async-done | bytes 1572880 | tf_op jit(solution)/shard_map/reduce_scatter | solution.py:187
  1393.8 360.2 %reduce-scatter.12.cloned.1.call-done = f32[4096,32]{0,1:T(8,128)} async-done(((f32[4096,1024]{0,1:T(8,128)}), f32[4096,32]{0,1:T(8,128)}) %reduce-scatter.12.cloned.1.call-update) | async-done | bytes 524304 | tf_op jit(solution)/shard_map/reduce_scatter | solution.py:196
  1754.0 377.6 %reduce-scatter.18.cloned.1.call-done = f32[1,2,128,2816]{3,2,1,0:T(8,128)} async-done(((f32[1,2,1024,2816]{3,2,1,0:T(8,128)}), f32[1,2,128,2816]{3,2,1,0:T(8,128)}) %reduce-scatter.18.cloned.1.call-update) | async-done | bytes 2883600 | tf_op jit(solution)/shard_map/reduce_scatter | solution.py:189
  (151 shorter events, 58.6 us)
Async XLA Ops:
  7.2 2.9 copy-start.34
  7.2 131.0 %all-gather.6.cloned.1.call-start = ((), (), s32[]{:S(2)}) async-start(), calls=%async_computation.7 | async-start | bytes 9437184 | tf_op jit(solution)/shard_map/all_gather | solution.py:70
  7.9 229.7 %all-gather.8.cloned.1.call-start = ((), (), s32[]{:S(2)}) async-start(), calls=%async_computation.8 | async-start | bytes 7077888 | tf_op jit(solution)/shard_map/all_gather | solution.py:76
  8.7 326.7 %all-gather.10.cloned.1.call-start = ((), (), s32[]{:S(2)}) async-start(), calls=%async_computation.9 | async-start | bytes 2359296 | tf_op jit(solution)/shard_map/all_gather | solution.py:77
  9.4 442.1 %all-gather.12.cloned.1.call-start = ((), (), s32[]{:S(2)}) async-start(), calls=%async_computation.10 | async-start | bytes 12976128 | tf_op jit(solution)/shard_map/all_gather | solution.py:78
  10.0 534.4 %all-gather.14.cloned.1.call-start = ((), (), s32[]{:S(2)}) async-start(), calls=%async_computation.11 | async-start | bytes 6488064 | tf_op jit(solution)/shard_map/all_gather | solution.py:79
  10.1 141.2 %copy-start.30 = (f32[1,1024]{1,0:T(1,128)}, f32[1,1024]{1,0:T(1,128)S(1)}, u32[]{:S(2)}) copy-start(f32[1,1024]{1,0:T(1,128)S(1)} %get-tuple-element.62) | copy-start | bytes 12292
  148.2 5.8 copy-start.32
  148.4 2.9 collective-permute-start
  154.0 90.2 %copy-start.25 = (bf16[512,1,1024]{2,0,1:T(8,128)(2,1)}, bf16[512,1,1024]{2,0,1:T(8,128)(2,1)S(1)}, u32[]{:S(2)}) copy-start(bf16[512,1,1024]{2,0,1:T(8,128)(2,1)S(1)} %get-tuple-element.59) | copy-start | bytes 3145732
  245.9 27.3 %collective-permute-start.2 = (bf16[512,2,512]{2,0,1:T(8,128)(2,1)}, bf16[512,2,512]{2,0,1:T(8,128)(2,1)}, u32[]{:S(2)}, u32[]{:S(2)}) collective-permute-start(bf16[512,2,512]{2,0,1:T(8,128)(2,1)} %get-tuple-element.49), channel_id=1, source_target_pairs={{0,16},{8,24},{1,17},{9,25},{2,18},{10,26},{3,19},{11,27},{4,20},{... | collective-permute-start | bytes 3145736 | tf_op jit(solution)/shard_map/ppermute | solution.py:22
  250.3 599.7 %reduce-scatter.22.cloned.1.call-start = ((), (), s32[]{:S(2)}) async-start(), calls=%async_computation.18 | async-start | bytes 540672
  255.7 46.2 %collective-permute-start.1 = (bf16[512,2,512]{2,0,1:T(8,128)(2,1)}, bf16[512,2,512]{2,0,1:T(8,128)(2,1)}, u32[]{:S(2)}, u32[]{:S(2)}) collective-permute-start(bf16[512,2,512]{2,0,1:T(8,128)(2,1)} %get-tuple-element.51), channel_id=1, source_target_pairs={{0,16},{8,24},{1,17},{9,25},{2,18},{10,26},{3,19},{11,27},{4,20},{... | collective-permute-start | bytes 3145736 | tf_op jit(solution)/shard_map/ppermute | solution.py:22
  287.9 14.0 copy-start.17
  316.3 8.5 copy-start.14
  322.9 2.0 copy-start.15
  338.4 0.7 copy-start.36
  338.4 1.6 copy-start.2
  339.0 4.2 collective-permute-start.3
  340.4 4.3 collective-permute-start.6
  343.8 3.0 copy-start
  344.1 2.7 collective-permute-start.4
  555.6 16.4 copy-start.18
  569.1 3.9 copy-start.37
  571.9 5.2 collective-permute-start.7
  576.4 1.6 copy-start.1
  576.4 2.8 copy-start.4
  577.0 4.2 copy-start.3
  577.0 4.2 collective-permute-start.5
  584.1 2.8 copy-start.19
  584.1 2.7 collective-permute-start.8
  586.9 2.3 copy-start.10
  586.9 2.3 copy-start.12
  595.3 11.3 copy-start.22
  632.1 64.0 %collective-permute-start.10 = (bf16[512,2,512]{2,0,1:T(8,128)(2,1)}, bf16[512,2,512]{2,0,1:T(8,128)(2,1)}, u32[]{:S(2)}, u32[]{:S(2)}) collective-permute-start(bf16[512,2,512]{2,0,1:T(8,128)(2,1)} %copy.105), channel_id=1, source_target_pairs={{16,0},{24,8},{17,1},{25,9},{18,2},{26,10},{19,3},{27,11},{20,4},{... | collective-permute-start | bytes 3145736 | tf_op jit(solution)/shard_map/ppermute | solution.py:22
  633.4 15.1 copy-start.21
  647.1 1.4 copy-start.20
  672.2 28.4 %collective-permute-start.9 = (bf16[512,2,512]{2,0,1:T(8,128)(2,1)}, bf16[512,2,512]{2,0,1:T(8,128)(2,1)}, u32[]{:S(2)}, u32[]{:S(2)}) collective-permute-start(bf16[512,2,512]{2,0,1:T(8,128)(2,1)} %copy.103), channel_id=1, source_target_pairs={{16,0},{24,8},{17,1},{25,9},{18,2},{26,10},{19,3},{27,11},{20,4},{... | collective-permute-start | bytes 3145736 | tf_op jit(solution)/shard_map/ppermute | solution.py:22
  696.1 4.4 copy-start.5
  698.5 3.7 copy-start.28
  698.5 3.7 copy-start.23
  702.2 6.0 copy-start.29
  708.2 4.8 copy-start.31
  708.2 4.8 copy-start.33
  708.7 7.7 copy-start.35
  708.8 4.2 collective-permute-start.11
  716.2 177.3 %reduce-scatter.10.cloned.1.call-start = ((), (), s32[]{:S(2)}) async-start(), calls=%async_computation.12 | async-start | bytes 5242880 | tf_op jit(solution)/shard_map/reduce_scatter | solution.py:200
  719.2 1.3 copy-start.6
  730.1 1.2 copy-start.11
  730.1 1.5 copy-start.13
  730.1 255.7 %reduce-scatter.16.cloned.1.call-start = ((), (), s32[]{:S(2)}) async-start(), calls=%async_computation.15 | async-start | bytes 4718592 | tf_op jit(solution)/shard_map/reduce_scatter | solution.py:188
  735.3 1.2 copy-start.8
  735.3 1.5 copy-start.9
  735.3 447.6 %reduce-scatter.20.cloned.1.call-start = ((), (), s32[]{:S(2)}) async-start(), calls=%async_computation.17 | async-start | bytes 12976128 | tf_op jit(solution)/shard_map/reduce_scatter | solution.py:190
  745.0 1.2 copy-start.24
  745.0 1.5 copy-start.26
  745.0 1.9 copy-start.27
  745.0 648.8 %reduce-scatter.14.cloned.1.call-start = ((), (), s32[]{:S(2)}) async-start(), calls=%async_computation.14 | async-start | bytes 14155776 | tf_op jit(solution)/shard_map/reduce_scatter | solution.py:187
  756.5 1.6 copy-start.7
  756.5 997.5 %reduce-scatter.12.cloned.1.call-start = ((), (), s32[]{:S(2)}) async-start(), calls=%async_computation.13 | async-start | bytes 17301504 | tf_op jit(solution)/shard_map/reduce_scatter | solution.py:196
  768.4 1.2 copy-start.16
  768.4 1363.3 %reduce-scatter.18.cloned.1.call-start = ((), (), s32[]{:S(2)}) async-start(), calls=%async_computation.16 | async-start | bytes 25952256 | tf_op jit(solution)/shard_map/reduce_scatter | solution.py:189
Sparse Core Ops, SparseCore 0:
  10.1 128.0 all-gather.5
  140.4 97.2 all-gather.7
  239.8 47.4 all-gather.9
  289.3 162.1 all-gather.11
  453.5 90.8 all-gather.13
  716.3 133.6 reduce-scatter.21
  852.7 40.8 reduce-scatter.9
  897.7 88.0 reduce-scatter.15
  990.5 192.4 reduce-scatter.19
  1187.4 206.3 reduce-scatter.13
  1396.8 357.1 reduce-scatter.11
  1758.8 372.7 reduce-scatter.17
where the time goes:
time: 2150 us; the launch traced here: 2140 us
  waiting for transfers between devices  1760 us (82%)
  matrix products  179 us (8%)
  local copies, waits for them, and re-layouts  115 us (5%)
  other arithmetic  54.5 us (3%)
    reduce_scatter x1, waiting for transfers between devices, shards(): lax.psum_scatter(grad_gate_up[None], 'frames', scatter_dimension=2, tiled...  378 us
    reduce_scatter x1, waiting for transfers between devices, shards(): lax.psum_scatter(ctx_term, ('stream', 'frames'), scatter_dimension=1, til...  360 us
    reduce_scatter x1, waiting for transfers between devices, shards(): lax.psum_scatter(grad_qkv[None], 'frames', scatter_dimension=2, tiled=True)  211 us
    reduce_scatter x1, waiting for transfers between devices, shards(): lax.psum_scatter(grad_down[None], 'frames', scatter_dimension=2, tiled=True)  197 us
    all_gather x1, waiting for transfers between devices, shards(): ctx_full = lax.all_gather(ctx_weight, 'frames', axis=1, tiled=True)  128 us
    all_gather x1, waiting for transfers between devices, shards(): lax.all_gather(gate_up_weight, 'frames', axis=2, tiled=True)  103 us
    reduce_scatter x1, waiting for transfers between devices, shards(): lax.psum_scatter(grad_out[None], 'frames', scatter_dimension=2, tiled=True)  89.6 us
    all_gather x1, waiting for transfers between devices, shards(): lax.all_gather(qkv_weight, 'frames', axis=2, tiled=True)  83.7 us
  transfers between devices with their start and end apart: 24, of which 20 were waited for; matrix products, arithmetic and copies ran while one was open for 12% of the time, Pallas kernels for 0%

commit v1 on v0

v1 whole, which is shorter than its diff:
```python
import functools

import jax
import jax.numpy as jnp
from jax import lax
from jax.experimental import pallas as pl
from jax.experimental.pallas import tpu as pltpu
from jax.sharding import PartitionSpec as P

HD = 64
SLOT = 128
LANES = 128
norm_eps = 1e-05
f32 = jnp.float32
bf16 = jnp.bfloat16

PAIRS = [(q, k) for q in range(4) for k in range(q + 1)]


def swap_frames(value, mask):
    n = lax.axis_size("frames")
    return lax.ppermute(value, "frames", [(d, d ^ mask) for d in range(n)])


def swap_stream(value, mask):
    n = lax.axis_size("stream")
    return lax.ppermute(value, "stream", [(d, d ^ mask) for d in range(n)])


def joint(value, target):
    streams, n = lax.axis_size("stream"), lax.axis_size("frames")
    pairs = []
    for s in range(streams):
        for f in range(n):
            to_s, to_f = target(s, f)
            pairs.append((s * n + f, to_s * n + to_f))
    return lax.ppermute(value, ("stream", "frames"), pairs)


def transposed(value):
    def target(s, f):
        core, place = s % 2, (f // 2) % 2
        return s - core + place, f - 2 * place + 2 * core

    return joint(value, target)


def peer(value, mask):
    return joint(value, lambda s, f: (s ^ (mask & 2), f ^ (2 * (mask & 1))))


def norm_scale(values):
    return lax.rsqrt(jnp.mean(values * values, axis=-1, keepdims=True) + norm_eps)


def norm_back(values, scale, gain, grad):
    weighted = grad * gain
    inner_mean = jnp.mean(weighted * values, axis=-1, keepdims=True)
    grad_values = scale * weighted - values * (scale * scale * scale) * inner_mean
    grad_gain = jnp.sum(grad * values * scale, axis=0)
    return (grad_values, grad_gain)


def exchange_rows(qkv, position):
    rows, width = qkv.shape
    quarter = rows // 4
    parts = qkv.reshape(4, quarter, width)
    out = jnp.zeros((4, quarter, width), qkv.dtype)
    own = lax.dynamic_index_in_dim(parts, position, 0, keepdims=False)
    out = lax.dynamic_update_index_in_dim(out, own, position, 0)
    for mask in (2, 1, 3):
        there = position ^ mask
        got = peer(lax.dynamic_index_in_dim(parts, there, 0, keepdims=False), mask)
        out = lax.dynamic_update_index_in_dim(out, got, there, 0)
    return out


def heads_sum(product, fold):
    high = product.astype(bf16)
    low = (product - high.astype(f32)).astype(bf16)
    return jnp.dot(high, fold, preferred_element_type=f32) + jnp.dot(
        low, fold, preferred_element_type=f32
    )


def attention_forward_body(qkv_ref, fold_ref, spread_ref, probs_ref, out_ref):
    width = out_ref.shape[2]
    fold, spread = fold_ref[...], spread_ref[...]
    for q in range(4):
        query = qkv_ref[q, :, :width].astype(f32)
        scores = []
        for k in range(q + 1):
            key = qkv_ref[k, :, width : 2 * width].astype(f32)
            scores.append(heads_sum(query * key, fold) * HD ** (-0.5))
        top = functools.reduce(jnp.maximum, scores)
        expo = [jnp.exp(s - top) for s in scores]
        total = functools.reduce(jnp.add, expo)
        mixed = None
        for k in range(q + 1):
            prob = expo[k] / total
            probs_ref[PAIRS.index((q, k))] = prob
            wide = jnp.dot(prob.astype(bf16), spread, preferred_element_type=f32)
            term = wide * qkv_ref[k, :, 2 * width :].astype(f32)
            mixed = term if mixed is None else mixed + term
        out_ref[q] = mixed.astype(bf16)


def attention_backward_body(qkv_ref, probs_ref, grad_ref, fold_ref, spread_ref, out_ref):
    width = grad_ref.shape[2]
    fold, spread = fold_ref[...], spread_ref[...]
    grad_keys, grad_values = [None] * 4, [None] * 4
    for q in range(4):
        grad = grad_ref[q].astype(f32)
        query = qkv_ref[q, :, :width].astype(f32)
        probs = [probs_ref[PAIRS.index((q, k))] for k in range(q + 1)]
        grad_probs = [
            heads_sum(grad * qkv_ref[k, :, 2 * width :].astype(f32), fold) for k in range(q + 1)
        ]
        total = functools.reduce(jnp.add, [p * g for p, g in zip(probs, grad_probs)])
        grad_query = None
        for k in range(q + 1):
            wide = jnp.dot(probs[k].astype(bf16), spread, preferred_element_type=f32)
            term = wide * grad
            grad_values[k] = term if grad_values[k] is None else grad_values[k] + term
            grad_score = (probs[k] * (grad_probs[k] - total)).astype(bf16)
            wide = jnp.dot(grad_score, spread, preferred_element_type=f32)
            term = wide * qkv_ref[k, :, width : 2 * width].astype(f32)
            grad_query = term if grad_query is None else grad_query + term
            term = wide * query
            grad_keys[k] = term if grad_keys[k] is None else grad_keys[k] + term
        out_ref[q, :, :width] = (grad_query * HD ** (-0.5)).astype(bf16)
    for k in range(4):
        out_ref[k, :, width : 2 * width] = (grad_keys[k] * HD ** (-0.5)).astype(bf16)
        out_ref[k, :, 2 * width :] = grad_values[k].astype(bf16)


def fold_matrices(width):
    feature = lax.broadcasted_iota(jnp.int32, (width, LANES), 0) // HD
    head = lax.broadcasted_iota(jnp.int32, (width, LANES), 1)
    fold = (feature == head).astype(bf16)
    return fold, fold.T


def attention_forward(qkv, step=64):
    _, rows, triple = qkv.shape
    width = triple // 3
    fold, spread = fold_matrices(width)
    return pl.pallas_call(
        attention_forward_body,
        grid=(rows // step,),
        in_specs=[
            pl.BlockSpec((4, step, triple), lambda r: (0, r, 0)),
            pl.BlockSpec((width, LANES), lambda r: (0, 0)),
            pl.BlockSpec((LANES, width), lambda r: (0, 0)),
        ],
        out_specs=[
            pl.BlockSpec((len(PAIRS), step, LANES), lambda r: (0, r, 0)),
            pl.BlockSpec((4, step, width), lambda r: (0, r, 0)),
        ],
        out_shape=[
            jax.ShapeDtypeStruct((len(PAIRS), rows, LANES), f32),
            jax.ShapeDtypeStruct((4, rows, width), bf16),
        ],
        name="attention_forward",
    )(qkv, fold, spread)


def attention_backward(qkv, probs, grad, step=64):
    _, rows, triple = qkv.shape
    width = triple // 3
    fold, spread = fold_matrices(width)
    return pl.pallas_call(
        attention_backward_body,
        grid=(rows // step,),
        in_specs=[
            pl.BlockSpec((4, step, triple), lambda r: (0, r, 0)),
            pl.BlockSpec((len(PAIRS), step, LANES), lambda r: (0, r, 0)),
            pl.BlockSpec((4, step, width), lambda r: (0, r, 0)),
            pl.BlockSpec((width, LANES), lambda r: (0, 0)),
            pl.BlockSpec((LANES, width), lambda r: (0, 0)),
        ],
        out_specs=pl.BlockSpec((4, step, triple), lambda r: (0, r, 0)),
        out_shape=jax.ShapeDtypeStruct((4, rows, triple), bf16),
        name="attention_backward",
    )(qkv, probs, grad, fold, spread)


def gathered(weight, frame_index, place):
    n = lax.axis_size("frames")
    own = lax.dynamic_index_in_dim(weight, place, 0, keepdims=False)
    other = lax.dynamic_index_in_dim(weight, 1 - place, 0, keepdims=False)
    block, width = own.shape
    full = jnp.zeros((n, block, width), own.dtype)
    for mask in range(0, n, 2):
        got = own if mask == 0 else swap_frames(other if mask & 2 else own, mask)
        near = swap_frames(got, 1)
        full = lax.dynamic_update_index_in_dim(full, got, frame_index ^ mask, 0)
        full = lax.dynamic_update_index_in_dim(full, near, frame_index ^ mask ^ 1, 0)
    return full.reshape(n * block, width)


def scattered(left, right, frame_index, place):
    n = lax.axis_size("frames")
    rows, depth = left.shape
    block = depth // n
    near = frame_index % 2
    shaped = left.reshape(rows, n // 2, 2, block)

    def product(which):
        part = lax.dynamic_index_in_dim(shaped, which, 2, keepdims=False).reshape(rows, depth // 2)
        return lax.dot_general(
            part, right, (((0,), (0,)), ((), ())), preferred_element_type=f32
        ).astype(bf16)

    arrived = swap_frames(product(1 - near), 1)
    half_sum = (product(near).astype(f32) + arrived.astype(f32)).astype(bf16)
    half_sum = half_sum.reshape(n // 2, block, -1)
    at = frame_index // 2
    own = lax.dynamic_index_in_dim(half_sum, at, 0, keepdims=False).astype(f32)
    other = None
    for mask in range(2, n, 2):
        got = swap_frames(
            lax.dynamic_index_in_dim(half_sum, at ^ (mask // 2), 0, keepdims=False), mask
        ).astype(f32)
        if mask & 2:
            other = got if other is None else other + got
        else:
            own = own + got
    first = jnp.where(place == 0, own, other)
    second = jnp.where(place == 0, other, own)
    return jnp.stack([first, second], axis=0)


def shards(
    inputs,
    context,
    cotangent,
    live_frames,
    ctx_weight,
    norm_gains,
    qkv_weight,
    out_weight,
    gate_up_weight,
    down_weight,
):
    n = lax.axis_size("frames")
    stream_index = lax.axis_index("stream")
    frame_index = lax.axis_index("frames")
    half_index = stream_index % 2
    place = (frame_index // 2) % 2
    position = (stream_index // 2) * 2 + place
    frame_count = inputs.shape[0]
    width_model = inputs.shape[2]
    offsets = lax.broadcasted_iota(jnp.int32, (frame_count,), 0)
    valid_mask = (offsets % SLOT < jnp.repeat(live_frames, SLOT)).astype(f32)[:, None]
    gain_one = norm_gains[0]
    gain_two = norm_gains[1]

    ctx_rows = ctx_weight.shape[0] // 4
    piece = lax.dynamic_slice_in_dim(ctx_weight, stream_index * ctx_rows, ctx_rows, 0)
    block = piece.shape[1]
    held = piece[None]
    order = [0]
    for bit in reversed(range(1, n.bit_length() - 1)):
        got = swap_frames(held, 1 << bit)
        held = jnp.concatenate([held, got], axis=0)
        order = order + [o ^ (1 << bit) for o in order]
    got = swap_frames(held, 1)
    held = jnp.concatenate([held, got], axis=0)
    order = order + [o ^ 1 for o in order]
    ctx_full = jnp.zeros((ctx_rows, n, block), bf16)
    for at, o in enumerate(order):
        ctx_full = lax.dynamic_update_index_in_dim(ctx_full, held[at], frame_index ^ o, 1)
    ctx_full = ctx_full.reshape(ctx_rows, width_model)
    context_part = lax.dynamic_slice_in_dim(context, stream_index * ctx_rows, ctx_rows, 1)
    projected = jnp.dot(context_part, ctx_full, preferred_element_type=f32)

    def summed(value):
        value = value.astype(f32) + swap_stream(value.astype(bf16), 1).astype(f32)
        half = value.shape[0] // 2
        mine = lax.dynamic_slice_in_dim(value, half_index * half, half, 0)
        mine = (mine + swap_stream(mine.astype(bf16), 2).astype(f32)).astype(bf16)
        far = swap_stream(mine, 1)
        first = jnp.where(half_index == 0, mine, far)
        second = jnp.where(half_index == 0, far, mine)
        return jnp.concatenate([first, second], axis=0)

    resid_home = inputs[:, 0].astype(f32) + summed(projected).astype(f32)
    resid_in = transposed(resid_home.astype(bf16)).astype(f32)
    grad_res = transposed((cotangent[:, 0] * valid_mask).astype(bf16))

    qkv_full = gathered(qkv_weight[0], frame_index, place)
    out_full = gathered(out_weight[0], frame_index, place)
    gate_up_full = gathered(gate_up_weight[0], frame_index, place)
    down_full = gathered(down_weight[0], frame_index, place)

    def paired(mine):
        return jnp.concatenate([mine, swap_stream(mine, 1)], axis=0)

    def own_sum(partial_value):
        return partial_value[:frame_count] + swap_stream(
            partial_value[frame_count:].astype(bf16), 1
        ).astype(f32)

    def rows_times(left, right):
        return jnp.dot(left, right, preferred_element_type=f32)

    def rows_back(left, right):
        return lax.dot_general(left, right, (((1,), (1,)), ((), ())), preferred_element_type=f32)

    scale_one = norm_scale(resid_in)
    paired_one = paired((resid_in * scale_one * gain_one).astype(bf16))
    qkv_rows = rows_times(paired_one, qkv_full).astype(bf16)
    qkv_mixed = exchange_rows(qkv_rows, position)
    probs, mixed_quarter = attention_forward(qkv_mixed)

    def returned(value):
        _, quarter, width = value.shape
        out = jnp.zeros((4, quarter, width), value.dtype)
        own = lax.dynamic_index_in_dim(value, position, 0, keepdims=False)
        out = lax.dynamic_update_index_in_dim(out, own, position, 0)
        for mask in (2, 1, 3):
            there = position ^ mask
            got = peer(lax.dynamic_index_in_dim(value, there, 0, keepdims=False), mask)
            out = lax.dynamic_update_index_in_dim(out, got, there, 0)
        return out.reshape(4 * quarter, width)

    mixed = returned(mixed_quarter)
    resid_mid = resid_in + own_sum(rows_back(mixed, out_full))
    scale_two = norm_scale(resid_mid)
    paired_two = paired((resid_mid * scale_two * gain_two).astype(bf16))
    gate_up = rows_times(paired_two, gate_up_full)
    ffn_half = down_full.shape[1]
    gate_part = gate_up[:, :ffn_half]
    up_part = gate_up[:, ffn_half:]
    sigmoid_gate = jax.nn.sigmoid(gate_part)
    activated = gate_part * sigmoid_gate
    hidden = (activated * up_part).astype(bf16)

    paired_grad_ffn = paired(grad_res)
    sum_down = scattered(paired_grad_ffn, hidden, frame_index, place)
    grad_hidden = rows_times(paired_grad_ffn, down_full)
    grad_gate = grad_hidden * up_part * (sigmoid_gate * (1.0 + gate_part * (1.0 - sigmoid_gate)))
    grad_up = grad_hidden * activated
    grad_gu_low = jnp.concatenate([grad_gate, grad_up], axis=-1).astype(bf16)
    grad_normed_two = own_sum(rows_back(grad_gu_low, gate_up_full))
    sum_gate_up = scattered(paired_two, grad_gu_low, frame_index, place)
    back_two, grad_gain_two = norm_back(resid_mid, scale_two, gain_two, grad_normed_two)
    grad_mid = grad_res.astype(f32) + back_two
    paired_grad_attn = paired(grad_mid.astype(bf16))
    grad_mixed = rows_times(paired_grad_attn, out_full).astype(bf16)
    sum_out = scattered(paired_grad_attn, mixed, frame_index, place)
    grad_qkv_mixed = attention_backward(qkv_mixed, probs, exchange_rows(grad_mixed, position))
    grad_qkv_low = returned(grad_qkv_mixed)
    grad_normed_one = own_sum(rows_back(grad_qkv_low, qkv_full))
    sum_qkv = scattered(paired_one, grad_qkv_low, frame_index, place)
    back_one, grad_gain_one = norm_back(resid_in, scale_one, gain_one, grad_normed_one)
    gain_rows = jnp.pad(jnp.stack([grad_gain_one, grad_gain_two]), ((0, 14), (0, 0)))
    carried = jnp.concatenate([grad_mid + back_one, gain_rows], axis=0).astype(bf16)
    grad_home = transposed(carried)

    ffn_sum = own_sum(rows_back(hidden, down_full))
    result = transposed((resid_mid + ffn_sum).astype(bf16)).astype(f32) * valid_mask

    grad_sum = summed(grad_home)
    grad_ctx_low = grad_sum[:frame_count]
    sum_context = rows_back(grad_ctx_low, ctx_full)
    share = width_model // 4
    grad_share = lax.dynamic_slice_in_dim(grad_sum, stream_index * share, share, 1)
    ctx_term = lax.dot_general(
        grad_share[:frame_count], context, (((0,), (0,)), ((), ())), preferred_element_type=f32
    ).astype(bf16)
    gain_term = jnp.pad(grad_share[frame_count : frame_count + 2].T, ((0, 0), (0, LANES - 2)))
    total = jnp.concatenate([ctx_term, gain_term], axis=1).reshape(n, share // n, -1)
    for bit in range(n.bit_length() - 1):
        shaped = total.reshape((-1, 2) + total.shape[1:])
        at = (frame_index >> bit) % 2
        keep = lax.dynamic_index_in_dim(shaped, at, 1, keepdims=False)
        send = lax.dynamic_index_in_dim(shaped, 1 - at, 1, keepdims=False)
        total = keep.astype(f32) + swap_frames(send.astype(bf16), 1 << bit).astype(f32)
    total = total.reshape(share // n, -1).T
    sum_ctx = total[: ctx_weight.shape[0]]
    sum_gains = total[ctx_weight.shape[0] : ctx_weight.shape[0] + 2]

    return (
        result[:, None],
        grad_home[:frame_count].astype(f32)[:, None],
        sum_context,
        sum_ctx,
        sum_gains,
        sum_qkv[None],
        sum_out[None],
        sum_gate_up[None],
        sum_down[None],
    )


def solution(mesh):
    placed = (
        P("frames", "stream", None),
        P("frames", None),
        P("frames", "stream", None),
        P("frames"),
        P(None, "frames"),
        P(),
        P("stream", None, "frames", None),
        P("stream", None, "frames", None),
        P("stream", None, "frames", None),
        P("stream", None, "frames", None),
    )
    return jax.shard_map(
        shards,
        mesh=mesh,
        in_specs=placed,
        out_specs=(
            P("frames", "stream", None),
            P("frames", "stream", None),
            P("frames", "stream"),
            P(None, ("stream", "frames")),
            P(None, ("stream", "frames")),
            P("stream", None, "frames", None),
            P("stream", None, "frames", None),
            P("stream", None, "frames", None),
            P("stream", None, "frames", None),
        ),
        check_vma=False,
    )
```

time: 2150 us -> 761 us (0.35)
  waiting for transfers between devices: 1760 us -> 270 us
  starting transfers between devices: 11 us -> 172 us
  matrix products: 179 us -> 83.9 us
  local copies, waits for them, and re-layouts: 115 us -> 165 us
    reduce_scatter x6 -> x0, waiting for transfers between devices: 1280 us -> none  [the longest x1 378 us: shards(): lax.psum_scatter(grad_gate_up[None], 'frames', scatter_dimension=2, tiled...]
    all_gather x5 -> x0, waiting for transfers between devices: 394 us -> none  [the longest x1 128 us: shards(): ctx_full = lax.all_gather(ctx_weight, 'frames', axis=1, tiled=True)]
    ppermute x12 -> x80, waiting for transfers between devices: 31.1 us -> 270 us  [the longest x50 193 us: swap_frames(): return lax.ppermute(value, 'frames', [(d, d ^ mask) for d in range(n)])]
    ppermute x12 -> x80, starting transfers between devices: 10.1 us -> 172 us  [the longest x50 97.2 us: swap_frames(): return lax.ppermute(value, 'frames', [(d, d ^ mask) for d in range(n)])]
    dot_general x20 -> x19, matrix products: 165 us -> 83.9 us  [the longest x4 29.6 us: rows_times(): return jnp.dot(left, right, preferred_element_type=f32)]
    unnamed x13 -> x0, waiting for transfers between devices: 60.7 us -> none
    dynamic_update_slice x0 -> x52, local copies, waits for them, and re-layouts: none -> 31 us  [the longest x16 12.5 us: gathered(): full = lax.dynamic_update_index_in_dim(full, got, frame_index ^ mask, 0)]
    dynamic_slice x0 -> x6, local copies, waits for them, and re-layouts: none -> 29.9 us  [the longest x4 29.8 us: product(): lax.dynamic_index_in_dim(shaped, which, 2, keepdims=False)]
  transfers between devices with their start and end apart: 24 -> 80, of which waited for: 20 -> 33; matrix products, arithmetic and copies ran while one was open for 12% -> 33% of each run, Pallas kernels for 0% -> 2%
where the time goes in v1:
time: 761 us; the launch traced here: 751 us
  waiting for transfers between devices  270 us (35%)
  starting transfers between devices  172 us (23%)
  local copies, waits for them, and re-layouts  165 us (22%)
  matrix products  83.9 us (11%)
  other arithmetic  42.4 us (6%)
  Pallas kernels  15.8 us (2%)
    ppermute x50, waiting for transfers between devices, swap_frames(): return lax.ppermute(value, 'frames', [(d, d ^ mask) for d in range(n)])  193 us
    ppermute x50, starting transfers between devices, swap_frames(): return lax.ppermute(value, 'frames', [(d, d ^ mask) for d in range(n)])  97.2 us
    ppermute x16, waiting for transfers between devices, joint(): return lax.ppermute(value, ('stream', 'frames'), pairs)  76.4 us
    unnamed x157, local copies, waits for them, and re-layouts  65.2 us
    ppermute x14, starting transfers between devices, swap_stream(): return lax.ppermute(value, 'stream', [(d, d ^ mask) for d in range(n)])  46.1 us
    dynamic_slice x4, local copies, waits for them, and re-layouts, product(): lax.dynamic_index_in_dim(shaped, which, 2, keepdims=False)  29.8 us
    dot_general x4, matrix products, rows_times(): return jnp.dot(left, right, preferred_element_type=f32)  29.6 us
    ppermute x16, starting transfers between devices, joint(): return lax.ppermute(value, ('stream', 'frames'), pairs)  28.2 us
  transfers between devices with their start and end apart: 80, of which 33 were waited for; matrix products, arithmetic and copies ran while one was open for 33% of the time, Pallas kernels for 2%

profile of v1, /device:TPU:0, one launch (start us, length us, event | category | flops | bytes accessed | tf_op | source)
XLA Modules:
  0.0 751.2 jit_solution(16340573850026507393)
XLA Ops:
  37.6 6.1 collective-permute-start.9
  44.5 4.2 collective-permute-done.27
  53.5 7.5 collective-permute-done.37
  61.0 11.2 %collective-permute-done.38 = bf16[128,1408]{1,0:T(8,128)(2,1)S(1)} collective-permute-done((bf16[128,1408]{1,0:T(8,128)(2,1)S(1)}, bf16[128,1408]{1,0:T(8,128)(2,1)S(1)}, u32[]{:S(2)}, u32[]{:S(2)}) %collective-permute-start.38) | collective-permute-done | bytes 360480 | tf_op jit(solution)/shard_map/ppermute | solution.py:22
  75.4 4.1 collective-permute-start.40
  80.3 14.6 %collective-permute-done.1 = bf16[2,1024,128]{1,2,0:T(8,128)(2,1)S(1)} collective-permute-done((bf16[2,1024,128]{1,2,0:T(8,128)(2,1)S(1)}, bf16[2,1024,128]{1,2,0:T(8,128)(2,1)S(1)}, u32[]{:S(2)}, u32[]{:S(2)}) %collective-permute-start.1) | collective-permute-done | bytes 524320 | tf_op jit(solution)/shard_map/ppermute | solution.py:22
  97.8 21.2 %collective-permute-done.2 = bf16[4,1024,128]{1,2,0:T(8,128)(2,1)S(1)} collective-permute-done((bf16[4,1024,128]{1,2,0:T(8,128)(2,1)S(1)}, bf16[4,1024,128]{1,2,0:T(8,128)(2,1)S(1)}, u32[]{:S(2)}, u32[]{:S(2)}) %collective-permute-start.2) | collective-permute-done | bytes 1048608 | tf_op jit(solution)/shard_map/ppermute | solution.py:22
  133.1 7.0 collective-permute-done.42
  140.1 8.5 %collective-permute-start.33 = (bf16[128,2816]{1,0:T(8,128)(2,1)S(1)}, bf16[128,2816]{1,0:T(8,128)(2,1)}, u32[]{:S(2)}, u32[]{:S(2)}) collective-permute-start(bf16[128,2816]{1,0:T(8,128)(2,1)S(1)} %copy-done.56), channel_id=1, source_target_pairs={{0,4},{1,5},{2,6},{3,7},{4,0},{5,1},{6,2},{7,3},{8,12},{9,13},{10,... | collective-permute-start | bytes 2162696 | tf_op jit(solution)/shard_map/ppermute | solution.py:22
  149.9 8.5 %collective-permute-done.43 = bf16[128,1408]{1,0:T(8,128)(2,1)S(1)} collective-permute-done((bf16[128,1408]{1,0:T(8,128)(2,1)S(1)}, bf16[128,1408]{1,0:T(8,128)(2,1)S(1)}, u32[]{:S(2)}, u32[]{:S(2)}) %collective-permute-start.43) | collective-permute-done | bytes 360480 | tf_op jit(solution)/shard_map/ppermute | solution.py:22
  162.4 9.5 %collective-permute-done.10 = bf16[128,1536]{1,0:T(8,128)(2,1)S(1)} collective-permute-done((bf16[128,1536]{1,0:T(8,128)(2,1)S(1)}, bf16[128,1536]{1,0:T(8,128)(2,1)S(1)}, u32[]{:S(2)}, u32[]{:S(2)}) %collective-permute-start.10) | collective-permute-done | bytes 393248 | tf_op jit(solution)/shard_map/ppermute | solution.py:22
  180.1 27.2 %collective-permute-start.7 = (bf16[512,1024]{1,0:T(8,128)(2,1)S(1)}, bf16[512,1024]{1,0:T(8,128)(2,1)S(1)}, u32[]{:S(2)}, u32[]{:S(2)}) collective-permute-start(bf16[512,1024]{1,0:T(8,128)(2,1)S(1)} %fusion.6), channel_id=1, source_target_pairs={{0,8},{8,0},{16,24},{24,16},{1,9},{9,1},{17,25},{25,17},{2,10},{10... | collective-permute-start | bytes 3145736 | tf_op jit(solution)/shard_map/ppermute | solution.py:27
  211.8 6.4 collective-permute-start.47
  220.4 6.7 convolution_convert_fusion.3
  232.2 15.0 %collective-permute-done.15 = bf16[256,1536]{1,0:T(8,128)(2,1)S(1)} collective-permute-done((bf16[256,1536]{1,0:T(8,128)(2,1)S(1)}, bf16[256,1536]{1,0:T(8,128)(2,1)S(1)}, u32[]{:S(2)}, u32[]{:S(2)}) %collective-permute-start.15) | collective-permute-done | bytes 786464 | tf_op jit(solution)/shard_map/ppermute | solution.py:37
  249.4 17.4 %collective-permute-done.17 = bf16[256,1536]{1,0:T(8,128)(2,1)S(1)} collective-permute-done((bf16[256,1536]{1,0:T(8,128)(2,1)S(1)}, bf16[256,1536]{1,0:T(8,128)(2,1)S(1)}, u32[]{:S(2)}, u32[]{:S(2)}) %collective-permute-start.17) | collective-permute-done | bytes 786464 | tf_op jit(solution)/shard_map/ppermute | solution.py:37
  268.5 7.5 attention_forward.1
  284.8 3.3 collective-permute-done.19
  293.4 3.4 bitcast_dynamic-update-slice_fusion.7
  307.2 6.3 constant_dynamic-slice_fusion
  313.6 5.8 copy.47
  319.4 5.9 copy.46
  328.3 4.8 reshape.216
  333.1 8.6 %constant_dynamic-slice_fusion.7 = (bf16[1024,4,1,128]{3,2,1,0:T(2,128)(2,1)}, bf16[1024,4,1,128]{3,2,1,0:T(2,128)(2,1)}) fusion(bf16[1024,4,2,128]{3,2,1,0:T(2,128)(2,1)} %reshape.216, s32[]{:T(128)S(6)} %select_n.386, s32[]{:T(128)S(6)} %select_n.387), kind=kLoop, calls=%fused_computation.228 | loop fusion | bytes 4194312 | tf_op jit(solution)/shard_map/jit(dynamic_index_in_dim)/dynamic_slice | solution.py:210
  341.7 5.8 copy.40
  347.5 5.8 copy.41
  353.3 12.0 %fusion.57 = f32[1024,2816]{1,0:T(8,128)} fusion(bf16[1024,2816]{1,0:T(8,128)(2,1)} %bitcast.59, bf16[512,1024]{1,0:T(8,128)(2,1)} %collective-permute-done.29, bf16[512,1024]{1,0:T(8,128)(2,1)} %multiply_convert_fusion.3), kind=kOutput, calls=%fused_computation.258 | convolution fusion | flops 5909774336 | bytes 19398656 | tf_op jit(solution)/shard_map/dot_general | solution.py:306
  365.4 8.1 %multiply_convert_fusion.1 = (bf16[1024,1408]{1,0:T(8,128)(2,1)S(1)}, bf16[1024,1408]{1,0:T(8,128)(2,1)S(1)}, bf16[1024,1408]{1,0:T(8,128)(2,1)S(1)}) fusion(f32[1024,2816]{1,0:T(8,128)} %fusion.57, bf16[1024,1024]{1,0:T(8,128)(2,1)S(1)} %copy-done.18, bf16[1024,1408]{1,0:T(8,128)(2,1)S(1)} %bitcast.325), kind=kOutput, calls=%fused_computation.3 | convolution fusion | flops 2974416896 | bytes 25165824 | tf_op jit(solution)/shard_map/dot_general | solution.py:306
  373.6 3.5 convolution_convert_fusion.4
  377.9 8.3 %fusion.18 = f32[1024,1024]{1,0:T(8,128)S(1)} fusion(bf16[1024,2816]{1,0:T(8,128)(2,1)} %bitcast.59, bf16[1024,1408]{1,0:T(8,128)(2,1)S(1)} %get-tuple-element.40, bf16[1024,1408]{1,0:T(8,128)(2,1)S(1)} %get-tuple-element.39), kind=kOutput, calls=%fused_computation.62 | convolution fusion | flops 5917114368 | bytes 15728640 | tf_op jit(solution)/shard_map/dot_general | solution.py:309
  387.5 3.4 fusion.62
  396.8 4.4 reshape.224
  401.2 8.5 %constant_dynamic-slice_fusion.3 = (bf16[1024,4,1,128]{3,2,1,0:T(2,128)(2,1)}, bf16[1024,4,1,128]{3,2,1,0:T(2,128)(2,1)}) fusion(bf16[1024,4,2,128]{3,2,1,0:T(2,128)(2,1)} %reshape.224, s32[]{:T(128)S(6)} %select_n.386, s32[]{:T(128)S(6)} %select_n.387), kind=kLoop, calls=%fused_computation.224 | loop fusion | bytes 4194312 | tf_op jit(solution)/shard_map/jit(dynamic_index_in_dim)/dynamic_slice | solution.py:210
  409.8 5.8 copy.45
  418.8 4.6 fusion.58
  424.9 5.2 convolution_convert_fusion.1
  431.3 4.2 copy.44
  435.6 9.4 %collective-permute-start.45 = (bf16[512,1024]{1,0:T(8,128)(2,1)}, bf16[512,1024]{1,0:T(8,128)(2,1)}, u32[]{:S(2)}, u32[]{:S(2)}) collective-permute-start(bf16[512,1024]{1,0:T(8,128)(2,1)} %get-tuple-element.67), channel_id=1, source_target_pairs={{0,0},{1,1},{2,8},{3,9},{4,4},{5,5},{6,12},{7,13},{8,2},{9,3},{10,... | collective-permute-start | bytes 3145736 | tf_op jit(solution)/shard_map/ppermute | solution.py:37
  445.0 4.3 add_convert_fusion.2
  456.9 11.9 %collective-permute-done.77 = bf16[128,1408]{1,0:T(8,128)(2,1)S(1)} collective-permute-done((bf16[128,1408]{1,0:T(8,128)(2,1)S(1)}, bf16[128,1408]{1,0:T(8,128)(2,1)S(1)}, u32[]{:S(2)}, u32[]{:S(2)}) %collective-permute-start.77) | collective-permute-done | bytes 360480 | tf_op jit(solution)/shard_map/ppermute | solution.py:22
  470.7 6.1 collective-permute-done.79
  478.1 5.1 collective-permute-start.52
  483.3 5.6 collective-permute-done.52
  489.8 8.4 %attention_backward.1 = bf16[4,256,1536]{2,1,0:T(8,128)(2,1)} custom-call(bf16[4,256,1536]{2,1,0:T(8,128)(2,1)} %copy-done.2, f32[10,256,128]{2,1,0:T(8,128)} %get-tuple-element.12.probs_ref, bf16[4,256,512]{2,1,0:T(8,128)(2,1)} %copy-done.21, bf16[512,128]{1,0:T(8,128)(2,1)} %fusion.39.fold_ref, bf16[128,512]{1,0:T(8,128)(2,1)} %fusion.40.spread_ref), custom_call_target="tpu_custom_call" | custom-call | tf_op jit(solution)/shard_map/attention_backward/pallas_call | solution.py:172
  509.5 6.3 constant_dynamic-slice_fusion.4
  515.8 4.6 copy.43
  526.1 15.2 %collective-permute-done.54 = bf16[256,1536]{1,0:T(8,128)(2,1)S(1)} collective-permute-done((bf16[256,1536]{1,0:T(8,128)(2,1)}, bf16[256,1536]{1,0:T(8,128)(2,1)S(1)}, u32[]{:S(2)}, u32[]{:S(2)}) %collective-permute-start.54) | collective-permute-done | bytes 786464 | tf_op jit(solution)/shard_map/ppermute | solution.py:37
  541.3 14.2 %collective-permute-done.55 = bf16[256,1536]{1,0:T(8,128)(2,1)S(1)} collective-permute-done((bf16[256,1536]{1,0:T(8,128)(2,1)}, bf16[256,1536]{1,0:T(8,128)(2,1)S(1)}, u32[]{:S(2)}, u32[]{:S(2)}) %collective-permute-start.55) | collective-permute-done | bytes 786464 | tf_op jit(solution)/shard_map/ppermute | solution.py:37
  555.6 6.5 fusion.63
  565.2 4.6 copy.42
  572.3 4.9 collective-permute-start.69
  580.2 3.5 copy.35
  594.0 5.5 add_convert_fusion
  599.4 9.5 %collective-permute-start.58 = (bf16[528,1024]{1,0:T(8,128)(2,1)S(1)}, bf16[528,1024]{1,0:T(8,128)(2,1)S(1)}, u32[]{:S(2)}, u32[]{:S(2)}) collective-permute-start(bf16[528,1024]{1,0:T(8,128)(2,1)S(1)} %collective-permute-done.57), channel_id=1, source_target_pairs={{0,8},{8,0},{16,24},{24,16},{1,9},{9,1},{17,25},{25,17},{2,10},{10... | collective-permute-start | bytes 3244040 | tf_op jit(solution)/shard_map/ppermute | solution.py:27
  619.1 25.5 %collective-permute-done.73 = bf16[128,2816]{1,0:T(8,128)(2,1)S(1)} collective-permute-done((bf16[128,2816]{1,0:T(8,128)(2,1)S(1)}, bf16[128,2816]{1,0:T(8,128)(2,1)S(1)}, u32[]{:S(2)}, u32[]{:S(2)}) %collective-permute-start.73) | collective-permute-done | bytes 720928 | tf_op jit(solution)/shard_map/ppermute | solution.py:22
  644.6 16.2 %collective-permute-done.75 = bf16[128,2816]{1,0:T(8,128)(2,1)S(1)} collective-permute-done((bf16[128,2816]{1,0:T(8,128)(2,1)S(1)}, bf16[128,2816]{1,0:T(8,128)(2,1)S(1)}, u32[]{:S(2)}, u32[]{:S(2)}) %collective-permute-start.75) | collective-permute-done | bytes 720928 | tf_op jit(solution)/shard_map/ppermute | solution.py:22
  670.2 15.6 %collective-permute-start.65 = (bf16[128,1536]{1,0:T(8,128)(2,1)S(1)}, bf16[128,1536]{1,0:T(8,128)(2,1)S(1)}, u32[]{:S(2)}, u32[]{:S(2)}) collective-permute-start(bf16[128,1536]{1,0:T(8,128)(2,1)S(1)} %get-tuple-element.68), channel_id=1, source_target_pairs={{0,4},{1,5},{2,6},{3,7},{4,0},{5,1},{6,2},{7,3},{8,12},{9,13},{10,... | collective-permute-start | bytes 1179656 | tf_op jit(solution)/shard_map/ppermute | solution.py:22
  689.1 15.1 %collective-permute-done.65 = bf16[128,1536]{1,0:T(8,128)(2,1)S(1)} collective-permute-done((bf16[128,1536]{1,0:T(8,128)(2,1)S(1)}, bf16[128,1536]{1,0:T(8,128)(2,1)S(1)}, u32[]{:S(2)}, u32[]{:S(2)}) %collective-permute-start.65) | collective-permute-done | bytes 393248 | tf_op jit(solution)/shard_map/ppermute | solution.py:22
  704.6 8.9 %collective-permute-done.67 = bf16[128,1536]{1,0:T(8,128)(2,1)S(1)} collective-permute-done((bf16[128,1536]{1,0:T(8,128)(2,1)S(1)}, bf16[128,1536]{1,0:T(8,128)(2,1)S(1)}, u32[]{:S(2)}, u32[]{:S(2)}) %collective-permute-start.67) | collective-permute-done | bytes 393248 | tf_op jit(solution)/shard_map/ppermute | solution.py:22
  714.1 8.1 %collective-permute-start.62 = (bf16[2,32,4224]{2,1,0:T(8,128)(2,1)S(1)}, bf16[2,32,4224]{2,1,0:T(8,128)(2,1)S(1)}, u32[]{:S(2)}, u32[]{:S(2)}) collective-permute-start(bf16[2,32,4224]{2,1,0:T(8,128)(2,1)S(1)} %fusion.30), channel_id=1, source_target_pairs={{0,2},{1,3},{2,0},{3,1},{4,6},{5,7},{6,4},{7,5},{8,10},{9,11},{10,... | collective-permute-start | bytes 1622024 | tf_op jit(solution)/shard_map/ppermute | solution.py:22
  723.7 3.5 copy.36
  727.2 7.5 collective-permute-done.62
  736.3 4.3 fusion.23
  740.6 8.9 %collective-permute-done.63 = bf16[1,32,4224]{2,1,0:T(8,128)(2,1)S(1)} collective-permute-done((bf16[1,32,4224]{2,1,0:T(8,128)(2,1)S(1)}, bf16[1,32,4224]{2,1,0:T(8,128)(2,1)S(1)}, u32[]{:S(2)}, u32[]{:S(2)}) %collective-permute-start.63) | collective-permute-done | bytes 270368 | tf_op jit(solution)/shard_map/ppermute | solution.py:22
  (419 shorter events, 208.9 us)
Async XLA Ops:
  2.9 70.7 %collective-permute-start.8 = (bf16[128,1536]{1,0:T(8,128)(2,1)}, bf16[128,1536]{1,0:T(8,128)(2,1)}, u32[]{:S(2)}, u32[]{:S(2)}) collective-permute-start(bf16[128,1536]{1,0:T(8,128)(2,1)} %get-tuple-element.91), channel_id=1, source_target_pairs={{0,1},{1,0},{2,3},{3,2},{4,5},{5,4},{6,7},{7,6},{8,9},{9,8},{10,11... | collective-permute-start | bytes 1179656 | tf_op jit(solution)/shard_map/ppermute | solution.py:22
  5.9 153.9 %collective-permute-start.11 = (bf16[128,1536]{1,0:T(8,128)(2,1)}, bf16[128,1536]{1,0:T(8,128)(2,1)}, u32[]{:S(2)}, u32[]{:S(2)}) collective-permute-start(bf16[128,1536]{1,0:T(8,128)(2,1)} %get-tuple-element.91), channel_id=1, source_target_pairs={{0,4},{1,5},{2,6},{3,7},{4,0},{5,1},{6,2},{7,3},{8,12},{9,13},{10,... | collective-permute-start | bytes 1179656 | tf_op jit(solution)/shard_map/ppermute | solution.py:22
  10.2 17.7 %collective-permute-start.21 = (bf16[128,512]{1,0:T(8,128)(2,1)}, bf16[128,512]{1,0:T(8,128)(2,1)}, u32[]{:S(2)}, u32[]{:S(2)}) collective-permute-start(bf16[128,512]{1,0:T(8,128)(2,1)} %get-tuple-element.98), channel_id=1, source_target_pairs={{0,1},{1,0},{2,3},{3,2},{4,5},{5,4},{6,7},{7,6},{8,9},{9,8},{10,11... | collective-permute-start | bytes 393224 | tf_op jit(solution)/shard_map/ppermute | solution.py:22
  10.7 24.9 %collective-permute-start.24 = (bf16[128,512]{1,0:T(8,128)(2,1)}, bf16[128,512]{1,0:T(8,128)(2,1)S(1)}, u32[]{:S(2)}, u32[]{:S(2)}) collective-permute-start(bf16[128,512]{1,0:T(8,128)(2,1)} %get-tuple-element.98), channel_id=1, source_target_pairs={{0,4},{1,5},{2,6},{3,7},{4,0},{5,1},{6,2},{7,3},{8,12},{9,13},{10,... | collective-permute-start | bytes 393224 | tf_op jit(solution)/shard_map/ppermute | solution.py:22
  10.7 19.8 %collective-permute-start.22 = (bf16[128,512]{1,0:T(8,128)(2,1)}, bf16[128,512]{1,0:T(8,128)(2,1)}, u32[]{:S(2)}, u32[]{:S(2)}) collective-permute-start(bf16[128,512]{1,0:T(8,128)(2,1)} %get-tuple-element.97), channel_id=1, source_target_pairs={{0,2},{1,3},{2,0},{3,1},{4,6},{5,7},{6,4},{7,5},{8,10},{9,11},{10,... | collective-permute-start | bytes 393224 | tf_op jit(solution)/shard_map/ppermute | solution.py:22
  35.6 16.5 %collective-permute-start = (bf16[1,1024,128]{1,2,0:T(8,128)(2,1)S(1)}, bf16[1,1024,128]{1,2,0:T(8,128)(2,1)S(1)}, u32[]{:S(2)}, u32[]{:S(2)}) collective-permute-start(bf16[1,1024,128]{1,2,0:T(8,128)(2,1)S(1)} %bitcast.316), channel_id=1, source_target_pairs={{0,4},{1,5},{2,6},{3,7},{4,0},{5,1},{6,2},{7,3},{8,12},{9,13},{10,... | collective-permute-start | bytes 786440 | tf_op jit(solution)/shard_map/ppermute | solution.py:22
  37.6 37.8 %collective-permute-start.9 = (bf16[128,1536]{1,0:T(8,128)(2,1)S(1)}, bf16[128,1536]{1,0:T(8,128)(2,1)S(1)}, u32[]{:S(2)}, u32[]{:S(2)}) collective-permute-start(bf16[128,1536]{1,0:T(8,128)(2,1)S(1)} %copy-done.58), channel_id=1, source_target_pairs={{0,2},{1,3},{2,0},{3,1},{4,6},{5,7},{6,4},{7,5},{8,10},{9,11},{10,... | collective-permute-start | bytes 1179656 | tf_op jit(solution)/shard_map/ppermute | solution.py:22
  48.8 126.4 %collective-permute-start.13 = (bf16[128,1536]{1,0:T(8,128)(2,1)S(1)}, bf16[128,1536]{1,0:T(8,128)(2,1)S(1)}, u32[]{:S(2)}, u32[]{:S(2)}) collective-permute-start(bf16[128,1536]{1,0:T(8,128)(2,1)S(1)} %copy-done.58), channel_id=1, source_target_pairs={{0,6},{1,7},{2,4},{3,5},{4,2},{5,3},{6,0},{7,1},{8,14},{9,15},{10,... | collective-permute-start | bytes 1179656 | tf_op jit(solution)/shard_map/ppermute | solution.py:22
  60.9 11.2 %collective-permute-start.38 = (bf16[128,1408]{1,0:T(8,128)(2,1)S(1)}, bf16[128,1408]{1,0:T(8,128)(2,1)S(1)}, u32[]{:S(2)}, u32[]{:S(2)}) collective-permute-start(bf16[128,1408]{1,0:T(8,128)(2,1)S(1)} %copy-done.59), channel_id=1, source_target_pairs={{0,2},{1,3},{2,0},{3,1},{4,6},{5,7},{6,4},{7,5},{8,10},{9,11},{10,... | collective-permute-start | bytes 1081352 | tf_op jit(solution)/shard_map/ppermute | solution.py:22
  72.2 22.9 %collective-permute-start.30 = (bf16[128,2816]{1,0:T(8,128)(2,1)S(1)}, bf16[128,2816]{1,0:T(8,128)(2,1)S(1)}, u32[]{:S(2)}, u32[]{:S(2)}) collective-permute-start(bf16[128,2816]{1,0:T(8,128)(2,1)S(1)} %copy-done.56), channel_id=1, source_target_pairs={{0,1},{1,0},{2,3},{3,2},{4,5},{5,4},{6,7},{7,6},{8,9},{9,8},{10,11... | collective-permute-start | bytes 2162696 | tf_op jit(solution)/shard_map/ppermute | solution.py:22
  73.6 21.4 %collective-permute-start.1 = (bf16[2,1024,128]{1,2,0:T(8,128)(2,1)S(1)}, bf16[2,1024,128]{1,2,0:T(8,128)(2,1)S(1)}, u32[]{:S(2)}, u32[]{:S(2)}) collective-permute-start(bf16[2,1024,128]{1,2,0:T(8,128)(2,1)S(1)} %pad_maximum_fusion.9), channel_id=1, source_target_pairs={{0,2},{1,3},{2,0},{3,1},{4,6},{5,7},{6,4},{7,5},{8,10},{9,11},{10,... | collective-permute-start | bytes 1572872 | tf_op jit(solution)/shard_map/ppermute | solution.py:22
  75.4 51.9 %collective-permute-start.40 = (bf16[128,1408]{1,0:T(8,128)(2,1)S(1)}, bf16[128,1408]{1,0:T(8,128)(2,1)S(1)}, u32[]{:S(2)}, u32[]{:S(2)}) collective-permute-start(bf16[128,1408]{1,0:T(8,128)(2,1)S(1)} %copy-done.60), channel_id=1, source_target_pairs={{0,4},{1,5},{2,6},{3,7},{4,0},{5,1},{6,2},{7,3},{8,12},{9,13},{10,... | collective-permute-start | bytes 1081352 | tf_op jit(solution)/shard_map/ppermute | solution.py:22
  94.9 34.9 %collective-permute-start.31 = (bf16[128,2816]{1,0:T(8,128)(2,1)S(1)}, bf16[128,2816]{1,0:T(8,128)(2,1)S(1)}, u32[]{:S(2)}, u32[]{:S(2)}) collective-permute-start(bf16[128,2816]{1,0:T(8,128)(2,1)S(1)} %copy-done.55), channel_id=1, source_target_pairs={{0,2},{1,3},{2,0},{3,1},{4,6},{5,7},{6,4},{7,5},{8,10},{9,11},{10,... | collective-permute-start | bytes 2162696 | tf_op jit(solution)/shard_map/ppermute | solution.py:22
  95.1 24.0 %collective-permute-start.2 = (bf16[4,1024,128]{1,2,0:T(8,128)(2,1)S(1)}, bf16[4,1024,128]{1,2,0:T(8,128)(2,1)S(1)}, u32[]{:S(2)}, u32[]{:S(2)}) collective-permute-start(bf16[4,1024,128]{1,2,0:T(8,128)(2,1)S(1)} %pad_maximum_fusion.8), channel_id=1, source_target_pairs={{0,1},{1,0},{2,3},{3,2},{4,5},{5,4},{6,7},{7,6},{8,9},{9,8},{10,11... | collective-permute-start | bytes 3145736 | tf_op jit(solution)/shard_map/ppermute | solution.py:22
  127.3 12.8 %collective-permute-start.42 = (bf16[128,1408]{1,0:T(8,128)(2,1)S(1)}, bf16[128,1408]{1,0:T(8,128)(2,1)S(1)}, u32[]{:S(2)}, u32[]{:S(2)}) collective-permute-start(bf16[128,1408]{1,0:T(8,128)(2,1)S(1)} %copy-done.59), channel_id=1, source_target_pairs={{0,6},{1,7},{2,4},{3,5},{4,2},{5,3},{6,0},{7,1},{8,14},{9,15},{10,... | collective-permute-start | bytes 1081352 | tf_op jit(solution)/shard_map/ppermute | solution.py:22
  129.8 18.8 %collective-permute-start.41 = (bf16[128,1408]{1,0:T(8,128)(2,1)S(1)}, bf16[128,1408]{1,0:T(8,128)(2,1)S(1)}, u32[]{:S(2)}, u32[]{:S(2)}) collective-permute-start(bf16[128,1408]{1,0:T(8,128)(2,1)S(1)} %collective-permute-done.40), channel_id=1, source_target_pairs={{0,1},{1,0},{2,3},{3,2},{4,5},{5,4},{6,7},{7,6},{8,9},{9,8},{10,11... | collective-permute-start | bytes 1081352 | tf_op jit(solution)/shard_map/ppermute | solution.py:22
  131.5 18.0 %collective-permute-start.4 = (bf16[256,1024]{1,0:T(8,128)(2,1)S(1)}, bf16[256,1024]{1,0:T(8,128)(2,1)S(1)}, u32[]{:S(2)}, u32[]{:S(2)}) collective-permute-start(bf16[256,1024]{1,0:T(8,128)(2,1)S(1)} %fusion.29), channel_id=1, source_target_pairs={{0,16},{8,24},{16,0},{24,8},{1,17},{9,25},{17,1},{25,9},{2,18},{10... | collective-permute-start | bytes 1572872 | tf_op jit(solution)/shard_map/ppermute | solution.py:27
  140.1 68.0 %collective-permute-start.33 = (bf16[128,2816]{1,0:T(8,128)(2,1)S(1)}, bf16[128,2816]{1,0:T(8,128)(2,1)}, u32[]{:S(2)}, u32[]{:S(2)}) collective-permute-start(bf16[128,2816]{1,0:T(8,128)(2,1)S(1)} %copy-done.56), channel_id=1, source_target_pairs={{0,4},{1,5},{2,6},{3,7},{4,0},{5,1},{6,2},{7,3},{8,12},{9,13},{10,... | collective-permute-start | bytes 2162696 | tf_op jit(solution)/shard_map/ppermute | solution.py:22
  149.8 10.9 %collective-permute-start.5 = (bf16[256,1024]{1,0:T(8,128)(2,1)S(1)}, bf16[256,1024]{1,0:T(8,128)(2,1)S(1)}, u32[]{:S(2)}, u32[]{:S(2)}) collective-permute-start(bf16[256,1024]{1,0:T(8,128)(2,1)S(1)} %add_convert_fusion.4), channel_id=1, source_target_pairs={{0,8},{8,0},{16,24},{24,16},{1,9},{9,1},{17,25},{25,17},{2,10},{10... | collective-permute-start | bytes 1572872 | tf_op jit(solution)/shard_map/ppermute | solution.py:27
  158.4 50.5 %collective-permute-start.35 = (bf16[128,2816]{1,0:T(8,128)(2,1)S(1)}, bf16[128,2816]{1,0:T(8,128)(2,1)}, u32[]{:S(2)}, u32[]{:S(2)}) collective-permute-start(bf16[128,2816]{1,0:T(8,128)(2,1)S(1)} %copy-done.55), channel_id=1, source_target_pairs={{0,6},{1,7},{2,4},{3,5},{4,2},{5,3},{6,0},{7,1},{8,14},{9,15},{10,... | collective-permute-start | bytes 2162696 | tf_op jit(solution)/shard_map/ppermute | solution.py:22
  159.8 12.1 %collective-permute-start.10 = (bf16[128,1536]{1,0:T(8,128)(2,1)S(1)}, bf16[128,1536]{1,0:T(8,128)(2,1)S(1)}, u32[]{:S(2)}, u32[]{:S(2)}) collective-permute-start(bf16[128,1536]{1,0:T(8,128)(2,1)S(1)} %collective-permute-done.9), channel_id=1, source_target_pairs={{0,1},{1,0},{2,3},{3,2},{4,5},{5,4},{6,7},{7,6},{8,9},{9,8},{10,11... | collective-permute-start | bytes 1179656 | tf_op jit(solution)/shard_map/ppermute | solution.py:22
  160.7 17.0 %collective-permute-start.12 = (bf16[128,1536]{1,0:T(8,128)(2,1)}, bf16[128,1536]{1,0:T(8,128)(2,1)S(1)}, u32[]{:S(2)}, u32[]{:S(2)}) collective-permute-start(bf16[128,1536]{1,0:T(8,128)(2,1)} %collective-permute-done.11), channel_id=1, source_target_pairs={{0,1},{1,0},{2,3},{3,2},{4,5},{5,4},{6,7},{7,6},{8,9},{9,8},{10,11... | collective-permute-start | bytes 1179656 | tf_op jit(solution)/shard_map/ppermute | solution.py:22
  175.2 36.6 %collective-permute-start.46 = (bf16[512,1024]{1,0:T(8,128)(2,1)S(1)}, bf16[512,1024]{1,0:T(8,128)(2,1)}, u32[]{:S(2)}, u32[]{:S(2)}) collective-permute-start(bf16[512,1024]{1,0:T(8,128)(2,1)S(1)} %copy-done.53), channel_id=1, source_target_pairs={{0,0},{1,1},{2,8},{3,9},{4,4},{5,5},{6,12},{7,13},{8,2},{9,3},{10,... | collective-permute-start | bytes 3145736 | tf_op jit(solution)/shard_map/ppermute | solution.py:37
  177.7 32.5 %collective-permute-start.14 = (bf16[128,1536]{1,0:T(8,128)(2,1)S(1)}, bf16[128,1536]{1,0:T(8,128)(2,1)S(1)}, u32[]{:S(2)}, u32[]{:S(2)}) collective-permute-start(bf16[128,1536]{1,0:T(8,128)(2,1)S(1)} %collective-permute-done.13), channel_id=1, source_target_pairs={{0,1},{1,0},{2,3},{3,2},{4,5},{5,4},{6,7},{7,6},{8,9},{9,8},{10,11... | collective-permute-start | bytes 1179656 | tf_op jit(solution)/shard_map/ppermute | solution.py:22
  180.1 40.3 %collective-permute-start.7 = (bf16[512,1024]{1,0:T(8,128)(2,1)S(1)}, bf16[512,1024]{1,0:T(8,128)(2,1)S(1)}, u32[]{:S(2)}, u32[]{:S(2)}) collective-permute-start(bf16[512,1024]{1,0:T(8,128)(2,1)S(1)} %fusion.6), channel_id=1, source_target_pairs={{0,8},{8,0},{16,24},{24,16},{1,9},{9,1},{17,25},{25,17},{2,10},{10... | collective-permute-start | bytes 3145736 | tf_op jit(solution)/shard_map/ppermute | solution.py:27
  208.1 21.1 %collective-permute-start.32 = (bf16[128,2816]{1,0:T(8,128)(2,1)S(1)}, bf16[128,2816]{1,0:T(8,128)(2,1)S(1)}, u32[]{:S(2)}, u32[]{:S(2)}) collective-permute-start(bf16[128,2816]{1,0:T(8,128)(2,1)S(1)} %collective-permute-done.31), channel_id=1, source_target_pairs={{0,1},{1,0},{2,3},{3,2},{4,5},{5,4},{6,7},{7,6},{8,9},{9,8},{10,11... | collective-permute-start | bytes 2162696 | tf_op jit(solution)/shard_map/ppermute | solution.py:22
  208.9 70.6 %collective-permute-start.34 = (bf16[128,2816]{1,0:T(8,128)(2,1)}, bf16[128,2816]{1,0:T(8,128)(2,1)}, u32[]{:S(2)}, u32[]{:S(2)}) collective-permute-start(bf16[128,2816]{1,0:T(8,128)(2,1)} %collective-permute-done.33), channel_id=1, source_target_pairs={{0,1},{1,0},{2,3},{3,2},{4,5},{5,4},{6,7},{7,6},{8,9},{9,8},{10,11... | collective-permute-start | bytes 2162696 | tf_op jit(solution)/shard_map/ppermute | solution.py:22
  210.2 86.6 %collective-permute-start.36 = (bf16[128,2816]{1,0:T(8,128)(2,1)}, bf16[128,2816]{1,0:T(8,128)(2,1)}, u32[]{:S(2)}, u32[]{:S(2)}) collective-permute-start(bf16[128,2816]{1,0:T(8,128)(2,1)} %collective-permute-done.35), channel_id=1, source_target_pairs={{0,1},{1,0},{2,3},{3,2},{4,5},{5,4},{6,7},{7,6},{8,9},{9,8},{10,11... | collective-permute-start | bytes 2162696 | tf_op jit(solution)/shard_map/ppermute | solution.py:22
  211.8 87.1 %collective-permute-start.47 = (bf16[512,1024]{1,0:T(8,128)(2,1)}, bf16[512,1024]{1,0:T(8,128)(2,1)}, u32[]{:S(2)}, u32[]{:S(2)}) collective-permute-start(bf16[512,1024]{1,0:T(8,128)(2,1)} %collective-permute-done.46), channel_id=1, source_target_pairs={{0,8},{8,0},{16,24},{24,16},{1,9},{9,1},{17,25},{25,17},{2,10},{10... | collective-permute-start | bytes 3145736 | tf_op jit(solution)/shard_map/ppermute | solution.py:27
  227.7 19.5 %collective-permute-start.15 = (bf16[256,1536]{1,0:T(8,128)(2,1)S(1)}, bf16[256,1536]{1,0:T(8,128)(2,1)S(1)}, u32[]{:S(2)}, u32[]{:S(2)}) collective-permute-start(bf16[256,1536]{1,0:T(8,128)(2,1)S(1)} %get-tuple-element.50), channel_id=1, source_target_pairs={{0,16},{1,17},{2,18},{3,19},{4,20},{5,21},{6,22},{7,23},{8,24},{9,... | collective-permute-start | bytes 2359304 | tf_op jit(solution)/shard_map/ppermute | solution.py:37
  230.2 19.2 %collective-permute-start.16 = (bf16[256,1536]{1,0:T(8,128)(2,1)S(1)}, bf16[256,1536]{1,0:T(8,128)(2,1)S(1)}, u32[]{:S(2)}, u32[]{:S(2)}) collective-permute-start(bf16[256,1536]{1,0:T(8,128)(2,1)S(1)} %get-tuple-element.49), channel_id=1, source_target_pairs={{0,2},{1,3},{2,0},{3,1},{4,6},{5,7},{6,4},{7,5},{8,10},{9,11},{10,... | collective-permute-start | bytes 2359304 | tf_op jit(solution)/shard_map/ppermute | solution.py:37
  247.2 19.6 %collective-permute-start.17 = (bf16[256,1536]{1,0:T(8,128)(2,1)S(1)}, bf16[256,1536]{1,0:T(8,128)(2,1)S(1)}, u32[]{:S(2)}, u32[]{:S(2)}) collective-permute-start(bf16[256,1536]{1,0:T(8,128)(2,1)S(1)} %get-tuple-element.48), channel_id=1, source_target_pairs={{0,18},{1,19},{2,16},{3,17},{4,22},{5,23},{6,20},{7,21},{8,26},{9,... | collective-permute-start | bytes 2359304 | tf_op jit(solution)/shard_map/ppermute | solution.py:37
  306.5 46.8 %collective-permute-start.29 = (bf16[512,1024]{1,0:T(8,128)(2,1)}, bf16[512,1024]{1,0:T(8,128)(2,1)}, u32[]{:S(2)}, u32[]{:S(2)}) collective-permute-start(bf16[512,1024]{1,0:T(8,128)(2,1)} %multiply_convert_fusion.3), channel_id=1, source_target_pairs={{0,8},{8,0},{16,24},{24,16},{1,9},{9,1},{17,25},{25,17},{2,10},{10... | collective-permute-start | bytes 3145736 | tf_op jit(solution)/shard_map/ppermute | solution.py:27
  377.1 67.9 %collective-permute-start.76 = (bf16[512,1408]{1,0:T(8,128)(2,1)}, bf16[512,1408]{1,0:T(8,128)(2,1)}, u32[]{:S(2)}, u32[]{:S(2)}) collective-permute-start(bf16[512,1408]{1,0:T(8,128)(2,1)} %convolution_convert_fusion.4), channel_id=1, source_target_pairs={{0,1},{1,0},{2,3},{3,2},{4,5},{5,4},{6,7},{7,6},{8,9},{9,8},{10,11... | collective-permute-start | bytes 4325384 | tf_op jit(solution)/shard_map/ppermute | solution.py:22
  387.5 28.1 %collective-permute-start.48 = (bf16[512,1024]{1,0:T(8,128)(2,1)}, bf16[512,1024]{1,0:T(8,128)(2,1)}, u32[]{:S(2)}, u32[]{:S(2)}) collective-permute-start(bf16[512,1024]{1,0:T(8,128)(2,1)} %slice.190), channel_id=1, source_target_pairs={{0,8},{8,0},{16,24},{24,16},{1,9},{9,1},{17,25},{25,17},{2,10},{10... | collective-permute-start | bytes 3145736 | tf_op jit(solution)/shard_map/ppermute | solution.py:27
  393.3 25.1 %collective-permute-start.44 = (bf16[512,1024]{1,0:T(8,128)(2,1)}, bf16[512,1024]{1,0:T(8,128)(2,1)}, u32[]{:S(2)}, u32[]{:S(2)}) collective-permute-start(bf16[512,1024]{1,0:T(8,128)(2,1)} %slice.191), channel_id=1, source_target_pairs={{0,8},{8,0},{16,24},{24,16},{1,9},{9,1},{17,25},{25,17},{2,10},{10... | collective-permute-start | bytes 3145736 | tf_op jit(solution)/shard_map/ppermute | solution.py:27
  423.3 28.3 %collective-permute-start.49 = (bf16[512,1024]{1,0:T(8,128)(2,1)}, bf16[512,1024]{1,0:T(8,128)(2,1)}, u32[]{:S(2)}, u32[]{:S(2)}) collective-permute-start(bf16[512,1024]{1,0:T(8,128)(2,1)} %get-tuple-element.35), channel_id=1, source_target_pairs={{0,8},{8,0},{16,24},{24,16},{1,9},{9,1},{17,25},{25,17},{2,10},{10... | collective-permute-start | bytes 3145736 | tf_op jit(solution)/shard_map/ppermute | solution.py:27
  430.1 163.9 %collective-permute-start.72 = (bf16[512,2816]{1,0:T(8,128)(2,1)}, bf16[512,2816]{1,0:T(8,128)(2,1)}, u32[]{:S(2)}, u32[]{:S(2)}) collective-permute-start(bf16[512,2816]{1,0:T(8,128)(2,1)} %convolution_convert_fusion.1), channel_id=1, source_target_pairs={{0,1},{1,0},{2,3},{3,2},{4,5},{5,4},{6,7},{7,6},{8,9},{9,8},{10,11... | collective-permute-start | bytes 8650760 | tf_op jit(solution)/shard_map/ppermute | solution.py:22
  435.6 141.9 %collective-permute-start.45 = (bf16[512,1024]{1,0:T(8,128)(2,1)}, bf16[512,1024]{1,0:T(8,128)(2,1)}, u32[]{:S(2)}, u32[]{:S(2)}) collective-permute-start(bf16[512,1024]{1,0:T(8,128)(2,1)} %get-tuple-element.67), channel_id=1, source_target_pairs={{0,0},{1,1},{2,8},{3,9},{4,4},{5,5},{6,12},{7,13},{8,2},{9,3},{10,... | collective-permute-start | bytes 3145736 | tf_op jit(solution)/shard_map/ppermute | solution.py:37
  449.4 19.4 %collective-permute-start.77 = (bf16[128,1408]{1,0:T(8,128)(2,1)S(1)}, bf16[128,1408]{1,0:T(8,128)(2,1)S(1)}, u32[]{:S(2)}, u32[]{:S(2)}) collective-permute-start(bf16[128,1408]{1,0:T(8,128)(2,1)S(1)} %get-tuple-element.71), channel_id=1, source_target_pairs={{0,4},{1,5},{2,6},{3,7},{4,0},{5,1},{6,2},{7,3},{8,12},{9,13},{10,... | collective-permute-start | bytes 1081352 | tf_op jit(solution)/shard_map/ppermute | solution.py:22
  451.6 18.6 %collective-permute-start.78 = (bf16[128,1408]{1,0:T(8,128)(2,1)S(1)}, bf16[128,1408]{1,0:T(8,128)(2,1)S(1)}, u32[]{:S(2)}, u32[]{:S(2)}) collective-permute-start(bf16[128,1408]{1,0:T(8,128)(2,1)S(1)} %get-tuple-element.73), channel_id=1, source_target_pairs={{0,2},{1,3},{2,0},{3,1},{4,6},{5,7},{6,4},{7,5},{8,10},{9,11},{10,... | collective-permute-start | bytes 1081352 | tf_op jit(solution)/shard_map/ppermute | solution.py:22
  451.6 25.2 %collective-permute-start.79 = (bf16[128,1408]{1,0:T(8,128)(2,1)S(1)}, bf16[128,1408]{1,0:T(8,128)(2,1)S(1)}, u32[]{:S(2)}, u32[]{:S(2)}) collective-permute-start(bf16[128,1408]{1,0:T(8,128)(2,1)S(1)} %get-tuple-element.72), channel_id=1, source_target_pairs={{0,6},{1,7},{2,4},{3,5},{4,2},{5,3},{6,0},{7,1},{8,14},{9,15},{10,... | collective-permute-start | bytes 1081352 | tf_op jit(solution)/shard_map/ppermute | solution.py:22
  468.8 14.4 %collective-permute-start.50 = (bf16[256,512]{1,0:T(8,128)(2,1)S(1)}, bf16[256,512]{1,0:T(8,128)(2,1)S(1)}, u32[]{:S(2)}, u32[]{:S(2)}) collective-permute-start(bf16[256,512]{1,0:T(8,128)(2,1)S(1)} %get-tuple-element.80), channel_id=1, source_target_pairs={{0,16},{1,17},{2,18},{3,19},{4,20},{5,21},{6,22},{7,23},{8,24},{9,... | collective-permute-start | bytes 786440 | tf_op jit(solution)/shard_map/ppermute | solution.py:37
  470.3 13.0 %collective-permute-start.51 = (bf16[256,512]{1,0:T(8,128)(2,1)S(1)}, bf16[256,512]{1,0:T(8,128)(2,1)S(1)}, u32[]{:S(2)}, u32[]{:S(2)}) collective-permute-start(bf16[256,512]{1,0:T(8,128)(2,1)S(1)} %get-tuple-element.79), channel_id=1, source_target_pairs={{0,2},{1,3},{2,0},{3,1},{4,6},{5,7},{6,4},{7,5},{8,10},{9,11},{10,... | collective-permute-start | bytes 786440 | tf_op jit(solution)/shard_map/ppermute | solution.py:37
  478.1 10.8 %collective-permute-start.52 = (bf16[256,512]{1,0:T(8,128)(2,1)S(1)}, bf16[256,512]{1,0:T(8,128)(2,1)S(1)}, u32[]{:S(2)}, u32[]{:S(2)}) collective-permute-start(bf16[256,512]{1,0:T(8,128)(2,1)S(1)} %get-tuple-element.78), channel_id=1, source_target_pairs={{0,18},{1,19},{2,16},{3,17},{4,22},{5,23},{6,20},{7,21},{8,26},{9,... | collective-permute-start | bytes 786440 | tf_op jit(solution)/shard_map/ppermute | solution.py:37
  501.6 22.1 %collective-permute-start.53 = (bf16[256,1536]{1,0:T(8,128)(2,1)}, bf16[256,1536]{1,0:T(8,128)(2,1)}, u32[]{:S(2)}, u32[]{:S(2)}) collective-permute-start(bf16[256,1536]{1,0:T(8,128)(2,1)} %get-tuple-element.46), channel_id=1, source_target_pairs={{0,16},{1,17},{2,18},{3,19},{4,20},{5,21},{6,22},{7,23},{8,24},{9,... | collective-permute-start | bytes 2359304 | tf_op jit(solution)/shard_map/ppermute | solution.py:37
  520.5 20.8 %collective-permute-start.54 = (bf16[256,1536]{1,0:T(8,128)(2,1)}, bf16[256,1536]{1,0:T(8,128)(2,1)S(1)}, u32[]{:S(2)}, u32[]{:S(2)}) collective-permute-start(bf16[256,1536]{1,0:T(8,128)(2,1)} %get-tuple-element.45), channel_id=1, source_target_pairs={{0,2},{1,3},{2,0},{3,1},{4,6},{5,7},{6,4},{7,5},{8,10},{9,11},{10,... | collective-permute-start | bytes 2359304 | tf_op jit(solution)/shard_map/ppermute | solution.py:37
  522.7 47.1 %collective-permute-start.68 = (bf16[512,512]{1,0:T(8,128)(2,1)}, bf16[512,512]{1,0:T(8,128)(2,1)}, u32[]{:S(2)}, u32[]{:S(2)}) collective-permute-start(bf16[512,512]{1,0:T(8,128)(2,1)} %convolution_convert_fusion.9), channel_id=1, source_target_pairs={{0,1},{1,0},{2,3},{3,2},{4,5},{5,4},{6,7},{7,6},{8,9},{9,8},{10,11... | collective-permute-start | bytes 1572872 | tf_op jit(solution)/shard_map/ppermute | solution.py:22
  523.6 31.9 %collective-permute-start.55 = (bf16[256,1536]{1,0:T(8,128)(2,1)}, bf16[256,1536]{1,0:T(8,128)(2,1)S(1)}, u32[]{:S(2)}, u32[]{:S(2)}) collective-permute-start(bf16[256,1536]{1,0:T(8,128)(2,1)} %get-tuple-element.44), channel_id=1, source_target_pairs={{0,18},{1,19},{2,16},{3,17},{4,22},{5,23},{6,20},{7,21},{8,26},{9,... | collective-permute-start | bytes 2359304 | tf_op jit(solution)/shard_map/ppermute | solution.py:37
  563.3 24.4 %collective-permute-start.56 = (bf16[512,1024]{1,0:T(8,128)(2,1)}, bf16[512,1024]{1,0:T(8,128)(2,1)}, u32[]{:S(2)}, u32[]{:S(2)}) collective-permute-start(bf16[512,1024]{1,0:T(8,128)(2,1)} %slice.189), channel_id=1, source_target_pairs={{0,8},{8,0},{16,24},{24,16},{1,9},{9,1},{17,25},{25,17},{2,10},{10... | collective-permute-start | bytes 3145736 | tf_op jit(solution)/shard_map/ppermute | solution.py:27
  572.3 13.8 %collective-permute-start.69 = (bf16[128,512]{1,0:T(8,128)(2,1)S(1)}, bf16[128,512]{1,0:T(8,128)(2,1)S(1)}, u32[]{:S(2)}, u32[]{:S(2)}) collective-permute-start(bf16[128,512]{1,0:T(8,128)(2,1)S(1)} %get-tuple-element.94), channel_id=1, source_target_pairs={{0,4},{1,5},{2,6},{3,7},{4,0},{5,1},{6,2},{7,3},{8,12},{9,13},{10,... | collective-permute-start | bytes 393224 | tf_op jit(solution)/shard_map/ppermute | solution.py:22
  577.2 10.4 %collective-permute-start.70 = (bf16[128,512]{1,0:T(8,128)(2,1)S(1)}, bf16[128,512]{1,0:T(8,128)(2,1)S(1)}, u32[]{:S(2)}, u32[]{:S(2)}) collective-permute-start(bf16[128,512]{1,0:T(8,128)(2,1)S(1)} %get-tuple-element.96), channel_id=1, source_target_pairs={{0,2},{1,3},{2,0},{3,1},{4,6},{5,7},{6,4},{7,5},{8,10},{9,11},{10,... | collective-permute-start | bytes 393224 | tf_op jit(solution)/shard_map/ppermute | solution.py:22
  599.4 18.8 %collective-permute-start.58 = (bf16[528,1024]{1,0:T(8,128)(2,1)S(1)}, bf16[528,1024]{1,0:T(8,128)(2,1)S(1)}, u32[]{:S(2)}, u32[]{:S(2)}) collective-permute-start(bf16[528,1024]{1,0:T(8,128)(2,1)S(1)} %collective-permute-done.57), channel_id=1, source_target_pairs={{0,8},{8,0},{16,24},{24,16},{1,9},{9,1},{17,25},{25,17},{2,10},{10... | collective-permute-start | bytes 3244040 | tf_op jit(solution)/shard_map/ppermute | solution.py:27
  609.1 35.4 %collective-permute-start.73 = (bf16[128,2816]{1,0:T(8,128)(2,1)S(1)}, bf16[128,2816]{1,0:T(8,128)(2,1)S(1)}, u32[]{:S(2)}, u32[]{:S(2)}) collective-permute-start(bf16[128,2816]{1,0:T(8,128)(2,1)S(1)} %get-tuple-element.52), channel_id=1, source_target_pairs={{0,4},{1,5},{2,6},{3,7},{4,0},{5,1},{6,2},{7,3},{8,12},{9,13},{10,... | collective-permute-start | bytes 2162696 | tf_op jit(solution)/shard_map/ppermute | solution.py:22
  610.9 33.6 %collective-permute-start.74 = (bf16[128,2816]{1,0:T(8,128)(2,1)S(1)}, bf16[128,2816]{1,0:T(8,128)(2,1)S(1)}, u32[]{:S(2)}, u32[]{:S(2)}) collective-permute-start(bf16[128,2816]{1,0:T(8,128)(2,1)S(1)} %get-tuple-element.54), channel_id=1, source_target_pairs={{0,2},{1,3},{2,0},{3,1},{4,6},{5,7},{6,4},{7,5},{8,10},{9,11},{10,... | collective-permute-start | bytes 2162696 | tf_op jit(solution)/shard_map/ppermute | solution.py:22
  612.0 48.8 %collective-permute-start.75 = (bf16[128,2816]{1,0:T(8,128)(2,1)S(1)}, bf16[128,2816]{1,0:T(8,128)(2,1)S(1)}, u32[]{:S(2)}, u32[]{:S(2)}) collective-permute-start(bf16[128,2816]{1,0:T(8,128)(2,1)S(1)} %get-tuple-element.53), channel_id=1, source_target_pairs={{0,6},{1,7},{2,4},{3,5},{4,2},{5,3},{6,0},{7,1},{8,14},{9,15},{10,... | collective-permute-start | bytes 2162696 | tf_op jit(solution)/shard_map/ppermute | solution.py:22
  615.4 47.2 %collective-permute-start.64 = (bf16[512,1536]{1,0:T(8,128)(2,1)S(1)}, bf16[512,1536]{1,0:T(8,128)(2,1)S(1)}, u32[]{:S(2)}, u32[]{:S(2)}) collective-permute-start(bf16[512,1536]{1,0:T(8,128)(2,1)S(1)} %convolution_convert_fusion.6), channel_id=1, source_target_pairs={{0,1},{1,0},{2,3},{3,2},{4,5},{5,4},{6,7},{7,6},{8,9},{9,8},{10,11... | collective-permute-start | bytes 4718600 | tf_op jit(solution)/shard_map/ppermute | solution.py:22
  618.4 43.8 %collective-permute-start.59 = (bf16[264,1024]{1,0:T(8,128)(2,1)S(1)}, bf16[264,1024]{1,0:T(8,128)(2,1)S(1)}, u32[]{:S(2)}, u32[]{:S(2)}) collective-permute-start(bf16[264,1024]{1,0:T(8,128)(2,1)S(1)} %fusion.28), channel_id=1, source_target_pairs={{0,16},{8,24},{16,0},{24,8},{1,17},{9,25},{17,1},{25,9},{2,18},{10... | collective-permute-start | bytes 1622024 | tf_op jit(solution)/shard_map/ppermute | solution.py:27
  668.9 45.0 %collective-permute-start.61 = (bf16[4,32,4224]{2,1,0:T(8,128)(2,1)S(1)}, bf16[4,32,4224]{2,1,0:T(8,128)(2,1)S(1)}, u32[]{:S(2)}, u32[]{:S(2)}) collective-permute-start(bf16[4,32,4224]{2,1,0:T(8,128)(2,1)S(1)} %dynamic-slice_bitcast_fusion), channel_id=1, source_target_pairs={{0,1},{1,0},{2,3},{3,2},{4,5},{5,4},{6,7},{7,6},{8,9},{9,8},{10,11... | collective-permute-start | bytes 3244040 | tf_op jit(solution)/shard_map/ppermute | solution.py:22
  670.2 34.0 %collective-permute-start.65 = (bf16[128,1536]{1,0:T(8,128)(2,1)S(1)}, bf16[128,1536]{1,0:T(8,128)(2,1)S(1)}, u32[]{:S(2)}, u32[]{:S(2)}) collective-permute-start(bf16[128,1536]{1,0:T(8,128)(2,1)S(1)} %get-tuple-element.68), channel_id=1, source_target_pairs={{0,4},{1,5},{2,6},{3,7},{4,0},{5,1},{6,2},{7,3},{8,12},{9,13},{10,... | collective-permute-start | bytes 1179656 | tf_op jit(solution)/shard_map/ppermute | solution.py:22
  685.8 18.8 %collective-permute-start.66 = (bf16[128,1536]{1,0:T(8,128)(2,1)S(1)}, bf16[128,1536]{1,0:T(8,128)(2,1)S(1)}, u32[]{:S(2)}, u32[]{:S(2)}) collective-permute-start(bf16[128,1536]{1,0:T(8,128)(2,1)S(1)} %get-tuple-element.70), channel_id=1, source_target_pairs={{0,2},{1,3},{2,0},{3,1},{4,6},{5,7},{6,4},{7,5},{8,10},{9,11},{10,... | collective-permute-start | bytes 1179656 | tf_op jit(solution)/shard_map/ppermute | solution.py:22
  685.8 27.7 %collective-permute-start.67 = (bf16[128,1536]{1,0:T(8,128)(2,1)S(1)}, bf16[128,1536]{1,0:T(8,128)(2,1)S(1)}, u32[]{:S(2)}, u32[]{:S(2)}) collective-permute-start(bf16[128,1536]{1,0:T(8,128)(2,1)S(1)} %get-tuple-element.69), channel_id=1, source_target_pairs={{0,6},{1,7},{2,4},{3,5},{4,2},{5,3},{6,0},{7,1},{8,14},{9,15},{10,... | collective-permute-start | bytes 1179656 | tf_op jit(solution)/shard_map/ppermute | solution.py:22
  714.1 20.5 %collective-permute-start.62 = (bf16[2,32,4224]{2,1,0:T(8,128)(2,1)S(1)}, bf16[2,32,4224]{2,1,0:T(8,128)(2,1)S(1)}, u32[]{:S(2)}, u32[]{:S(2)}) collective-permute-start(bf16[2,32,4224]{2,1,0:T(8,128)(2,1)S(1)} %fusion.30), channel_id=1, source_target_pairs={{0,2},{1,3},{2,0},{3,1},{4,6},{5,7},{6,4},{7,5},{8,10},{9,11},{10,... | collective-permute-start | bytes 1622024 | tf_op jit(solution)/shard_map/ppermute | solution.py:22
  734.8 14.6 %collective-permute-start.63 = (bf16[1,32,4224]{2,1,0:T(8,128)(2,1)S(1)}, bf16[1,32,4224]{2,1,0:T(8,128)(2,1)S(1)}, u32[]{:S(2)}, u32[]{:S(2)}) collective-permute-start(bf16[1,32,4224]{2,1,0:T(8,128)(2,1)S(1)} %dynamic-slice_convert_fusion.1), channel_id=1, source_target_pairs={{0,4},{1,5},{2,6},{3,7},{4,0},{5,1},{6,2},{7,3},{8,12},{9,13},{10,... | collective-permute-start | bytes 811016 | tf_op jit(solution)/shard_map/ppermute | solution.py:22
  (88 other events, 804.4 us)

commit v2 on v1

--- a/solution.py
+++ b/solution.py
@@ -15,6 +15,369 @@
 bf16 = jnp.bfloat16
 
 PAIRS = [(q, k) for q in range(4) for k in range(q + 1)]
+
+
+ANY = pl.BlockSpec(memory_space=pl.ANY)
+VMEM = pl.BlockSpec(memory_space=pltpu.VMEM)
+EXTRA = 32
+
+
+def flip(value, mask):
+    bit = 1
+    while bit <= mask:
+        if mask & bit:
+            value = value + bit - 2 * bit * ((value // bit) % 2)
+        bit *= 2
+    return value
+
+
+class Where:
+    def __init__(self, n):
+        self.n = n
+        self.stream = lax.axis_index("stream")
+        self.frame = lax.axis_index("frames")
+        self.core = self.stream % 2
+        self.place = (self.frame // 2) % 2
+        self.position = (self.stream // 2) * 2 + self.place
+        self.near = self.frame % 2
+        self.at = self.frame // 2
+        self.far_masks = [m for m in range(2, n, 2) if not m & 2]
+        self.both_masks = [m for m in range(2, n, 2) if m & 2 and m > 2]
+        self.masks = self.far_masks + self.both_masks + [2]
+
+    def along_stream(self, mask):
+        return (flip(self.stream, mask), self.frame)
+
+    def along_frames(self, mask):
+        return (self.stream, flip(self.frame, mask))
+
+    def with_position(self, mask):
+        return (flip(self.stream, mask & 2), flip(self.frame, 2 * (mask & 1)))
+
+    def across(self):
+        return (flip(self.stream, 1), flip(self.frame, 2))
+
+
+class Wire:
+    def __init__(self, send, recv):
+        self.send, self.recv, self.count, self.started = send, recv, 0, []
+
+    def make(self, src, dst, device):
+        k = self.count
+        self.count += 1
+        return pltpu.make_async_remote_copy(
+            src_ref=src,
+            dst_ref=dst,
+            send_sem=self.send.at[k],
+            recv_sem=self.recv.at[k],
+            device_id=device,
+            device_id_type=pl.DeviceIdType.MESH,
+        )
+
+    def start(self, src, dst, device):
+        copy = self.make(src, dst, device)
+        copy.start()
+        self.started.append(copy)
+        return copy
+
+    def finish(self):
+        for copy in self.started:
+            copy.wait_send()
+
+
+class Local:
+    def __init__(self, sems):
+        self.sems, self.count = sems, 0
+
+    def start(self, src, dst):
+        copy = pltpu.make_async_copy(src, dst, self.sems.at[self.count])
+        self.count += 1
+        copy.start()
+        return copy
+
+
+def greet(devices):
+    barrier = pltpu.get_barrier_semaphore()
+    for device in devices:
+        pl.semaphore_signal(
+            barrier, inc=1, device_id=device, device_id_type=pl.DeviceIdType.MESH
+        )
+    pl.semaphore_wait(barrier, len(devices))
+
+
+def dot_rows(left, right):
+    return lax.dot_general(left, right, (((0,), (0,)), ((), ())), preferred_element_type=f32)
+
+
+def dot_columns(left, right):
+    return lax.dot_general(left, right, (((1,), (1,)), ((), ())), preferred_element_type=f32)
+
+
+class Reduction:
+    def __init__(self, w, wire, send, keep, arrived, sums, landed, out):
+        self.w, self.wire = w, wire
+        self.send, self.keep, self.arrived = send, keep, arrived
+        self.sums, self.landed, self.out = sums, landed, out
+        self.first, self.second = {}, {}
+        self.order = w.masks + [0]
+
+    def begin(self, mask):
+        block = flip(self.w.at, mask // 2)
+        self.first[mask] = self.wire.start(
+            self.send.at[block], self.arrived.at[block], self.w.along_frames(1)
+        )
+
+    def forward(self, mask):
+        block = flip(self.w.at, mask // 2)
+        self.first[mask].wait_recv()
+        total = self.keep[block].astype(f32) + self.arrived[block].astype(f32)
+        self.sums[block] = total.astype(bf16)
+        if mask:
+            self.second[mask] = self.wire.start(
+                self.sums.at[block], self.landed.at[mask // 2], self.w.along_frames(mask)
+            )
+
+    def close(self):
+        own, other = self.sums[self.w.at].astype(f32), None
+        for mask in self.w.masks:
+            self.second[mask].wait_recv()
+            got = self.landed[mask // 2].astype(f32)
+            if mask & 2:
+                other = got if other is None else other + got
+            else:
+                own = own + got
+        self.out[self.w.place] = own
+        self.out[1 - self.w.place] = other
+
+
+def tail_body(
+    n, part_send, part_own, resid, mid, gains, gain_two, result_rows,
+    gq_send, gq_keep, go_send, go_keep, context, ctx_full,
+    out_q, out_o, out_grad, out_result, out_context, out_ctx,
+    part_got, low, home, partner_half, half_sum, far_half, whole, kept_q, kept_o,
+    arrived_q, arrived_o, sums_q, sums_o, landed_q, landed_o,
+    context_held, ctx_held, term, term_got, term_sum, term_landed, gain_sum,
+    send_sem, recv_sem, local_sem,
+):
+    w = Where(n)
+    wire, local = Wire(send_sem, recv_sem), Local(local_sem)
+    rows, depth = resid.shape
+    crossing = w.core != w.place
+    load_q = local.start(gq_keep, kept_q)
+    load_o = local.start(go_keep, kept_o)
+    load_context = local.start(context, context_held)
+    load_ctx = local.start(ctx_full, ctx_held)
+    greet(
+        [w.along_stream(1), w.along_stream(2), w.along_frames(1)]
+        + [w.along_frames(m) for m in w.masks]
+        + [w.across()]
+    )
+    part = wire.start(part_send, part_got, w.along_stream(1))
+    red_o = Reduction(w, wire, go_send, kept_o, arrived_o, sums_o, landed_o, out_o)
+    red_q = Reduction(w, wire, gq_send, kept_q, arrived_q, sums_q, landed_q, out_q)
+    for mask in red_o.order:
+        red_o.begin(mask)
+    for mask in red_q.order:
+        red_q.begin(mask)
+
+    part.wait_recv()
+    gain = gains[0:1, :]
+    gain_sum[...] = jnp.zeros_like(gain_sum)
+    step = 64
+
+    @pl.loop(0, rows // step)
+    def _(t):
+        at = pl.ds(pl.multiple_of(t * step, step), step)
+        grad = part_own[at, :].astype(f32) + part_got[at, :].astype(f32)
+        values = resid[at, :].astype(f32)
+        scale = lax.rsqrt(jnp.mean(values * values, axis=-1, keepdims=True) + norm_eps)
+        weighted = grad * gain
+        inner = jnp.mean(weighted * values, axis=-1, keepdims=True)
+        back = scale * weighted - values * (scale * scale * scale * inner)
+        low[at, :] = (mid[at, :] + back).astype(bf16)
+        gain_sum[...] += jnp.sum(grad * values * scale, axis=0, keepdims=True)
+
+    row = lax.broadcasted_iota(jnp.int32, (EXTRA, depth), 0)
+    low[rows:, :] = jnp.where(
+        row == 0, gain_sum[...], jnp.where(row == 1, gain_two[...], 0.0)
+    ).astype(bf16)
+
+    cross = wire.make(low, home, w.across())
+    cross_result = wire.make(result_rows, out_result, w.across())
+
+    @pl.when(crossing)
+    def _():
+        cross.start()
+
+    load_o.wait()
+    load_q.wait()
+    for mask in red_o.order:
+        red_o.forward(mask)
+
+    @pl.when(crossing)
+    def _():
+        cross_result.start()
+        cross.wait_recv()
+
+    stay = pltpu.make_async_copy(low, home, local.sems.at[4])
+    stay_result = pltpu.make_async_copy(result_rows, out_result, local.sems.at[5])
+
+    @pl.when(jnp.logical_not(crossing))
+    def _():
+        stay.start()
+        stay_result.start()
+        stay.wait()
+
+    half = (rows + EXTRA) // 2
+    mine = pl.ds(pl.multiple_of(w.core * half, 16), half)
+    theirs = pl.ds(pl.multiple_of((1 - w.core) * half, 16), half)
+    first = wire.start(home.at[theirs, :], partner_half, w.along_stream(1))
+    out_grad[...] = home[:rows, :].astype(f32)
+    first.wait_recv()
+    half_sum[...] = (home[mine, :].astype(f32) + partner_half[...].astype(f32)).astype(bf16)
+    second = wire.start(half_sum, far_half, w.along_stream(2))
+    red_q.forward(red_q.order[0])
+    red_q.forward(red_q.order[1])
+    second.wait_recv()
+    whole[mine, :] = (half_sum[...].astype(f32) + far_half[...].astype(f32)).astype(bf16)
+    third = wire.start(whole.at[mine, :], whole.at[mine, :], w.along_stream(1))
+    load_context.wait()
+    third.wait_recv()
+
+    share = depth // 4
+    columns = pl.ds(pl.multiple_of(w.stream * share, LANES), share)
+    block = share // n
+    wide = context_held.shape[1]
+    pieces = 2
+    grad_share = whole[:rows, columns]
+    firsts, seconds = [], []
+    row = lax.broadcasted_iota(jnp.int32, (EXTRA, LANES), 0)
+    select = (row == lax.broadcasted_iota(jnp.int32, (EXTRA, LANES), 1)).astype(bf16)
+    edges = [wide * p // pieces for p in range(pieces)] + [wide + LANES]
+    for p in range(pieces):
+        lo, hi = edges[p], edges[p + 1]
+        for at in range(lo, min(hi, wide), 1024):
+            to = min(at + 1024, wide)
+            value = dot_rows(grad_share, context_held[:, at:to]).astype(bf16)
+            for k in range(n):
+                term[k // 2, k % 2, :, at:to] = value[k * block : (k + 1) * block]
+        if hi > wide:
+            value = dot_rows(whole[rows:, columns], select).astype(bf16)
+            for k in range(n):
+                term[k // 2, k % 2, :, wide:hi] = value[k * block : (k + 1) * block]
+        firsts.append(
+            wire.start(
+                term.at[:, 1 - w.near, :, lo:hi], term_got.at[:, :, lo:hi], w.along_frames(1)
+            )
+        )
+    for mask in red_q.order[2:]:
+        red_q.forward(mask)
+    load_ctx.wait()
+
+    def context_rows(t):
+        at = pl.ds(pl.multiple_of(t * LANES, LANES), LANES)
+        out_context[at, :] = dot_columns(whole[at, :], ctx_held[...])
+
+    @pl.loop(0, rows // LANES)
+    def _(t):
+        context_rows(t)
+
+    for p in range(pieces):
+        lo, hi = edges[p], edges[p + 1]
+        firsts[p].wait_recv()
+        for mask in w.masks + [0]:
+            to = flip(w.at, mask // 2)
+            total = term[to, w.near, :, lo:hi].astype(f32) + term_got[to, :, lo:hi].astype(f32)
+            term_sum[to, :, lo:hi] = total.astype(bf16)
+            if mask:
+                seconds.append(
+                    wire.start(
+                        term_sum.at[to, :, lo:hi],
+                        term_landed.at[mask // 2, :, lo:hi],
+                        w.along_frames(mask),
+                    )
+                )
+    red_o.close()
+    red_q.close()
+
+    @pl.when(crossing)
+    def _():
+        cross_result.wait_recv()
+        cross.wait_send()
+        cross_result.wait_send()
+
+    @pl.when(jnp.logical_not(crossing))
+    def _():
+        stay_result.wait()
+
+    for copy in seconds:
+        copy.wait_recv()
+    total = term_sum[w.at].astype(f32)
+    for mask in w.masks:
+        total = total + term_landed[mask // 2].astype(f32)
+    out_ctx[...] = total
+    wire.finish()
+
+
+def tail(
+    n, part_send, part_own, resid, mid, gains, gain_two, result_rows,
+    gq_send, gq_keep, go_send, go_keep, context, ctx_full,
+):
+    rows, depth = resid.shape
+    halfn, block, wide_q = gq_send.shape
+    wide_o = go_send.shape[2]
+    share = depth // 4 // n
+    wide = context.shape[1] + LANES
+    half = (rows + EXTRA) // 2
+    count = 64 + 2 * n
+    scratch = [
+        pltpu.VMEM((rows, depth), bf16),
+        pltpu.VMEM((rows + EXTRA, depth), bf16),
+        pltpu.VMEM((rows + EXTRA, depth), bf16),
+        pltpu.VMEM((half, depth), bf16),
+        pltpu.VMEM((half, depth), bf16),
+        pltpu.VMEM((half, depth), bf16),
+        pltpu.VMEM((rows + EXTRA, depth), bf16),
+        pltpu.VMEM((halfn, block, wide_q), bf16),
+        pltpu.VMEM((halfn, block, wide_o), bf16),
+        pltpu.VMEM((halfn, block, wide_q), bf16),
+        pltpu.VMEM((halfn, block, wide_o), bf16),
+        pltpu.VMEM((halfn, block, wide_q), bf16),
+        pltpu.VMEM((halfn, block, wide_o), bf16),
+        pltpu.VMEM((halfn, block, wide_q), bf16),
+        pltpu.VMEM((halfn, block, wide_o), bf16),
+        pltpu.VMEM(context.shape, bf16),
+        pltpu.VMEM(ctx_full.shape, bf16),
+        pltpu.VMEM((halfn, 2, share, wide), bf16),
+        pltpu.VMEM((halfn, share, wide), bf16),
+        pltpu.VMEM((halfn, share, wide), bf16),
+        pltpu.VMEM((halfn, share, wide), bf16),
+        pltpu.VMEM((1, depth), f32),
+        pltpu.SemaphoreType.DMA((count,)),
+        pltpu.SemaphoreType.DMA((count,)),
+        pltpu.SemaphoreType.DMA((6,)),
+    ]
+    return pl.pallas_call(
+        functools.partial(tail_body, n),
+        in_specs=[ANY, VMEM, VMEM, VMEM, VMEM, VMEM, VMEM, ANY, ANY, ANY, ANY, ANY, ANY],
+        out_specs=[VMEM, VMEM, VMEM, VMEM, VMEM, VMEM],
+        out_shape=[
+            jax.ShapeDtypeStruct((2, block, wide_q), f32),
+            jax.ShapeDtypeStruct((2, block, wide_o), f32),
+            jax.ShapeDtypeStruct((rows, depth), f32),
+            jax.ShapeDtypeStruct((rows, depth), bf16),
+            jax.ShapeDtypeStruct((rows, ctx_full.shape[0]), f32),
+            jax.ShapeDtypeStruct((share, wide), f32),
+        ],
+        scratch_shapes=scratch,
+        compiler_params=pltpu.CompilerParams(
+            collective_id=5, has_side_effects=True, vmem_limit_bytes=60 << 20
+        ),
+        name="tail",
+    )(
+        part_send, part_own, resid, mid, gains, gain_two, result_rows,
+        gq_send, gq_keep, go_send, go_keep, context, ctx_full,
+    )
 
 
 def swap_frames(value, mask):
@@ -185,36 +548,48 @@
     )(qkv, probs, grad, fold, spread)
 
 
-def gathered(weight, frame_index, place):
+def after(value, *others):
+    return lax.optimization_barrier((value,) + others)[0]
+
+
+def taken(weights, place):
+    own = [lax.dynamic_index_in_dim(w, place, 0, keepdims=False) for w in weights]
+    other = [lax.dynamic_index_in_dim(w, 1 - place, 0, keepdims=False) for w in weights]
+    if len(weights) == 1:
+        return own[0], other[0]
+    return jnp.concatenate(own, axis=1), jnp.concatenate(other, axis=1)
+
+
+def placed_rows(pieces, frame_index, start, width):
     n = lax.axis_size("frames")
-    own = lax.dynamic_index_in_dim(weight, place, 0, keepdims=False)
-    other = lax.dynamic_index_in_dim(weight, 1 - place, 0, keepdims=False)
-    block, width = own.shape
-    full = jnp.zeros((n, block, width), own.dtype)
-    for mask in range(0, n, 2):
-        got = own if mask == 0 else swap_frames(other if mask & 2 else own, mask)
-        near = swap_frames(got, 1)
-        full = lax.dynamic_update_index_in_dim(full, got, frame_index ^ mask, 0)
-        full = lax.dynamic_update_index_in_dim(full, near, frame_index ^ mask ^ 1, 0)
+    block = pieces[0].shape[0]
+    full = jnp.zeros((n, block, width), pieces[0].dtype)
+    for mask in range(n):
+        part = pieces[mask][:, start : start + width]
+        full = lax.dynamic_update_index_in_dim(full, part, frame_index ^ mask, 0)
     return full.reshape(n * block, width)
 
 
-def scattered(left, right, frame_index, place):
+def halves(left, near):
     n = lax.axis_size("frames")
     rows, depth = left.shape
     block = depth // n
-    near = frame_index % 2
-    shaped = left.reshape(rows, n // 2, 2, block)
-
-    def product(which):
-        part = lax.dynamic_index_in_dim(shaped, which, 2, keepdims=False).reshape(rows, depth // 2)
+    even = jnp.concatenate([left[:, k * block : (k + 1) * block] for k in range(0, n, 2)], axis=1)
+    odd = jnp.concatenate([left[:, k * block : (k + 1) * block] for k in range(1, n, 2)], axis=1)
+    return jnp.where(near == 0, odd, even), jnp.where(near == 0, even, odd)
+
+
+def scattered(left_halves, right, frame_index, place):
+    n = lax.axis_size("frames")
+
+    def product(part):
         return lax.dot_general(
             part, right, (((0,), (0,)), ((), ())), preferred_element_type=f32
         ).astype(bf16)
 
-    arrived = swap_frames(product(1 - near), 1)
-    half_sum = (product(near).astype(f32) + arrived.astype(f32)).astype(bf16)
-    half_sum = half_sum.reshape(n // 2, block, -1)
+    arrived = swap_frames(product(left_halves[0]), 1)
+    half_sum = (product(left_halves[1]).astype(f32) + arrived.astype(f32)).astype(bf16)
+    half_sum = half_sum.reshape(n // 2, -1, right.shape[1])
     at = frame_index // 2
     own = lax.dynamic_index_in_dim(half_sum, at, 0, keepdims=False).astype(f32)
     other = None
@@ -261,12 +636,21 @@
     block = piece.shape[1]
     held = piece[None]
     order = [0]
+    near_pieces = []
+    attn_own, attn_other = taken((qkv_weight[0], out_weight[0]), place)
+    near_first = {}
+    near_first["attn"] = swap_frames(attn_own, 1)
+    far_context = None
     for bit in reversed(range(1, n.bit_length() - 1)):
         got = swap_frames(held, 1 << bit)
+        if far_context is None:
+            far_context = got
+            near_pieces.append(swap_frames(jnp.concatenate([held, got], axis=0), 1))
+        else:
+            near_pieces.append(swap_frames(got, 1))
         held = jnp.concatenate([held, got], axis=0)
         order = order + [o ^ (1 << bit) for o in order]
-    got = swap_frames(held, 1)
-    held = jnp.concatenate([held, got], axis=0)
+    held = jnp.concatenate([held] + near_pieces, axis=0)
     order = order + [o ^ 1 for o in order]
     ctx_full = jnp.zeros((ctx_rows, n, block), bf16)
     for at, o in enumerate(order):
@@ -285,14 +669,30 @@
         second = jnp.where(half_index == 0, far, mine)
         return jnp.concatenate([first, second], axis=0)
 
-    resid_home = inputs[:, 0].astype(f32) + summed(projected).astype(f32)
-    resid_in = transposed(resid_home.astype(bf16)).astype(f32)
-    grad_res = transposed((cotangent[:, 0] * valid_mask).astype(bf16))
-
-    qkv_full = gathered(qkv_weight[0], frame_index, place)
-    out_full = gathered(out_weight[0], frame_index, place)
-    gate_up_full = gathered(gate_up_weight[0], frame_index, place)
-    down_full = gathered(down_weight[0], frame_index, place)
+    def sent(own, other, masks, *others):
+        pieces = {}
+        for mask in masks:
+            got = swap_frames(after(other if mask & 2 else own, *others), mask)
+            pieces[mask] = got
+            pieces[mask + 1] = swap_frames(got, 1)
+        return pieces
+
+    far_masks = [m for m in range(2, n, 2) if not m & 2]
+    both_masks = [m for m in range(2, n, 2) if m & 2 and m > 2]
+    near_masks = [2]
+    attn_pieces = {0: attn_own, 1: near_first["attn"]}
+    attn_pieces.update(sent(attn_own, attn_other, far_masks + both_masks + near_masks, far_context))
+    head_width = out_weight.shape[3]
+    qkv_full = placed_rows(attn_pieces, frame_index, 0, 3 * head_width)
+    out_full = placed_rows(attn_pieces, frame_index, 3 * head_width, head_width)
+
+    home_sum = summed(projected).astype(f32)
+    resid_home = (inputs[:, 0].astype(f32) + home_sum).astype(bf16)
+    resid_in = transposed(resid_home).astype(f32)
+    gu_own, gu_other = taken((gate_up_weight[0],), place)
+    down_own, down_other = taken((down_weight[0],), place)
+    gu_pieces = {0: gu_own, 1: swap_frames(after(gu_own, near_pieces[-1]), 1)}
+    gu_pieces.update(sent(gu_own, gu_other, far_masks, resid_home))
 
     def paired(mine):
         return jnp.concatenate([mine, swap_stream(mine, 1)], axis=0)
@@ -312,6 +712,8 @@
     paired_one = paired((resid_in * scale_one * gain_one).astype(bf16))
     qkv_rows = rows_times(paired_one, qkv_full).astype(bf16)
     qkv_mixed = exchange_rows(qkv_rows, position)
+    gu_pieces.update(sent(gu_own, gu_other, both_masks, qkv_rows))
+    down_pieces = {0: down_own, 1: swap_frames(after(down_own, qkv_rows), 1)}
     probs, mixed_quarter = attention_forward(qkv_mixed)
 
     def returned(value):
@@ -326,6 +728,15 @@
         return out.reshape(4 * quarter, width)
 
     mixed = returned(mixed_quarter)
+    gu_pieces.update(sent(gu_own, gu_other, near_masks, mixed_quarter))
+    gate_up_full = placed_rows(gu_pieces, frame_index, 0, gate_up_weight.shape[3])
+    down_pieces.update(
+        sent(down_own, down_other, far_masks + both_masks + near_masks, mixed_quarter)
+    )
+    down_full = placed_rows(down_pieces, frame_index, 0, down_weight.shape[3])
+    grad_home_rows = (cotangent[:, 0] * valid_mask).astype(bf16)
+    grad_res = transposed(after(grad_home_rows, mixed_quarter))
+    near = frame_index % 2
     resid_mid = resid_in + own_sum(rows_back(mixed, out_full))
     scale_two = norm_scale(resid_mid)
     paired_two = paired((resid_mid * scale_two * gain_two).astype(bf16))
@@ -338,53 +749,52 @@
     hidden = (activated * up_part).astype(bf16)
 
     paired_grad_ffn = paired(grad_res)
-    sum_down = scattered(paired_grad_ffn, hidden, frame_index, place)
+    sum_down = scattered(halves(paired_grad_ffn, near), hidden, frame_index, place)
     grad_hidden = rows_times(paired_grad_ffn, down_full)
     grad_gate = grad_hidden * up_part * (sigmoid_gate * (1.0 + gate_part * (1.0 - sigmoid_gate)))
     grad_up = grad_hidden * activated
     grad_gu_low = jnp.concatenate([grad_gate, grad_up], axis=-1).astype(bf16)
     grad_normed_two = own_sum(rows_back(grad_gu_low, gate_up_full))
-    sum_gate_up = scattered(paired_two, grad_gu_low, frame_index, place)
+    sum_gate_up = scattered(halves(paired_two, near), grad_gu_low, frame_index, place)
     back_two, grad_gain_two = norm_back(resid_mid, scale_two, gain_two, grad_normed_two)
     grad_mid = grad_res.astype(f32) + back_two
     paired_grad_attn = paired(grad_mid.astype(bf16))
     grad_mixed = rows_times(paired_grad_attn, out_full).astype(bf16)
-    sum_out = scattered(paired_grad_attn, mixed, frame_index, place)
     grad_qkv_mixed = attention_backward(qkv_mixed, probs, exchange_rows(grad_mixed, position))
     grad_qkv_low = returned(grad_qkv_mixed)
-    grad_normed_one = own_sum(rows_back(grad_qkv_low, qkv_full))
-    sum_qkv = scattered(paired_one, grad_qkv_low, frame_index, place)
-    back_one, grad_gain_one = norm_back(resid_in, scale_one, gain_one, grad_normed_one)
-    gain_rows = jnp.pad(jnp.stack([grad_gain_one, grad_gain_two]), ((0, 14), (0, 0)))
-    carried = jnp.concatenate([grad_mid + back_one, gain_rows], axis=0).astype(bf16)
-    grad_home = transposed(carried)
-
-    ffn_sum = own_sum(rows_back(hidden, down_full))
-    result = transposed((resid_mid + ffn_sum).astype(bf16)).astype(f32) * valid_mask
-
-    grad_sum = summed(grad_home)
-    grad_ctx_low = grad_sum[:frame_count]
-    sum_context = rows_back(grad_ctx_low, ctx_full)
-    share = width_model // 4
-    grad_share = lax.dynamic_slice_in_dim(grad_sum, stream_index * share, share, 1)
-    ctx_term = lax.dot_general(
-        grad_share[:frame_count], context, (((0,), (0,)), ((), ())), preferred_element_type=f32
-    ).astype(bf16)
-    gain_term = jnp.pad(grad_share[frame_count : frame_count + 2].T, ((0, 0), (0, LANES - 2)))
-    total = jnp.concatenate([ctx_term, gain_term], axis=1).reshape(n, share // n, -1)
-    for bit in range(n.bit_length() - 1):
-        shaped = total.reshape((-1, 2) + total.shape[1:])
-        at = (frame_index >> bit) % 2
-        keep = lax.dynamic_index_in_dim(shaped, at, 1, keepdims=False)
-        send = lax.dynamic_index_in_dim(shaped, 1 - at, 1, keepdims=False)
-        total = keep.astype(f32) + swap_frames(send.astype(bf16), 1 << bit).astype(f32)
-    total = total.reshape(share // n, -1).T
-    sum_ctx = total[: ctx_weight.shape[0]]
-    sum_gains = total[ctx_weight.shape[0] : ctx_weight.shape[0] + 2]
+    def parts(left, right):
+        away, stay = halves(left, near)
+        block = width_model // n
+        return [
+            dot_rows(part, right).astype(bf16).reshape(n // 2, block, right.shape[1])
+            for part in (away, stay)
+        ]
+
+    part_away = rows_back(grad_qkv_low[frame_count:], qkv_full).astype(bf16)
+    part_stay = rows_back(grad_qkv_low[:frame_count], qkv_full)
+    result_rows = (resid_mid + own_sum(rows_back(hidden, down_full))).astype(bf16)
+    sum_qkv, sum_out, grad_home, result, sum_context, ctx_total = tail(
+        n,
+        part_away,
+        part_stay,
+        resid_in.astype(bf16),
+        grad_mid,
+        norm_gains,
+        grad_gain_two[None],
+        result_rows,
+        *parts(paired_one, grad_qkv_low),
+        *parts(paired_grad_attn, mixed),
+        context,
+        ctx_full,
+    )
+    result = result.astype(f32) * valid_mask
+    ctx_total = ctx_total.T
+    sum_ctx = ctx_total[: ctx_weight.shape[0]]
+    sum_gains = ctx_total[ctx_weight.shape[0] : ctx_weight.shape[0] + 2]
 
     return (
         result[:, None],
-        grad_home[:frame_count].astype(f32)[:, None],
+        grad_home[:, None],
         sum_context,
         sum_ctx,
         sum_gains,

time: 761 us -> 743 us (0.976)
  starting transfers between devices: 172 us -> 74.1 us
  Pallas kernels: 15.8 us -> 105 us
  other arithmetic: 42.4 us -> 20.5 us
  waiting for transfers between devices: 270 us -> 290 us
    dynamic_update_slice x8, local copies, waits for them, and re-layouts: 5.79 us -> 97.3 us  [shards(): lax.dynamic_update_index_in_dim(ctx_full, held[at], frame_index ^ o, 1)]
    pallas_call x0 -> x1, Pallas kernels: none -> 89.4 us  [tail(): pl.pallas_call(functools.partial(tail_body, n), in_specs=[ANY, VMEM, VMEM...]
    ppermute x50 -> x33, starting transfers between devices: 97.2 us -> 37.2 us  [swap_frames(): return lax.ppermute(value, 'frames', [(d, d ^ mask) for d in range(n)])]
    unnamed x157 -> x138, local copies, waits for them, and re-layouts: 65.2 us -> 22.4 us
    dynamic_slice x6 -> x0, local copies, waits for them, and re-layouts: 29.9 us -> none  [the longest x4 29.8 us: product(): lax.dynamic_index_in_dim(shaped, which, 2, keepdims=False)]
    ppermute x16 -> x14, waiting for transfers between devices: 76.4 us -> 105 us  [joint(): return lax.ppermute(value, ('stream', 'frames'), pairs)]
    ppermute x14 -> x10, starting transfers between devices: 46.1 us -> 20.7 us  [swap_stream(): return lax.ppermute(value, 'stream', [(d, d ^ mask) for d in range(n)])]
    reshape x4 -> x0, local copies, waits for them, and re-layouts: 15.2 us -> none  [scattered(): shaped = left.reshape(rows, n // 2, 2, block)]
  transfers between devices with their start and end apart: 80 -> 57, of which waited for: 33 -> 29; matrix products, arithmetic and copies ran while one was open for 33% -> 29% of each run, Pallas kernels for 2% -> 14%
where the time goes in v2:
time: 743 us; the launch traced here: 731 us
  waiting for transfers between devices  290 us (39%)
  local copies, waits for them, and re-layouts  161 us (22%)
  Pallas kernels  105 us (14%)
  matrix products  76.9 us (10%)
  starting transfers between devices  74.1 us (10%)
  other arithmetic  20.5 us (3%)
    ppermute x33, waiting for transfers between devices, swap_frames(): return lax.ppermute(value, 'frames', [(d, d ^ mask) for d in range(n)])  185 us
    ppermute x14, waiting for transfers between devices, joint(): return lax.ppermute(value, ('stream', 'frames'), pairs)  105 us
    dynamic_update_slice x8, local copies, waits for them, and re-layouts, shards(): lax.dynamic_update_index_in_dim(ctx_full, held[at], frame_index ^ o, 1)  97.3 us
    pallas_call x1, Pallas kernels, tail(): pl.pallas_call(functools.partial(tail_body, n), in_specs=[ANY, VMEM, VMEM...  89.4 us
    ppermute x33, starting transfers between devices, swap_frames(): return lax.ppermute(value, 'frames', [(d, d ^ mask) for d in range(n)])  37.2 us
    dot_general x4, matrix products, rows_times(): return jnp.dot(left, right, preferred_element_type=f32)  27.5 us
    unnamed x138, local copies, waits for them, and re-layouts  22.4 us
    dot_general x5, matrix products, rows_back(): lax.dot_general(left, right, (((1,), (1,)), ((), ())), preferred_element_...  22.3 us
  transfers between devices with their start and end apart: 57, of which 29 were waited for; matrix products, arithmetic and copies ran while one was open for 29% of the time, Pallas kernels for 14%

profile of v2, /device:TPU:0, one launch (start us, length us, event | category | flops | bytes accessed | tf_op | source)
XLA Modules:
  0.0 730.8 jit_solution(10480279471160259021)
XLA Ops:
  3.8 3.0 collective-permute-start.9
  7.8 2.7 collective-permute-start
  17.3 4.9 collective-permute-done
  25.7 10.4 %collective-permute-done.1 = bf16[2,1024,128]{2,1,0:T(8,128)(2,1)} collective-permute-done((bf16[2,1024,128]{2,1,0:T(8,128)(2,1)}, bf16[2,1024,128]{2,1,0:T(8,128)(2,1)}, u32[]{:S(2)}, u32[]{:S(2)}) %collective-permute-start.1) | collective-permute-done | bytes 524320 | tf_op jit(solution)/shard_map/ppermute | solution.py:385
  39.8 12.3 %dynamic_update_slice.175 = bf16[1024,8,128]{2,1,0:T(8,128)(2,1)S(1)} dynamic-update-slice(bf16[1024,8,128]{2,1,0:T(8,128)(2,1)S(1)} %broadcast_in_dim.205, bf16[1024,1,128]{2,1,0:T(2,128)(2,1)} %copy.28, s32[]{:T(128)} %constant.317.clone.1, s32[]{:T(128)S(6)} %select_n.268, s32[]{:T(128)} %constant.317.clone.1) | dynamic-update-slice | bytes 524292 | tf_op jit(solution)/shard_map/jit(dynamic_update_index_in_dim)/dynamic_update_slice | solution.py:657
  52.2 2.1 copy.29
  54.4 12.1 %dynamic_update_slice.176 = bf16[1024,8,128]{2,1,0:T(8,128)(2,1)S(1)} dynamic-update-slice(bf16[1024,8,128]{2,1,0:T(8,128)(2,1)S(1)} %dynamic_update_slice.175, bf16[1024,1,128]{2,1,0:T(2,128)(2,1)} %copy.29, s32[]{:T(128)} %constant.317.clone.1, s32[]{:T(128)S(6)} %select_n.269, s32[]{:T(128)} %constant.317.clone.1) | dynamic-update-slice | bytes 524292 | tf_op jit(solution)/shard_map/jit(dynamic_update_index_in_dim)/dynamic_update_slice | solution.py:657
  73.4 12.1 %dynamic_update_slice.177 = bf16[1024,8,128]{2,1,0:T(8,128)(2,1)S(1)} dynamic-update-slice(bf16[1024,8,128]{2,1,0:T(8,128)(2,1)S(1)} %dynamic_update_slice.176, bf16[1024,1,128]{2,1,0:T(2,128)(2,1)} %copy.30, s32[]{:T(128)} %constant.317.clone.1, s32[]{:T(128)S(6)} %select_n.270, s32[]{:T(128)} %constant.317.clone.1) | dynamic-update-slice | bytes 524292 | tf_op jit(solution)/shard_map/jit(dynamic_update_index_in_dim)/dynamic_update_slice | solution.py:657
  85.6 12.1 %dynamic_update_slice.178 = bf16[1024,8,128]{2,1,0:T(8,128)(2,1)S(1)} dynamic-update-slice(bf16[1024,8,128]{2,1,0:T(8,128)(2,1)S(1)} %dynamic_update_slice.177, bf16[1024,1,128]{2,1,0:T(2,128)(2,1)} %copy.31, s32[]{:T(128)} %constant.317.clone.1, s32[]{:T(128)S(6)} %select_n.271, s32[]{:T(128)} %constant.317.clone.1) | dynamic-update-slice | bytes 524292 | tf_op jit(solution)/shard_map/jit(dynamic_update_index_in_dim)/dynamic_update_slice | solution.py:657
  97.7 12.1 %dynamic_update_slice.179 = bf16[1024,8,128]{2,1,0:T(8,128)(2,1)S(1)} dynamic-update-slice(bf16[1024,8,128]{2,1,0:T(8,128)(2,1)S(1)} %dynamic_update_slice.178, bf16[1024,1,128]{2,1,0:T(2,128)(2,1)} %copy.32, s32[]{:T(128)} %constant.317.clone.1, s32[]{:T(128)S(6)} %select_n.272, s32[]{:T(128)} %constant.317.clone.1) | dynamic-update-slice | bytes 524292 | tf_op jit(solution)/shard_map/jit(dynamic_update_index_in_dim)/dynamic_update_slice | solution.py:657
  109.9 12.1 %dynamic_update_slice.180 = bf16[1024,8,128]{2,1,0:T(8,128)(2,1)S(1)} dynamic-update-slice(bf16[1024,8,128]{2,1,0:T(8,128)(2,1)S(1)} %dynamic_update_slice.179, bf16[1024,1,128]{2,1,0:T(2,128)(2,1)} %copy.33, s32[]{:T(128)} %constant.317.clone.1, s32[]{:T(128)S(6)} %select_n.273, s32[]{:T(128)} %constant.317.clone.1) | dynamic-update-slice | bytes 524292 | tf_op jit(solution)/shard_map/jit(dynamic_update_index_in_dim)/dynamic_update_slice | solution.py:657
  125.5 12.1 %dynamic_update_slice.181 = bf16[1024,8,128]{2,1,0:T(8,128)(2,1)S(1)} dynamic-update-slice(bf16[1024,8,128]{2,1,0:T(8,128)(2,1)S(1)} %dynamic_update_slice.180, bf16[1024,1,128]{2,1,0:T(2,128)(2,1)} %copy.34, s32[]{:T(128)} %constant.317.clone.1, s32[]{:T(128)S(6)} %select_n.274, s32[]{:T(128)} %constant.317.clone.1) | dynamic-update-slice | bytes 524292 | tf_op jit(solution)/shard_map/jit(dynamic_update_index_in_dim)/dynamic_update_slice | solution.py:657
  137.6 12.1 %dynamic_update_slice.182 = bf16[1024,8,128]{2,1,0:T(8,128)(2,1)S(1)} dynamic-update-slice(bf16[1024,8,128]{2,1,0:T(8,128)(2,1)S(1)} %dynamic_update_slice.181, bf16[1024,1,128]{2,1,0:T(2,128)(2,1)} %copy.35, s32[]{:T(128)} %constant.317.clone.1, s32[]{:T(128)S(6)} %select_n.275, s32[]{:T(128)} %constant.317.clone.1) | dynamic-update-slice | bytes 524292 | tf_op jit(solution)/shard_map/jit(dynamic_update_index_in_dim)/dynamic_update_slice | solution.py:657
  149.8 3.2 fusion.99
  155.8 3.1 collective-permute-start.14
  161.8 6.3 collective-permute-done.10
  171.4 33.4 %collective-permute-done.12 = bf16[128,2048]{1,0:T(8,128)(2,1)S(1)} collective-permute-done((bf16[128,2048]{1,0:T(8,128)(2,1)}, bf16[128,2048]{1,0:T(8,128)(2,1)S(1)}, u32[]{:S(2)}, u32[]{:S(2)}) %collective-permute-start.12) | collective-permute-done | bytes 524320 | tf_op jit(solution)/shard_map/ppermute | solution.py:385
  213.2 6.5 collective-permute-done.13
  221.1 8.7 %collective-permute-start.8 = (bf16[512,1024]{1,0:T(8,128)(2,1)S(1)}, bf16[512,1024]{1,0:T(8,128)(2,1)S(1)}, u32[]{:S(2)}, u32[]{:S(2)}) collective-permute-start(bf16[512,1024]{1,0:T(8,128)(2,1)S(1)} %fusion.4), channel_id=1, source_target_pairs={{0,8},{8,0},{16,24},{24,16},{1,9},{9,1},{17,25},{25,17},{2,10},{10... | collective-permute-start | bytes 3145736 | tf_op jit(solution)/shard_map/ppermute | solution.py:390
  232.0 4.7 convolution_convert_fusion.2
  241.4 2.2 collective-permute-start.17
  244.7 20.6 %collective-permute-done.36 = bf16[128,2816]{1,0:T(8,128)(2,1)} collective-permute-done((bf16[128,2816]{1,0:T(8,128)(2,1)S(1)}, bf16[128,2816]{1,0:T(8,128)(2,1)}, u32[]{:S(2)}, u32[]{:S(2)}) %collective-permute-start.36) | collective-permute-done | bytes 720928 | tf_op jit(solution)/shard_map/ppermute | solution.py:385
  266.1 2.1 collective-permute-start.38
  269.7 7.7 %collective-permute-done.17 = bf16[256,1536]{1,0:T(8,128)(2,1)S(1)} collective-permute-done((bf16[256,1536]{1,0:T(8,128)(2,1)S(1)}, bf16[256,1536]{1,0:T(8,128)(2,1)S(1)}, u32[]{:S(2)}, u32[]{:S(2)}) %collective-permute-start.17) | collective-permute-done | bytes 786464 | tf_op jit(solution)/shard_map/ppermute | solution.py:400
  277.5 31.5 %collective-permute-done.18 = bf16[256,1536]{1,0:T(8,128)(2,1)S(1)} collective-permute-done((bf16[256,1536]{1,0:T(8,128)(2,1)S(1)}, bf16[256,1536]{1,0:T(8,128)(2,1)S(1)}, u32[]{:S(2)}, u32[]{:S(2)}) %collective-permute-start.18) | collective-permute-done | bytes 786464 | tf_op jit(solution)/shard_map/ppermute | solution.py:400
  310.7 7.5 %attention_forward.1 = (f32[10,256,128]{2,1,0:T(8,128)}, bf16[4,256,512]{2,1,0:T(8,128)(2,1)}) custom-call(bf16[4,256,1536]{2,1,0:T(8,128)(2,1)} %copy-done, bf16[512,128]{1,0:T(8,128)(2,1)} %fusion.65.fold_ref, bf16[128,512]{1,0:T(8,128)(2,1)} %fusion.66.spread_ref), custom_call_target="tpu_custom_call" | custom-call | tf_op jit(solution)/shard_map/attention_forward/pallas_call | solution.py:511
  321.5 2.4 collective-permute-start.22
  323.8 4.2 collective-permute-done.20
  330.1 2.3 collective-permute-start.30
  332.4 3.8 collective-permute-done.22
  337.0 2.7 fusion.100
  339.8 13.2 %collective-permute-done.26 = bf16[128,1408]{1,0:T(8,128)(2,1)S(1)} collective-permute-done((bf16[128,1408]{1,0:T(8,128)(2,1)S(1)}, bf16[128,1408]{1,0:T(8,128)(2,1)S(1)}, u32[]{:S(2)}, u32[]{:S(2)}) %collective-permute-start.26) | collective-permute-done | bytes 360480 | tf_op jit(solution)/shard_map/ppermute | solution.py:385
  353.1 7.5 %collective-permute-done.28 = bf16[128,1408]{1,0:T(8,128)(2,1)S(1)} collective-permute-done((bf16[128,1408]{1,0:T(8,128)(2,1)}, bf16[128,1408]{1,0:T(8,128)(2,1)S(1)}, u32[]{:S(2)}, u32[]{:S(2)}) %collective-permute-start.28) | collective-permute-done | bytes 360480 | tf_op jit(solution)/shard_map/ppermute | solution.py:385
  361.7 6.9 collective-permute-done.29
  368.8 8.8 %collective-permute-done.34 = bf16[128,2816]{1,0:T(8,128)(2,1)S(1)} collective-permute-done((bf16[128,2816]{1,0:T(8,128)(2,1)}, bf16[128,2816]{1,0:T(8,128)(2,1)S(1)}, u32[]{:S(2)}, u32[]{:S(2)}) %collective-permute-start.34) | collective-permute-done | bytes 720928 | tf_op jit(solution)/shard_map/ppermute | solution.py:385
  377.9 9.6 %collective-permute-start.24 = (bf16[512,1024]{1,0:T(8,128)(2,1)S(1)}, bf16[512,1024]{1,0:T(8,128)(2,1)S(1)}, u32[]{:S(2)}, u32[]{:S(2)}) collective-permute-start(bf16[512,1024]{1,0:T(8,128)(2,1)S(1)} %collective-permute-done.19), channel_id=1, source_target_pairs={{0,8},{8,0},{16,24},{24,16},{1,9},{9,1},{17,25},{25,17},{2,10},{10... | collective-permute-start | bytes 3145736 | tf_op jit(solution)/shard_map/ppermute | solution.py:390
  388.5 7.6 %collective-permute-done.35 = bf16[128,2816]{1,0:T(8,128)(2,1)S(1)} collective-permute-done((bf16[128,2816]{1,0:T(8,128)(2,1)S(1)}, bf16[128,2816]{1,0:T(8,128)(2,1)S(1)}, u32[]{:S(2)}, u32[]{:S(2)}) %collective-permute-start.35) | collective-permute-done | bytes 720928 | tf_op jit(solution)/shard_map/ppermute | solution.py:385
  400.3 10.2 %fusion.6 = f32[1024,2816]{1,0:T(8,128)} fusion(bf16[1024,2816]{1,0:T(8,128)(2,1)S(1)} %bitcast.275, bf16[512,1024]{1,0:T(8,128)(2,1)S(1)} %collective-permute-done.32, bf16[512,1024]{1,0:T(8,128)(2,1)S(1)} %multiply_convert_fusion.3), kind=kOutput, calls=%fused_computation.75 | convolution fusion | flops 5909774336 | bytes 19398656 | tf_op jit(solution)/shard_map/dot_general | solution.py:706
  410.5 10.1 %multiply_convert_fusion.2 = (bf16[1024,1408]{1,0:T(8,128)(2,1)}, bf16[1024,1408]{1,0:T(8,128)(2,1)}, bf16[1024,1408]{1,0:T(8,128)(2,1)}) fusion(f32[1024,2816]{1,0:T(8,128)} %fusion.6, bf16[1024,1024]{1,0:T(8,128)(2,1)S(1)} %constant_dynamic-update-slice_fusion, bf16[1024,1408]{1,0:T(8,128)(2,1)S(1)} %bitcast.283), kind=kOutput, calls=%fused_computation.4 | convolution fusion | flops 2974416896 | bytes 25165824 | tf_op jit(solution)/shard_map/dot_general | solution.py:706
  420.6 8.3 %fusion.11 = f32[1024,1024]{1,0:T(8,128)S(1)} fusion(bf16[1024,2816]{1,0:T(8,128)(2,1)S(1)} %bitcast.276, bf16[1024,1408]{1,0:T(8,128)(2,1)} %get-tuple-element.70, bf16[1024,1408]{1,0:T(8,128)(2,1)} %get-tuple-element.69), kind=kOutput, calls=%fused_computation.95 | convolution fusion | flops 5917114368 | bytes 15728640 | tf_op jit(solution)/shard_map/dot_general | solution.py:709
  429.2 5.4 fusion.102
  440.7 2.6 fusion.95
  443.4 27.4 %collective-permute-done.53 = bf16[512,1408]{1,0:T(8,128)(2,1)S(1)} collective-permute-done((bf16[512,1408]{1,0:T(8,128)(2,1)S(1)}, bf16[512,1408]{1,0:T(8,128)(2,1)S(1)}, u32[]{:S(2)}, u32[]{:S(2)}) %collective-permute-start.53) | collective-permute-done | bytes 1441824 | tf_op jit(solution)/shard_map/ppermute | solution.py:385
  472.8 4.7 collective-permute-start.56
  478.2 5.0 convolution_convert_fusion
  483.5 3.3 collective-permute-done.56
  486.9 7.3 collective-permute-done.55
  494.1 13.2 %collective-permute-done.54 = bf16[128,1408]{1,0:T(8,128)(2,1)S(1)} collective-permute-done((bf16[128,1408]{1,0:T(8,128)(2,1)S(1)}, bf16[128,1408]{1,0:T(8,128)(2,1)S(1)}, u32[]{:S(2)}, u32[]{:S(2)}) %collective-permute-start.54) | collective-permute-done | bytes 360480 | tf_op jit(solution)/shard_map/ppermute | solution.py:385
  508.8 2.5 fusion.12
  515.8 2.6 collective-permute-start.44
  520.6 4.8 collective-permute-done.44
  526.4 8.6 %attention_backward.1 = bf16[4,256,1536]{2,1,0:T(8,128)(2,1)} custom-call(bf16[4,256,1536]{2,1,0:T(8,128)(2,1)} %copy-done, f32[10,256,128]{2,1,0:T(8,128)} %get-tuple-element.29.probs_ref, bf16[4,256,512]{2,1,0:T(8,128)(2,1)} %copy-done.7, bf16[512,128]{1,0:T(8,128)(2,1)} %fusion.65.fold_ref, bf16[128,512]{1,0:T(8,128)(2,1)} %fusion.66.spread_ref), custom_call_target="tpu_custom_call" | custom-call | tf_op jit(solution)/shard_map/attention_backward/pallas_call | solution.py:535
  538.4 2.4 collective-permute-start.47
  540.8 5.8 collective-permute-done.49
  546.6 5.9 add_convert_fusion
  554.0 3.5 collective-permute-start.52
  558.6 48.3 %collective-permute-done.47 = bf16[256,1536]{1,0:T(8,128)(2,1)S(1)} collective-permute-done((bf16[256,1536]{1,0:T(8,128)(2,1)S(1)}, bf16[256,1536]{1,0:T(8,128)(2,1)S(1)}, u32[]{:S(2)}, u32[]{:S(2)}) %collective-permute-start.47) | collective-permute-done | bytes 786464 | tf_op jit(solution)/shard_map/ppermute | solution.py:400
  608.4 3.0 convolution_convert_fusion.6
  611.4 3.0 convolution_convert_fusion.5
  614.4 2.8 convolution_convert_fusion.7.part_send
  617.2 3.1 fusion.101.part_own
  620.3 89.4 %tail.1 = (f32[2,128,1536]{2,1,0:T(8,128)}, f32[2,128,512]{2,1,0:T(8,128)}, f32[512,1024]{1,0:T(8,128)}, bf16[512,1024]{1,0:T(8,128)(2,1)}, f32[512,1024]{1,0:T(8,128)}, /*index=5*/f32[32,4224]{1,0:T(8,128)}) custom-call(bf16[512,1024]{1,0:T(8,128)(2,1)} %convolution_convert_fusion.7.part_send, f32[512,1024]{1,0:T(8,128)} %fusion.101.part_own, ...), custom_call_target="tpu_custom_call" | custom-call | tf_op jit(solution)/shard_map/tail/pallas_call | solution.py:360
  713.8 3.5 copy.36
  717.2 3.5 copy.37
  (332 shorter events, 111.3 us)
Async XLA Ops:
  3.8 155.4 %collective-permute-start.9 = (bf16[128,2048]{1,0:T(8,128)(2,1)}, bf16[128,2048]{1,0:T(8,128)(2,1)}, u32[]{:S(2)}, u32[]{:S(2)}) collective-permute-start(bf16[128,2048]{1,0:T(8,128)(2,1)} %pad_maximum_fusion.21), channel_id=1, source_target_pairs={{0,1},{1,0},{2,3},{3,2},{4,5},{5,4},{6,7},{7,6},{8,9},{9,8},{10,11... | collective-permute-start | bytes 1572872 | tf_op jit(solution)/shard_map/ppermute | solution.py:385
  7.8 14.3 %collective-permute-start = (bf16[1,1024,128]{2,1,0:T(8,128)(2,1)S(1)}, bf16[1,1024,128]{2,1,0:T(8,128)(2,1)S(1)}, u32[]{:S(2)}, u32[]{:S(2)}) collective-permute-start(bf16[1,1024,128]{2,1,0:T(8,128)(2,1)S(1)} %get-tuple-element.138), channel_id=1, source_target_pairs={{0,4},{1,5},{2,6},{3,7},{4,0},{5,1},{6,2},{7,3},{8,12},{9,13},{10,... | collective-permute-start | bytes 786440 | tf_op jit(solution)/shard_map/ppermute | solution.py:385
  23.0 13.1 %collective-permute-start.1 = (bf16[2,1024,128]{2,1,0:T(8,128)(2,1)}, bf16[2,1024,128]{2,1,0:T(8,128)(2,1)}, u32[]{:S(2)}, u32[]{:S(2)}) collective-permute-start(bf16[2,1024,128]{2,1,0:T(8,128)(2,1)} %pad_maximum_fusion.20), channel_id=1, source_target_pairs={{0,2},{1,3},{2,0},{3,1},{4,6},{5,7},{6,4},{7,5},{8,10},{9,11},{10,... | collective-permute-start | bytes 1572872 | tf_op jit(solution)/shard_map/ppermute | solution.py:385
  25.2 44.8 %collective-permute-start.2 = (bf16[2,1024,128]{2,1,0:T(8,128)(2,1)}, bf16[2,1024,128]{2,1,0:T(8,128)(2,1)}, u32[]{:S(2)}, u32[]{:S(2)}) collective-permute-start(bf16[2,1024,128]{2,1,0:T(8,128)(2,1)} %pad_maximum_fusion.20), channel_id=1, source_target_pairs={{0,1},{1,0},{2,3},{3,2},{4,5},{5,4},{6,7},{7,6},{8,9},{9,8},{10,11... | collective-permute-start | bytes 1572872 | tf_op jit(solution)/shard_map/ppermute | solution.py:385
  36.1 85.9 %collective-permute-start.3 = (bf16[2,1024,128]{2,1,0:T(8,128)(2,1)}, bf16[2,1024,128]{2,1,0:T(8,128)(2,1)}, u32[]{:S(2)}, u32[]{:S(2)}) collective-permute-start(bf16[2,1024,128]{2,1,0:T(8,128)(2,1)} %collective-permute-done.1), channel_id=1, source_target_pairs={{0,1},{1,0},{2,3},{3,2},{4,5},{5,4},{6,7},{7,6},{8,9},{9,8},{10,11... | collective-permute-start | bytes 1572872 | tf_op jit(solution)/shard_map/ppermute | solution.py:385
  153.1 16.6 %collective-permute-start.4 = (bf16[512,1024]{1,0:T(8,128)(2,1)S(1)}, bf16[512,1024]{1,0:T(8,128)(2,1)S(1)}, u32[]{:S(2)}, u32[]{:S(2)}) collective-permute-start(bf16[512,1024]{1,0:T(8,128)(2,1)S(1)} %get-tuple-element.155), channel_id=1, source_target_pairs={{0,8},{8,0},{16,24},{24,16},{1,9},{9,1},{17,25},{25,17},{2,10},{10... | collective-permute-start | bytes 3145736 | tf_op jit(solution)/shard_map/ppermute | solution.py:390
  154.1 53.4 %copy-start.28 = (bf16[128,2816]{1,0:T(8,128)(2,1)S(1)}, bf16[128,2816]{1,0:T(8,128)(2,1)}, u32[]{:S(2)}) copy-start(bf16[128,2816]{1,0:T(8,128)(2,1)} %get-tuple-element.37) | copy-start | bytes 2162692
  154.1 14.0 %collective-permute-start.10 = (bf16[128,2048]{1,0:T(8,128)(2,1)S(1)}, bf16[128,2048]{1,0:T(8,128)(2,1)S(1)}, u32[]{:S(2)}, u32[]{:S(2)}) collective-permute-start(bf16[128,2048]{1,0:T(8,128)(2,1)S(1)} %copy-done.30), channel_id=1, source_target_pairs={{0,2},{1,3},{2,0},{3,1},{4,6},{5,7},{6,4},{7,5},{8,10},{9,11},{10,... | collective-permute-start | bytes 1572872 | tf_op jit(solution)/shard_map/ppermute | solution.py:385
  155.8 50.5 %collective-permute-start.14 = (bf16[128,2048]{1,0:T(8,128)(2,1)S(1)}, bf16[128,2048]{1,0:T(8,128)(2,1)S(1)}, u32[]{:S(2)}, u32[]{:S(2)}) collective-permute-start(bf16[128,2048]{1,0:T(8,128)(2,1)S(1)} %copy-done.30), channel_id=1, source_target_pairs={{0,6},{1,7},{2,4},{3,5},{4,2},{5,3},{6,0},{7,1},{8,14},{9,15},{10,... | collective-permute-start | bytes 1572872 | tf_op jit(solution)/shard_map/ppermute | solution.py:385
  158.9 45.9 %collective-permute-start.12 = (bf16[128,2048]{1,0:T(8,128)(2,1)}, bf16[128,2048]{1,0:T(8,128)(2,1)S(1)}, u32[]{:S(2)}, u32[]{:S(2)}) collective-permute-start(bf16[128,2048]{1,0:T(8,128)(2,1)} %pad_maximum_fusion.21), channel_id=1, source_target_pairs={{0,4},{1,5},{2,6},{3,7},{4,0},{5,1},{6,2},{7,3},{8,12},{9,13},{10,... | collective-permute-start | bytes 1572872 | tf_op jit(solution)/shard_map/ppermute | solution.py:385
  168.1 40.9 %collective-permute-start.11 = (bf16[128,2048]{1,0:T(8,128)(2,1)S(1)}, bf16[128,2048]{1,0:T(8,128)(2,1)S(1)}, u32[]{:S(2)}, u32[]{:S(2)}) collective-permute-start(bf16[128,2048]{1,0:T(8,128)(2,1)S(1)} %collective-permute-done.10), channel_id=1, source_target_pairs={{0,1},{1,0},{2,3},{3,2},{4,5},{5,4},{6,7},{7,6},{8,9},{9,8},{10,11... | collective-permute-start | bytes 1572872 | tf_op jit(solution)/shard_map/ppermute | solution.py:385
  169.8 39.9 %collective-permute-start.5 = (bf16[256,1024]{1,0:T(8,128)(2,1)S(1)}, bf16[256,1024]{1,0:T(8,128)(2,1)S(1)}, u32[]{:S(2)}, u32[]{:S(2)}) collective-permute-start(bf16[256,1024]{1,0:T(8,128)(2,1)S(1)} %fusion.33), channel_id=1, source_target_pairs={{0,16},{8,24},{16,0},{24,8},{1,17},{9,25},{17,1},{25,9},{2,18},{10... | collective-permute-start | bytes 1572872 | tf_op jit(solution)/shard_map/ppermute | solution.py:390
  204.8 14.9 %collective-permute-start.13 = (bf16[128,2048]{1,0:T(8,128)(2,1)S(1)}, bf16[128,2048]{1,0:T(8,128)(2,1)S(1)}, u32[]{:S(2)}, u32[]{:S(2)}) collective-permute-start(bf16[128,2048]{1,0:T(8,128)(2,1)S(1)} %collective-permute-done.12), channel_id=1, source_target_pairs={{0,1},{1,0},{2,3},{3,2},{4,5},{5,4},{6,7},{7,6},{8,9},{9,8},{10,11... | collective-permute-start | bytes 1572872 | tf_op jit(solution)/shard_map/ppermute | solution.py:385
  206.3 24.6 %collective-permute-start.15 = (bf16[128,2048]{1,0:T(8,128)(2,1)S(1)}, bf16[128,2048]{1,0:T(8,128)(2,1)S(1)}, u32[]{:S(2)}, u32[]{:S(2)}) collective-permute-start(bf16[128,2048]{1,0:T(8,128)(2,1)S(1)} %collective-permute-done.14), channel_id=1, source_target_pairs={{0,1},{1,0},{2,3},{3,2},{4,5},{5,4},{6,7},{7,6},{8,9},{9,8},{10,11... | collective-permute-start | bytes 1572872 | tf_op jit(solution)/shard_map/ppermute | solution.py:385
  207.5 37.1 %collective-permute-start.33 = (bf16[128,2816]{1,0:T(8,128)(2,1)S(1)}, bf16[128,2816]{1,0:T(8,128)(2,1)S(1)}, u32[]{:S(2)}, u32[]{:S(2)}) collective-permute-start(bf16[128,2816]{1,0:T(8,128)(2,1)S(1)} %copy-done.28), channel_id=1, source_target_pairs={{0,1},{1,0},{2,3},{3,2},{4,5},{5,4},{6,7},{7,6},{8,9},{9,8},{10,11... | collective-permute-start | bytes 2162696 | tf_op jit(solution)/shard_map/ppermute | solution.py:385
  210.0 2.0 collective-permute-start.6
  212.5 7.9 %collective-permute-start.7 = (bf16[512,1024]{1,0:T(8,128)(2,1)S(1)}, bf16[512,1024]{1,0:T(8,128)(2,1)S(1)}, u32[]{:S(2)}, u32[]{:S(2)}) collective-permute-start(bf16[512,1024]{1,0:T(8,128)(2,1)S(1)} %fusion.10), channel_id=1, source_target_pairs={{0,0},{1,1},{2,8},{3,9},{4,4},{5,5},{6,12},{7,13},{8,2},{9,3},{10,... | collective-permute-start | bytes 3145736 | tf_op jit(solution)/shard_map/ppermute | solution.py:400
  221.1 11.0 %collective-permute-start.8 = (bf16[512,1024]{1,0:T(8,128)(2,1)S(1)}, bf16[512,1024]{1,0:T(8,128)(2,1)S(1)}, u32[]{:S(2)}, u32[]{:S(2)}) collective-permute-start(bf16[512,1024]{1,0:T(8,128)(2,1)S(1)} %fusion.4), channel_id=1, source_target_pairs={{0,8},{8,0},{16,24},{24,16},{1,9},{9,1},{17,25},{25,17},{2,10},{10... | collective-permute-start | bytes 3145736 | tf_op jit(solution)/shard_map/ppermute | solution.py:390
  231.0 34.3 %collective-permute-start.36 = (bf16[128,2816]{1,0:T(8,128)(2,1)S(1)}, bf16[128,2816]{1,0:T(8,128)(2,1)}, u32[]{:S(2)}, u32[]{:S(2)}) collective-permute-start(bf16[128,2816]{1,0:T(8,128)(2,1)S(1)} %copy-done.28), channel_id=1, source_target_pairs={{0,4},{1,5},{2,6},{3,7},{4,0},{5,1},{6,2},{7,3},{8,12},{9,13},{10,... | collective-permute-start | bytes 2162696 | tf_op jit(solution)/shard_map/ppermute | solution.py:385
  237.2 30.9 %collective-permute-start.16 = (bf16[256,1536]{1,0:T(8,128)(2,1)S(1)}, bf16[256,1536]{1,0:T(8,128)(2,1)S(1)}, u32[]{:S(2)}, u32[]{:S(2)}) collective-permute-start(bf16[256,1536]{1,0:T(8,128)(2,1)S(1)} %get-tuple-element.82), channel_id=1, source_target_pairs={{0,16},{1,17},{2,18},{3,19},{4,20},{5,21},{6,22},{7,23},{8,24},{9,... | collective-permute-start | bytes 2359304 | tf_op jit(solution)/shard_map/ppermute | solution.py:400
  241.4 36.0 %collective-permute-start.17 = (bf16[256,1536]{1,0:T(8,128)(2,1)S(1)}, bf16[256,1536]{1,0:T(8,128)(2,1)S(1)}, u32[]{:S(2)}, u32[]{:S(2)}) collective-permute-start(bf16[256,1536]{1,0:T(8,128)(2,1)S(1)} %get-tuple-element.81), channel_id=1, source_target_pairs={{0,2},{1,3},{2,0},{3,1},{4,6},{5,7},{6,4},{7,5},{8,10},{9,11},{10,... | collective-permute-start | bytes 2359304 | tf_op jit(solution)/shard_map/ppermute | solution.py:400
  265.2 132.1 %collective-permute-start.37 = (bf16[128,2816]{1,0:T(8,128)(2,1)}, bf16[128,2816]{1,0:T(8,128)(2,1)}, u32[]{:S(2)}, u32[]{:S(2)}) collective-permute-start(bf16[128,2816]{1,0:T(8,128)(2,1)} %collective-permute-done.36), channel_id=1, source_target_pairs={{0,1},{1,0},{2,3},{3,2},{4,5},{5,4},{6,7},{7,6},{8,9},{9,8},{10,11... | collective-permute-start | bytes 2162696 | tf_op jit(solution)/shard_map/ppermute | solution.py:385
  265.8 43.2 %collective-permute-start.18 = (bf16[256,1536]{1,0:T(8,128)(2,1)S(1)}, bf16[256,1536]{1,0:T(8,128)(2,1)S(1)}, u32[]{:S(2)}, u32[]{:S(2)}) collective-permute-start(bf16[256,1536]{1,0:T(8,128)(2,1)S(1)} %get-tuple-element.80), channel_id=1, source_target_pairs={{0,18},{1,19},{2,16},{3,17},{4,22},{5,23},{6,20},{7,21},{8,26},{9,... | collective-permute-start | bytes 2359304 | tf_op jit(solution)/shard_map/ppermute | solution.py:400
  266.1 54.8 %collective-permute-start.38 = (bf16[128,2816]{1,0:T(8,128)(2,1)}, bf16[128,2816]{1,0:T(8,128)(2,1)}, u32[]{:S(2)}, u32[]{:S(2)}) collective-permute-start(bf16[128,2816]{1,0:T(8,128)(2,1)} %get-tuple-element.38), channel_id=1, source_target_pairs={{0,6},{1,7},{2,4},{3,5},{4,2},{5,3},{6,0},{7,1},{8,14},{9,15},{10,... | collective-permute-start | bytes 2162696 | tf_op jit(solution)/shard_map/ppermute | solution.py:385
  268.2 52.6 %collective-permute-start.25 = (bf16[128,1408]{1,0:T(8,128)(2,1)}, bf16[128,1408]{1,0:T(8,128)(2,1)S(1)}, u32[]{:S(2)}, u32[]{:S(2)}) collective-permute-start(bf16[128,1408]{1,0:T(8,128)(2,1)} %get-tuple-element.34), channel_id=1, source_target_pairs={{0,1},{1,0},{2,3},{3,2},{4,5},{5,4},{6,7},{7,6},{8,9},{9,8},{10,11... | collective-permute-start | bytes 1081352 | tf_op jit(solution)/shard_map/ppermute | solution.py:385
  319.7 8.4 %collective-permute-start.20 = (bf16[256,512]{1,0:T(8,128)(2,1)S(1)}, bf16[256,512]{1,0:T(8,128)(2,1)S(1)}, u32[]{:S(2)}, u32[]{:S(2)}) collective-permute-start(bf16[256,512]{1,0:T(8,128)(2,1)S(1)} %get-tuple-element.133), channel_id=1, source_target_pairs={{0,16},{1,17},{2,18},{3,19},{4,20},{5,21},{6,22},{7,23},{8,24},{9,... | collective-permute-start | bytes 786440 | tf_op jit(solution)/shard_map/ppermute | solution.py:400
  320.8 9.2 %collective-permute-start.21 = (bf16[256,512]{1,0:T(8,128)(2,1)S(1)}, bf16[256,512]{1,0:T(8,128)(2,1)S(1)}, u32[]{:S(2)}, u32[]{:S(2)}) collective-permute-start(bf16[256,512]{1,0:T(8,128)(2,1)S(1)} %get-tuple-element.132), channel_id=1, source_target_pairs={{0,2},{1,3},{2,0},{3,1},{4,6},{5,7},{6,4},{7,5},{8,10},{9,11},{10,... | collective-permute-start | bytes 786440 | tf_op jit(solution)/shard_map/ppermute | solution.py:400
  320.9 78.8 %collective-permute-start.39 = (bf16[128,2816]{1,0:T(8,128)(2,1)}, bf16[128,2816]{1,0:T(8,128)(2,1)S(1)}, u32[]{:S(2)}, u32[]{:S(2)}) collective-permute-start(bf16[128,2816]{1,0:T(8,128)(2,1)} %collective-permute-done.38), channel_id=1, source_target_pairs={{0,1},{1,0},{2,3},{3,2},{4,5},{5,4},{6,7},{7,6},{8,9},{9,8},{10,11... | collective-permute-start | bytes 2162696 | tf_op jit(solution)/shard_map/ppermute | solution.py:385
  321.5 14.8 %collective-permute-start.22 = (bf16[256,512]{1,0:T(8,128)(2,1)S(1)}, bf16[256,512]{1,0:T(8,128)(2,1)S(1)}, u32[]{:S(2)}, u32[]{:S(2)}) collective-permute-start(bf16[256,512]{1,0:T(8,128)(2,1)S(1)} %get-tuple-element.131), channel_id=1, source_target_pairs={{0,18},{1,19},{2,16},{3,17},{4,22},{5,23},{6,20},{7,21},{8,26},{9,... | collective-permute-start | bytes 786440 | tf_op jit(solution)/shard_map/ppermute | solution.py:400
  328.1 25.0 %collective-permute-start.26 = (bf16[128,1408]{1,0:T(8,128)(2,1)S(1)}, bf16[128,1408]{1,0:T(8,128)(2,1)S(1)}, u32[]{:S(2)}, u32[]{:S(2)}) collective-permute-start(bf16[128,1408]{1,0:T(8,128)(2,1)S(1)} %copy-done.32), channel_id=1, source_target_pairs={{0,2},{1,3},{2,0},{3,1},{4,6},{5,7},{6,4},{7,5},{8,10},{9,11},{10,... | collective-permute-start | bytes 1081352 | tf_op jit(solution)/shard_map/ppermute | solution.py:385
  330.1 30.9 %collective-permute-start.30 = (bf16[128,1408]{1,0:T(8,128)(2,1)S(1)}, bf16[128,1408]{1,0:T(8,128)(2,1)S(1)}, u32[]{:S(2)}, u32[]{:S(2)}) collective-permute-start(bf16[128,1408]{1,0:T(8,128)(2,1)S(1)} %copy-done.32), channel_id=1, source_target_pairs={{0,6},{1,7},{2,4},{3,5},{4,2},{5,3},{6,0},{7,1},{8,14},{9,15},{10,... | collective-permute-start | bytes 1081352 | tf_op jit(solution)/shard_map/ppermute | solution.py:385
  336.2 24.4 %collective-permute-start.28 = (bf16[128,1408]{1,0:T(8,128)(2,1)}, bf16[128,1408]{1,0:T(8,128)(2,1)S(1)}, u32[]{:S(2)}, u32[]{:S(2)}) collective-permute-start(bf16[128,1408]{1,0:T(8,128)(2,1)} %get-tuple-element.34), channel_id=1, source_target_pairs={{0,4},{1,5},{2,6},{3,7},{4,0},{5,1},{6,2},{7,3},{8,12},{9,13},{10,... | collective-permute-start | bytes 1081352 | tf_op jit(solution)/shard_map/ppermute | solution.py:385
  337.0 40.9 %slice-start = ((s8[5767168]{0:T(1024)(128)(4,1)}), s8[4194304]{0:T(1024)(128)(4,1)S(1)}, s32[]{:S(2)}) async-start(s8[5767168]{0:T(1024)(128)(4,1)} %bitcast.273), calls=%async_computation | async-start | bytes 8388608
  337.0 40.9 %slice-start.1 = ((s8[5767168]{0:T(1024)(128)(4,1)}), s8[1572864]{0:T(1024)(128)(4,1)S(1)}, s32[]{:S(2)}) async-start(s8[5767168]{0:T(1024)(128)(4,1)} %bitcast.273), calls=%async_computation.1 | async-start | bytes 3145728
  353.0 7.6 %collective-permute-start.27 = (bf16[128,1408]{1,0:T(8,128)(2,1)S(1)}, bf16[128,1408]{1,0:T(8,128)(2,1)S(1)}, u32[]{:S(2)}, u32[]{:S(2)}) collective-permute-start(bf16[128,1408]{1,0:T(8,128)(2,1)S(1)} %collective-permute-done.26), channel_id=1, source_target_pairs={{0,1},{1,0},{2,3},{3,2},{4,5},{5,4},{6,7},{7,6},{8,9},{9,8},{10,11... | collective-permute-start | bytes 1081352 | tf_op jit(solution)/shard_map/ppermute | solution.py:385
  360.7 16.9 %collective-permute-start.34 = (bf16[128,2816]{1,0:T(8,128)(2,1)}, bf16[128,2816]{1,0:T(8,128)(2,1)S(1)}, u32[]{:S(2)}, u32[]{:S(2)}) collective-permute-start(bf16[128,2816]{1,0:T(8,128)(2,1)} %get-tuple-element.38), channel_id=1, source_target_pairs={{0,2},{1,3},{2,0},{3,1},{4,6},{5,7},{6,4},{7,5},{8,10},{9,11},{10,... | collective-permute-start | bytes 2162696 | tf_op jit(solution)/shard_map/ppermute | solution.py:385
  360.7 8.0 %collective-permute-start.29 = (bf16[128,1408]{1,0:T(8,128)(2,1)S(1)}, bf16[128,1408]{1,0:T(8,128)(2,1)S(1)}, u32[]{:S(2)}, u32[]{:S(2)}) collective-permute-start(bf16[128,1408]{1,0:T(8,128)(2,1)S(1)} %collective-permute-done.28), channel_id=1, source_target_pairs={{0,1},{1,0},{2,3},{3,2},{4,5},{5,4},{6,7},{7,6},{8,9},{9,8},{10,11... | collective-permute-start | bytes 1081352 | tf_op jit(solution)/shard_map/ppermute | solution.py:385
  361.0 16.9 %collective-permute-start.19 = (bf16[512,1024]{1,0:T(8,128)(2,1)S(1)}, bf16[512,1024]{1,0:T(8,128)(2,1)S(1)}, u32[]{:S(2)}, u32[]{:S(2)}) collective-permute-start(bf16[512,1024]{1,0:T(8,128)(2,1)S(1)} %copy-done.25), channel_id=1, source_target_pairs={{0,0},{1,1},{2,8},{3,9},{4,4},{5,5},{6,12},{7,13},{8,2},{9,3},{10,... | collective-permute-start | bytes 3145736 | tf_op jit(solution)/shard_map/ppermute | solution.py:400
  368.7 8.9 %collective-permute-start.31 = (bf16[128,1408]{1,0:T(8,128)(2,1)S(1)}, bf16[128,1408]{1,0:T(8,128)(2,1)S(1)}, u32[]{:S(2)}, u32[]{:S(2)}) collective-permute-start(bf16[128,1408]{1,0:T(8,128)(2,1)S(1)} %collective-permute-done.30), channel_id=1, source_target_pairs={{0,1},{1,0},{2,3},{3,2},{4,5},{5,4},{6,7},{7,6},{8,9},{9,8},{10,11... | collective-permute-start | bytes 1081352 | tf_op jit(solution)/shard_map/ppermute | solution.py:385
  377.6 10.0 %collective-permute-start.23 = (bf16[512,1024]{1,0:T(8,128)(2,1)S(1)}, bf16[512,1024]{1,0:T(8,128)(2,1)S(1)}, u32[]{:S(2)}, u32[]{:S(2)}) collective-permute-start(bf16[512,1024]{1,0:T(8,128)(2,1)S(1)} %slice.583), channel_id=1, source_target_pairs={{0,8},{8,0},{16,24},{24,16},{1,9},{9,1},{17,25},{25,17},{2,10},{10... | collective-permute-start | bytes 3145736 | tf_op jit(solution)/shard_map/ppermute | solution.py:390
  377.6 18.6 %collective-permute-start.35 = (bf16[128,2816]{1,0:T(8,128)(2,1)S(1)}, bf16[128,2816]{1,0:T(8,128)(2,1)S(1)}, u32[]{:S(2)}, u32[]{:S(2)}) collective-permute-start(bf16[128,2816]{1,0:T(8,128)(2,1)S(1)} %collective-permute-done.34), channel_id=1, source_target_pairs={{0,1},{1,0},{2,3},{3,2},{4,5},{5,4},{6,7},{7,6},{8,9},{9,8},{10,11... | collective-permute-start | bytes 2162696 | tf_op jit(solution)/shard_map/ppermute | solution.py:385
  377.9 21.8 %collective-permute-start.24 = (bf16[512,1024]{1,0:T(8,128)(2,1)S(1)}, bf16[512,1024]{1,0:T(8,128)(2,1)S(1)}, u32[]{:S(2)}, u32[]{:S(2)}) collective-permute-start(bf16[512,1024]{1,0:T(8,128)(2,1)S(1)} %collective-permute-done.19), channel_id=1, source_target_pairs={{0,8},{8,0},{16,24},{24,16},{1,9},{9,1},{17,25},{25,17},{2,10},{10... | collective-permute-start | bytes 3145736 | tf_op jit(solution)/shard_map/ppermute | solution.py:390
  388.4 11.8 %collective-permute-start.32 = (bf16[512,1024]{1,0:T(8,128)(2,1)S(1)}, bf16[512,1024]{1,0:T(8,128)(2,1)S(1)}, u32[]{:S(2)}, u32[]{:S(2)}) collective-permute-start(bf16[512,1024]{1,0:T(8,128)(2,1)S(1)} %multiply_convert_fusion.3), channel_id=1, source_target_pairs={{0,8},{8,0},{16,24},{24,16},{1,9},{9,1},{17,25},{25,17},{2,10},{10... | collective-permute-start | bytes 3145736 | tf_op jit(solution)/shard_map/ppermute | solution.py:390
  429.1 10.3 %collective-permute-start.40 = (bf16[512,1024]{1,0:T(8,128)(2,1)S(1)}, bf16[512,1024]{1,0:T(8,128)(2,1)S(1)}, u32[]{:S(2)}, u32[]{:S(2)}) collective-permute-start(bf16[512,1024]{1,0:T(8,128)(2,1)S(1)} %slice.582), channel_id=1, source_target_pairs={{0,8},{8,0},{16,24},{24,16},{1,9},{9,1},{17,25},{25,17},{2,10},{10... | collective-permute-start | bytes 3145736 | tf_op jit(solution)/shard_map/ppermute | solution.py:390
  434.8 5.9 collective-permute-start.48
  437.2 33.6 %collective-permute-start.53 = (bf16[512,1408]{1,0:T(8,128)(2,1)S(1)}, bf16[512,1408]{1,0:T(8,128)(2,1)S(1)}, u32[]{:S(2)}, u32[]{:S(2)}) collective-permute-start(bf16[512,1408]{1,0:T(8,128)(2,1)S(1)} %convolution_convert_fusion.3), channel_id=1, source_target_pairs={{0,1},{1,0},{2,3},{3,2},{4,5},{5,4},{6,7},{7,6},{8,9},{9,8},{10,11... | collective-permute-start | bytes 4325384 | tf_op jit(solution)/shard_map/ppermute | solution.py:385
  439.4 38.8 %copy-start.39 = (bf16[1024,128]{1,0:T(8,128)(2,1)}, bf16[1024,128]{1,0:T(8,128)(2,1)S(1)}, u32[]{:S(2)}) copy-start(bf16[1024,128]{1,0:T(8,128)(2,1)S(1)} %get-tuple-element.97) | copy-start | bytes 786436
  439.4 38.8 %copy-start.41 = (bf16[1024,128]{1,0:T(8,128)(2,1)}, bf16[1024,128]{1,0:T(8,128)(2,1)S(1)}, u32[]{:S(2)}) copy-start(bf16[1024,128]{1,0:T(8,128)(2,1)S(1)} %get-tuple-element.98) | copy-start | bytes 786436
  439.4 38.8 %copy-start.43 = (bf16[1024,128]{1,0:T(8,128)(2,1)}, bf16[1024,128]{1,0:T(8,128)(2,1)S(1)}, u32[]{:S(2)}) copy-start(bf16[1024,128]{1,0:T(8,128)(2,1)S(1)} %get-tuple-element.99) | copy-start | bytes 786436
  443.3 65.4 %collective-permute-start.41 = (bf16[512,1024]{1,0:T(8,128)(2,1)S(1)}, bf16[512,1024]{1,0:T(8,128)(2,1)S(1)}, u32[]{:S(2)}, u32[]{:S(2)}) collective-permute-start(bf16[512,1024]{1,0:T(8,128)(2,1)S(1)} %get-tuple-element.65), channel_id=1, source_target_pairs={{0,8},{8,0},{16,24},{24,16},{1,9},{9,1},{17,25},{25,17},{2,10},{10... | collective-permute-start | bytes 3145736 | tf_op jit(solution)/shard_map/ppermute | solution.py:390
  472.8 14.0 %collective-permute-start.56 = (bf16[128,1408]{1,0:T(8,128)(2,1)S(1)}, bf16[128,1408]{1,0:T(8,128)(2,1)S(1)}, u32[]{:S(2)}, u32[]{:S(2)}) collective-permute-start(bf16[128,1408]{1,0:T(8,128)(2,1)S(1)} %get-tuple-element.123), channel_id=1, source_target_pairs={{0,6},{1,7},{2,4},{3,5},{4,2},{5,3},{6,0},{7,1},{8,14},{9,15},{10,... | collective-permute-start | bytes 1081352 | tf_op jit(solution)/shard_map/ppermute | solution.py:385
  477.5 16.6 %collective-permute-start.55 = (bf16[128,1408]{1,0:T(8,128)(2,1)S(1)}, bf16[128,1408]{1,0:T(8,128)(2,1)S(1)}, u32[]{:S(2)}, u32[]{:S(2)}) collective-permute-start(bf16[128,1408]{1,0:T(8,128)(2,1)S(1)} %get-tuple-element.124), channel_id=1, source_target_pairs={{0,2},{1,3},{2,0},{3,1},{4,6},{5,7},{6,4},{7,5},{8,10},{9,11},{10,... | collective-permute-start | bytes 1081352 | tf_op jit(solution)/shard_map/ppermute | solution.py:385
  477.5 29.9 %collective-permute-start.54 = (bf16[128,1408]{1,0:T(8,128)(2,1)S(1)}, bf16[128,1408]{1,0:T(8,128)(2,1)S(1)}, u32[]{:S(2)}, u32[]{:S(2)}) collective-permute-start(bf16[128,1408]{1,0:T(8,128)(2,1)S(1)} %get-tuple-element.122), channel_id=1, source_target_pairs={{0,4},{1,5},{2,6},{3,7},{4,0},{5,1},{6,2},{7,3},{8,12},{9,13},{10,... | collective-permute-start | bytes 1081352 | tf_op jit(solution)/shard_map/ppermute | solution.py:385
  483.2 63.3 %collective-permute-start.49 = (bf16[512,2816]{1,0:T(8,128)(2,1)}, bf16[512,2816]{1,0:T(8,128)(2,1)}, u32[]{:S(2)}, u32[]{:S(2)}) collective-permute-start(bf16[512,2816]{1,0:T(8,128)(2,1)} %convolution_convert_fusion), channel_id=1, source_target_pairs={{0,1},{1,0},{2,3},{3,2},{4,5},{5,4},{6,7},{7,6},{8,9},{9,8},{10,11... | collective-permute-start | bytes 8650760 | tf_op jit(solution)/shard_map/ppermute | solution.py:385
  511.4 7.8 %collective-permute-start.42 = (bf16[256,512]{1,0:T(8,128)(2,1)S(1)}, bf16[256,512]{1,0:T(8,128)(2,1)S(1)}, u32[]{:S(2)}, u32[]{:S(2)}) collective-permute-start(bf16[256,512]{1,0:T(8,128)(2,1)S(1)} %get-tuple-element.129), channel_id=1, source_target_pairs={{0,16},{1,17},{2,18},{3,19},{4,20},{5,21},{6,22},{7,23},{8,24},{9,... | collective-permute-start | bytes 786440 | tf_op jit(solution)/shard_map/ppermute | solution.py:400
  512.3 8.3 %collective-permute-start.43 = (bf16[256,512]{1,0:T(8,128)(2,1)S(1)}, bf16[256,512]{1,0:T(8,128)(2,1)S(1)}, u32[]{:S(2)}, u32[]{:S(2)}) collective-permute-start(bf16[256,512]{1,0:T(8,128)(2,1)S(1)} %get-tuple-element.128), channel_id=1, source_target_pairs={{0,2},{1,3},{2,0},{3,1},{4,6},{5,7},{6,4},{7,5},{8,10},{9,11},{10,... | collective-permute-start | bytes 786440 | tf_op jit(solution)/shard_map/ppermute | solution.py:400
  515.8 9.6 %collective-permute-start.44 = (bf16[256,512]{1,0:T(8,128)(2,1)S(1)}, bf16[256,512]{1,0:T(8,128)(2,1)S(1)}, u32[]{:S(2)}, u32[]{:S(2)}) collective-permute-start(bf16[256,512]{1,0:T(8,128)(2,1)S(1)} %get-tuple-element.127), channel_id=1, source_target_pairs={{0,18},{1,19},{2,16},{3,17},{4,22},{5,23},{6,20},{7,21},{8,26},{9,... | collective-permute-start | bytes 786440 | tf_op jit(solution)/shard_map/ppermute | solution.py:400
  537.2 20.3 %collective-permute-start.45 = (bf16[256,1536]{1,0:T(8,128)(2,1)S(1)}, bf16[256,1536]{1,0:T(8,128)(2,1)S(1)}, u32[]{:S(2)}, u32[]{:S(2)}) collective-permute-start(bf16[256,1536]{1,0:T(8,128)(2,1)S(1)} %get-tuple-element.78), channel_id=1, source_target_pairs={{0,16},{1,17},{2,18},{3,19},{4,20},{5,21},{6,22},{7,23},{8,24},{9,... | collective-permute-start | bytes 2359304 | tf_op jit(solution)/shard_map/ppermute | solution.py:400
  538.1 20.5 %collective-permute-start.46 = (bf16[256,1536]{1,0:T(8,128)(2,1)S(1)}, bf16[256,1536]{1,0:T(8,128)(2,1)S(1)}, u32[]{:S(2)}, u32[]{:S(2)}) collective-permute-start(bf16[256,1536]{1,0:T(8,128)(2,1)S(1)} %get-tuple-element.77), channel_id=1, source_target_pairs={{0,2},{1,3},{2,0},{3,1},{4,6},{5,7},{6,4},{7,5},{8,10},{9,11},{10,... | collective-permute-start | bytes 2359304 | tf_op jit(solution)/shard_map/ppermute | solution.py:400
  538.4 68.6 %collective-permute-start.47 = (bf16[256,1536]{1,0:T(8,128)(2,1)S(1)}, bf16[256,1536]{1,0:T(8,128)(2,1)S(1)}, u32[]{:S(2)}, u32[]{:S(2)}) collective-permute-start(bf16[256,1536]{1,0:T(8,128)(2,1)S(1)} %get-tuple-element.76), channel_id=1, source_target_pairs={{0,18},{1,19},{2,16},{3,17},{4,22},{5,23},{6,20},{7,21},{8,26},{9,... | collective-permute-start | bytes 2359304 | tf_op jit(solution)/shard_map/ppermute | solution.py:400
  554.0 167.4 %collective-permute-start.52 = (bf16[128,2816]{1,0:T(8,128)(2,1)}, bf16[128,2816]{1,0:T(8,128)(2,1)}, u32[]{:S(2)}, u32[]{:S(2)}) collective-permute-start(bf16[128,2816]{1,0:T(8,128)(2,1)} %get-tuple-element.85), channel_id=1, source_target_pairs={{0,6},{1,7},{2,4},{3,5},{4,2},{5,3},{6,0},{7,1},{8,14},{9,15},{10,... | collective-permute-start | bytes 2162696 | tf_op jit(solution)/shard_map/ppermute | solution.py:385
  557.5 163.9 %collective-permute-start.51 = (bf16[128,2816]{1,0:T(8,128)(2,1)}, bf16[128,2816]{1,0:T(8,128)(2,1)}, u32[]{:S(2)}, u32[]{:S(2)}) collective-permute-start(bf16[128,2816]{1,0:T(8,128)(2,1)} %get-tuple-element.86), channel_id=1, source_target_pairs={{0,2},{1,3},{2,0},{3,1},{4,6},{5,7},{6,4},{7,5},{8,10},{9,11},{10,... | collective-permute-start | bytes 2162696 | tf_op jit(solution)/shard_map/ppermute | solution.py:385
  557.5 163.9 %collective-permute-start.50 = (bf16[128,2816]{1,0:T(8,128)(2,1)}, bf16[128,2816]{1,0:T(8,128)(2,1)}, u32[]{:S(2)}, u32[]{:S(2)}) collective-permute-start(bf16[128,2816]{1,0:T(8,128)(2,1)} %get-tuple-element.84), channel_id=1, source_target_pairs={{0,4},{1,5},{2,6},{3,7},{4,0},{5,1},{6,2},{7,3},{8,12},{9,13},{10,... | collective-permute-start | bytes 2162696 | tf_op jit(solution)/shard_map/ppermute | solution.py:385
  620.3 92.0 %copy-start.57 = (f32[512]{0:T(512)S(1)}, f32[512]{0:T(512)}, u32[]{:S(2)}) copy-start(f32[512]{0:T(512)} %copy-done.56) | copy-start | bytes 6148
  (58 other events, 537.9 us)

commit v3 on v2

--- a/solution.py
+++ b/solution.py
@@ -79,6 +79,10 @@
         copy.start()
         self.started.append(copy)
         return copy
+
+    def sent(self, copy):
+        self.started = [c for c in self.started if c is not copy]
+        copy.wait_send()
 
     def finish(self):
         for copy in self.started:
@@ -446,14 +450,13 @@
     )
 
 
-def attention_forward_body(qkv_ref, fold_ref, spread_ref, probs_ref, out_ref):
+def attention_forward_rows(at, qkv_ref, fold, spread, probs_ref, out_ref):
     width = out_ref.shape[2]
-    fold, spread = fold_ref[...], spread_ref[...]
     for q in range(4):
-        query = qkv_ref[q, :, :width].astype(f32)
+        query = qkv_ref[q, at, :width].astype(f32)
         scores = []
         for k in range(q + 1):
-            key = qkv_ref[k, :, width : 2 * width].astype(f32)
+            key = qkv_ref[k, at, width : 2 * width].astype(f32)
             scores.append(heads_sum(query * key, fold) * HD ** (-0.5))
         top = functools.reduce(jnp.maximum, scores)
         expo = [jnp.exp(s - top) for s in scores]
@@ -461,11 +464,11 @@
         mixed = None
         for k in range(q + 1):
             prob = expo[k] / total
-            probs_ref[PAIRS.index((q, k))] = prob
+            probs_ref[PAIRS.index((q, k)), at, :] = prob
             wide = jnp.dot(prob.astype(bf16), spread, preferred_element_type=f32)
-            term = wide * qkv_ref[k, :, 2 * width :].astype(f32)
+            term = wide * qkv_ref[k, at, 2 * width :].astype(f32)
             mixed = term if mixed is None else mixed + term
-        out_ref[q] = mixed.astype(bf16)
+        out_ref[q, at, :] = mixed.astype(bf16)
 
 
 def attention_backward_body(qkv_ref, probs_ref, grad_ref, fold_ref, spread_ref, out_ref):
@@ -504,30 +507,6 @@
     return fold, fold.T
 
 
-def attention_forward(qkv, step=64):
-    _, rows, triple = qkv.shape
-    width = triple // 3
-    fold, spread = fold_matrices(width)
-    return pl.pallas_call(
-        attention_forward_body,
-        grid=(rows // step,),
-        in_specs=[
-            pl.BlockSpec((4, step, triple), lambda r: (0, r, 0)),
-            pl.BlockSpec((width, LANES), lambda r: (0, 0)),
-            pl.BlockSpec((LANES, width), lambda r: (0, 0)),
-        ],
-        out_specs=[
-            pl.BlockSpec((len(PAIRS), step, LANES), lambda r: (0, r, 0)),
-            pl.BlockSpec((4, step, width), lambda r: (0, r, 0)),
-        ],
-        out_shape=[
-            jax.ShapeDtypeStruct((len(PAIRS), rows, LANES), f32),
-            jax.ShapeDtypeStruct((4, rows, width), bf16),
-        ],
-        name="attention_forward",
-    )(qkv, fold, spread)
-
-
 def attention_backward(qkv, probs, grad, step=64):
     _, rows, triple = qkv.shape
     width = triple // 3
@@ -604,6 +583,404 @@
     first = jnp.where(place == 0, own, other)
     second = jnp.where(place == 0, other, own)
     return jnp.stack([first, second], axis=0)
+
+
+class Spread:
+    def __init__(self, w, wire, weight, full):
+        self.w, self.wire, self.weight, self.full = w, wire, weight, full
+        self.block = full.shape[0] // w.n
+        self.far, self.near = {}, {}
+
+    def rows(self, frame):
+        return self.full.at[pl.ds(pl.multiple_of(frame * self.block, self.block), self.block), :]
+
+    def own(self, local):
+        return local.start(self.weight.at[self.w.place], self.rows(self.w.frame))
+
+    def own_near(self):
+        w = self.w
+        self.near[0] = self.wire.start(
+            self.weight.at[w.place], self.rows(w.frame), w.along_frames(1)
+        )
+
+    def send(self, mask):
+        w = self.w
+        which = 1 - w.place if mask & 2 else w.place
+        self.far[mask] = self.wire.start(
+            self.weight.at[which], self.rows(w.frame), w.along_frames(mask)
+        )
+
+    def relay(self, mask):
+        self.far[mask].wait_recv()
+        rows = self.rows(flip(self.w.frame, mask))
+        self.near[mask] = self.wire.start(rows, rows, self.w.along_frames(1))
+
+    def close(self):
+        for copy in self.near.values():
+            copy.wait_recv()
+
+
+def front_body(
+    n, context, ctx_weight, inputs, grad_rows, gains, fold, spread,
+    qkv_weight, out_weight, gu_weight, down_weight,
+    out_qkv, out_out, out_gu, out_down, out_ctx, out_resid, out_mid, out_one, out_two, out_grad,
+    out_qkv_mixed, out_probs, out_mixed,
+    ctx_held, context_held, total, partner_half, half_sum, far_half, whole, home, resid, pair,
+    qkv_full, out_full, qkv_rows, qkv_mixed, probs, mixed_quarter, mixed, away, got, grad_pair,
+    send_sem, recv_sem, local_sem,
+):
+    w = Where(n)
+    wire, local = Wire(send_sem, recv_sem), Local(local_sem)
+    rows, depth = inputs.shape
+    count = ctx_weight.shape[0] // 4
+    piece = depth // n
+    crossing = w.core != w.place
+    half = rows // 2
+    step = 64
+    quarter_of_context = pl.ds(pl.multiple_of(w.stream * count, LANES), count)
+    load_context = local.start(context.at[:, quarter_of_context], context_held)
+    load_ctx = local.start(ctx_weight.at[quarter_of_context, :], ctx_held.at[w.frame])
+    qkv = Spread(w, wire, qkv_weight, qkv_full)
+    out = Spread(w, wire, out_weight, out_full)
+    gu = Spread(w, wire, gu_weight, out_gu)
+    down = Spread(w, wire, down_weight, out_down)
+    owns = [qkv.own(local), out.own(local)]
+    greet(
+        [w.along_stream(1), w.along_stream(2), w.along_frames(1)]
+        + [w.along_frames(m) for m in w.masks]
+        + [w.across(), w.with_position(3)]
+    )
+
+    load_ctx.wait()
+    held, near = [0], {}
+
+    def ctx_near(o):
+        at = flip(w.frame, o)
+        near[o] = wire.start(ctx_held.at[at], ctx_held.at[at], w.along_frames(1))
+
+    ready = []
+    for bit in reversed(range(1, n.bit_length() - 1)):
+        copies = []
+        for o in held:
+            at = flip(w.frame, o)
+            copies.append(
+                (o, wire.start(ctx_held.at[at], ctx_held.at[at], w.along_frames(1 << bit)))
+            )
+        if bit == n.bit_length() - 2:
+            ctx_near(0)
+            qkv.own_near()
+            out.own_near()
+        if bit == 1:
+            for mask in w.masks:
+                qkv.send(mask)
+                out.send(mask)
+        for o, copy in copies:
+            copy.wait_recv()
+            ctx_near(o ^ (1 << bit))
+            held.append(o ^ (1 << bit))
+
+    load_context.wait()
+
+    def project(o):
+        at = flip(w.frame, o)
+        columns = pl.ds(pl.multiple_of(at * piece, piece), piece)
+        value = jnp.dot(context_held[...], ctx_held[at], preferred_element_type=f32)
+        total[:, columns] = value
+
+    if piece % LANES == 0:
+        for o in held:
+            project(o)
+        for o in held:
+            near[o].wait_recv()
+            project(o ^ 1)
+    else:
+        for o in held:
+            near[o].wait_recv()
+        total[...] = jnp.zeros_like(total)
+
+        @pl.loop(0, n)
+        def _(at):
+            line = lax.broadcasted_iota(jnp.int32, (piece, depth), 0)
+            column = lax.broadcasted_iota(jnp.int32, (piece, depth), 1)
+            select = (column == line + at * piece).astype(bf16)
+            laid = jnp.dot(ctx_held[at], select, preferred_element_type=f32).astype(bf16)
+
+            @pl.loop(0, rows // LANES)
+            def _(t):
+                here = pl.ds(pl.multiple_of(t * LANES, LANES), LANES)
+                total[here, :] += jnp.dot(
+                    context_held[here, :], laid, preferred_element_type=f32
+                )
+
+    store_ctx = local.start(ctx_held, out_ctx)
+
+    mine = pl.ds(pl.multiple_of(w.core * half, 16), half)
+    theirs = pl.ds(pl.multiple_of((1 - w.core) * half, 16), half)
+    whole[theirs, :] = total[theirs, :].astype(bf16)
+    first = wire.start(whole.at[theirs, :], partner_half, w.along_stream(1))
+    first.wait_recv()
+    half_sum[...] = (total[mine, :] + partner_half[...].astype(f32)).astype(bf16)
+    second = wire.start(half_sum, far_half, w.along_stream(2))
+    for mask in w.masks[:1]:
+        qkv.relay(mask)
+        out.relay(mask)
+    second.wait_recv()
+    home[mine, :] = (half_sum[...].astype(f32) + far_half[...].astype(f32)).astype(bf16)
+    third = wire.start(home.at[mine, :], home.at[mine, :], w.along_stream(1))
+    third.wait_recv()
+    wire.sent(third)
+
+    @pl.loop(0, rows // step)
+    def _(t):
+        at = pl.ds(pl.multiple_of(t * step, step), step)
+        home[at, :] = (home[at, :].astype(f32) + inputs[at, :].astype(f32)).astype(bf16)
+
+    cross = wire.make(home, resid, w.across())
+    cross_grad = wire.make(grad_rows, grad_pair.at[:rows, :], w.across())
+    stay = pltpu.make_async_copy(home, resid, local_sem.at[22])
+    stay_grad = pltpu.make_async_copy(grad_rows, grad_pair.at[:rows, :], local_sem.at[23])
+
+    @pl.when(crossing)
+    def _():
+        cross.start()
+
+    @pl.when(jnp.logical_not(crossing))
+    def _():
+        stay.start()
+        stay_grad.start()
+
+    gu.own_near()
+    for mask in w.far_masks:
+        gu.send(mask)
+    for mask in w.masks[1:]:
+        qkv.relay(mask)
+        out.relay(mask)
+    down.own_near()
+
+    @pl.when(crossing)
+    def _():
+        cross.wait_recv()
+
+    @pl.when(jnp.logical_not(crossing))
+    def _():
+        stay.wait()
+
+    def normed(source, gain):
+        @pl.loop(0, rows // step)
+        def _(t):
+            at = pl.ds(pl.multiple_of(t * step, step), step)
+            values = source[at, :].astype(f32)
+            scale = lax.rsqrt(jnp.mean(values * values, axis=-1, keepdims=True) + norm_eps)
+            pair[at, :] = (values * scale * gain).astype(bf16)
+
+    normed(resid, gains[0:1, :])
+    upper = pair.at[rows:, :]
+    first_pair = wire.start(pair.at[:rows, :], upper, w.along_stream(1))
+    for copy in owns:
+        copy.wait()
+    qkv.close()
+    out.close()
+    quarter = 2 * rows // 4
+    width = out_full.shape[1]
+
+    def qkv_of(lo, hi):
+        @pl.loop(lo, hi)
+        def _(t):
+            at = pl.ds(pl.multiple_of(t * quarter, quarter), quarter)
+            left = pair[at, :]
+            for p in range(3):
+                columns = slice(p * width, (p + 1) * width)
+                value = jnp.dot(left, qkv_full[:, columns], preferred_element_type=f32)
+                qkv_rows[at, columns] = value.astype(bf16)
+
+    qkv_of(0, 2)
+    first_pair.wait_recv()
+    qkv_of(2, 4)
+    mixing = {}
+
+    def rows_of(position):
+        return pl.ds(pl.multiple_of(position * quarter, quarter), quarter)
+
+    for mask in (3, 1, 2):
+        mixing[mask] = wire.start(
+            qkv_rows.at[rows_of(flip(w.position, mask)), :],
+            qkv_mixed.at[w.position],
+            w.with_position(mask),
+        )
+    own_quarter = local.start(qkv_rows.at[rows_of(w.position), :], qkv_mixed.at[w.position])
+    for mask in w.both_masks:
+        gu.send(mask)
+    stores = [
+        local.start(pair, out_one),
+        local.start(qkv_full, out_qkv),
+        local.start(out_full, out_out),
+        local.start(resid, out_resid),
+    ]
+    gu_own, down_own = gu.own(local), down.own(local)
+    for mask in w.far_masks:
+        gu.relay(mask)
+    own_quarter.wait()
+    for mask in (2, 1, 3):
+        mixing[mask].wait_recv()
+
+    fold_held, spread_held = fold[...], spread[...]
+
+    @pl.loop(0, quarter // step)
+    def _(t):
+        at = pl.ds(pl.multiple_of(t * step, step), step)
+        attention_forward_rows(at, qkv_mixed, fold_held, spread_held, probs, mixed_quarter)
+
+    returning = {}
+    for mask in (3, 1, 2):
+        returning[mask] = wire.start(
+            mixed_quarter.at[flip(w.position, mask)],
+            mixed.at[rows_of(w.position), :],
+            w.with_position(mask),
+        )
+    own_back = local.start(mixed_quarter.at[w.position], mixed.at[rows_of(w.position), :])
+    gu.send(2)
+    for mask in w.masks:
+        down.send(mask)
+
+    @pl.when(crossing)
+    def _():
+        cross_grad.start()
+
+    stores += [local.start(qkv_mixed, out_qkv_mixed), local.start(probs, out_probs)]
+    for mask in w.both_masks:
+        gu.relay(mask)
+    own_back.wait()
+    for mask in (2, 1, 3):
+        returning[mask].wait_recv()
+    stores.append(local.start(mixed, out_mixed))
+    stores[0].wait()
+
+    @pl.loop(2, 4)
+    def _(t):
+        at = pl.ds(pl.multiple_of(t * quarter, quarter), quarter)
+        to = pl.ds(pl.multiple_of(t * quarter - rows, quarter), quarter)
+        away[to, :] = dot_columns(mixed[at, :], out_full[...]).astype(bf16)
+
+    part = wire.start(away, got, w.along_stream(1))
+
+    @pl.loop(0, 2)
+    def _(t):
+        at = pl.ds(pl.multiple_of(t * quarter, quarter), quarter)
+        total[at, :] = dot_columns(mixed[at, :], out_full[...])
+
+    part.wait_recv()
+    wire.sent(first_pair)
+    gain = gains[1:2, :]
+
+    @pl.loop(0, rows // step)
+    def _(t):
+        at = pl.ds(pl.multiple_of(t * step, step), step)
+        values = resid[at, :].astype(f32) + total[at, :] + got[at, :].astype(f32)
+        total[at, :] = values
+        scale = lax.rsqrt(jnp.mean(values * values, axis=-1, keepdims=True) + norm_eps)
+        pair[at, :] = (values * scale * gain).astype(bf16)
+
+    second_pair = wire.start(pair.at[:rows, :], upper, w.along_stream(1))
+    stores.append(local.start(total, out_mid))
+    gu.relay(2)
+    for mask in w.masks[:-1]:
+        down.relay(mask)
+
+    @pl.when(crossing)
+    def _():
+        cross_grad.wait_recv()
+
+    @pl.when(jnp.logical_not(crossing))
+    def _():
+        stay_grad.wait()
+
+    grad_copy = wire.start(grad_pair.at[:rows, :], grad_pair.at[rows:, :], w.along_stream(1))
+    for mask in w.masks[-1:]:
+        down.relay(mask)
+    second_pair.wait_recv()
+    stores.append(local.start(pair, out_two))
+    grad_copy.wait_recv()
+    stores.append(local.start(grad_pair, out_grad))
+    gu.close()
+    down.close()
+    for copy in stores[1:]:
+        copy.wait()
+    for copy in (store_ctx, gu_own, down_own):
+        copy.wait()
+
+    @pl.when(crossing)
+    def _():
+        cross.wait_send()
+        cross_grad.wait_send()
+
+    wire.finish()
+
+
+def front(
+    n, context, ctx_weight, inputs, grad_rows, gains,
+    qkv_weight, out_weight, gu_weight, down_weight,
+):
+    rows, depth = inputs.shape
+    count = ctx_weight.shape[0] // 4
+    wide_q, wide_o = qkv_weight.shape[2], out_weight.shape[2]
+    fold, spread = fold_matrices(wide_o)
+    quarter = rows // 2
+    half = rows // 2
+    pairs = len(PAIRS)
+    scratch = [
+        pltpu.VMEM((n, count, depth // n), bf16),
+        pltpu.VMEM((rows, count), bf16),
+        pltpu.VMEM((rows, depth), f32),
+        pltpu.VMEM((half, depth), bf16),
+        pltpu.VMEM((half, depth), bf16),
+        pltpu.VMEM((half, depth), bf16),
+        pltpu.VMEM((rows, depth), bf16),
+        pltpu.VMEM((rows, depth), bf16),
+        pltpu.VMEM((rows, depth), bf16),
+        pltpu.VMEM((2 * rows, depth), bf16),
+        pltpu.VMEM((depth, wide_q), bf16),
+        pltpu.VMEM((depth, wide_o), bf16),
+        pltpu.VMEM((2 * rows, wide_q), bf16),
+        pltpu.VMEM((4, quarter, wide_q), bf16),
+        pltpu.VMEM((pairs, quarter, LANES), f32),
+        pltpu.VMEM((4, quarter, wide_o), bf16),
+        pltpu.VMEM((2 * rows, wide_o), bf16),
+        pltpu.VMEM((rows, depth), bf16),
+        pltpu.VMEM((rows, depth), bf16),
+        pltpu.VMEM((2 * rows, depth), bf16),
+        pltpu.SemaphoreType.DMA((24 + 10 * n,)),
+        pltpu.SemaphoreType.DMA((24 + 10 * n,)),
+        pltpu.SemaphoreType.DMA((24,)),
+    ]
+    shape = jax.ShapeDtypeStruct
+    return pl.pallas_call(
+        functools.partial(front_body, n),
+        in_specs=[ANY, ANY, VMEM, ANY, VMEM, VMEM, VMEM, ANY, ANY, ANY, ANY],
+        out_specs=[ANY] * 13,
+        out_shape=[
+            shape((depth, wide_q), bf16),
+            shape((depth, wide_o), bf16),
+            shape((depth, gu_weight.shape[2]), bf16),
+            shape((depth, down_weight.shape[2]), bf16),
+            shape((n, count, depth // n), bf16),
+            shape((rows, depth), bf16),
+            shape((rows, depth), f32),
+            shape((2 * rows, depth), bf16),
+            shape((2 * rows, depth), bf16),
+            shape((2 * rows, depth), bf16),
+            shape((4, quarter, wide_q), bf16),
+            shape((pairs, quarter, LANES), f32),
+            shape((2 * rows, wide_o), bf16),
+        ],
+        scratch_shapes=scratch,
+        compiler_params=pltpu.CompilerParams(
+            collective_id=3, has_side_effects=True, vmem_limit_bytes=62 << 20
+        ),
+        name="front",
+    )(
+        context, ctx_weight, inputs, grad_rows, gains, fold, spread,
+        qkv_weight, out_weight, gu_weight, down_weight,
+    )
 
 
 def shards(
@@ -631,68 +1008,35 @@
     gain_one = norm_gains[0]
     gain_two = norm_gains[1]
 
-    ctx_rows = ctx_weight.shape[0] // 4
-    piece = lax.dynamic_slice_in_dim(ctx_weight, stream_index * ctx_rows, ctx_rows, 0)
-    block = piece.shape[1]
-    held = piece[None]
-    order = [0]
-    near_pieces = []
-    attn_own, attn_other = taken((qkv_weight[0], out_weight[0]), place)
-    near_first = {}
-    near_first["attn"] = swap_frames(attn_own, 1)
-    far_context = None
-    for bit in reversed(range(1, n.bit_length() - 1)):
-        got = swap_frames(held, 1 << bit)
-        if far_context is None:
-            far_context = got
-            near_pieces.append(swap_frames(jnp.concatenate([held, got], axis=0), 1))
-        else:
-            near_pieces.append(swap_frames(got, 1))
-        held = jnp.concatenate([held, got], axis=0)
-        order = order + [o ^ (1 << bit) for o in order]
-    held = jnp.concatenate([held] + near_pieces, axis=0)
-    order = order + [o ^ 1 for o in order]
-    ctx_full = jnp.zeros((ctx_rows, n, block), bf16)
-    for at, o in enumerate(order):
-        ctx_full = lax.dynamic_update_index_in_dim(ctx_full, held[at], frame_index ^ o, 1)
-    ctx_full = ctx_full.reshape(ctx_rows, width_model)
-    context_part = lax.dynamic_slice_in_dim(context, stream_index * ctx_rows, ctx_rows, 1)
-    projected = jnp.dot(context_part, ctx_full, preferred_element_type=f32)
-
-    def summed(value):
-        value = value.astype(f32) + swap_stream(value.astype(bf16), 1).astype(f32)
-        half = value.shape[0] // 2
-        mine = lax.dynamic_slice_in_dim(value, half_index * half, half, 0)
-        mine = (mine + swap_stream(mine.astype(bf16), 2).astype(f32)).astype(bf16)
-        far = swap_stream(mine, 1)
-        first = jnp.where(half_index == 0, mine, far)
-        second = jnp.where(half_index == 0, far, mine)
-        return jnp.concatenate([first, second], axis=0)
-
-    def sent(own, other, masks, *others):
-        pieces = {}
-        for mask in masks:
-            got = swap_frames(after(other if mask & 2 else own, *others), mask)
-            pieces[mask] = got
-            pieces[mask + 1] = swap_frames(got, 1)
-        return pieces
-
-    far_masks = [m for m in range(2, n, 2) if not m & 2]
-    both_masks = [m for m in range(2, n, 2) if m & 2 and m > 2]
-    near_masks = [2]
-    attn_pieces = {0: attn_own, 1: near_first["attn"]}
-    attn_pieces.update(sent(attn_own, attn_other, far_masks + both_masks + near_masks, far_context))
-    head_width = out_weight.shape[3]
-    qkv_full = placed_rows(attn_pieces, frame_index, 0, 3 * head_width)
-    out_full = placed_rows(attn_pieces, frame_index, 3 * head_width, head_width)
-
-    home_sum = summed(projected).astype(f32)
-    resid_home = (inputs[:, 0].astype(f32) + home_sum).astype(bf16)
-    resid_in = transposed(resid_home).astype(f32)
-    gu_own, gu_other = taken((gate_up_weight[0],), place)
-    down_own, down_other = taken((down_weight[0],), place)
-    gu_pieces = {0: gu_own, 1: swap_frames(after(gu_own, near_pieces[-1]), 1)}
-    gu_pieces.update(sent(gu_own, gu_other, far_masks, resid_home))
+    grad_rows = (cotangent[:, 0] * valid_mask).astype(bf16)
+    (
+        qkv_full,
+        out_full,
+        gate_up_full,
+        down_full,
+        ctx_pieces,
+        resid_in,
+        resid_mid,
+        paired_one,
+        paired_two,
+        paired_grad_ffn,
+        qkv_mixed,
+        probs,
+        mixed,
+    ) = front(
+        n,
+        context,
+        ctx_weight,
+        inputs[:, 0],
+        grad_rows,
+        norm_gains,
+        qkv_weight[0],
+        out_weight[0],
+        gate_up_weight[0],
+        down_weight[0],
+    )
+    ctx_full = ctx_pieces.transpose(1, 0, 2).reshape(-1, width_model)
+    near = frame_index % 2
 
     def paired(mine):
         return jnp.concatenate([mine, swap_stream(mine, 1)], axis=0)
@@ -707,14 +1051,6 @@
 
     def rows_back(left, right):
         return lax.dot_general(left, right, (((1,), (1,)), ((), ())), preferred_element_type=f32)
-
-    scale_one = norm_scale(resid_in)
-    paired_one = paired((resid_in * scale_one * gain_one).astype(bf16))
-    qkv_rows = rows_times(paired_one, qkv_full).astype(bf16)
-    qkv_mixed = exchange_rows(qkv_rows, position)
-    gu_pieces.update(sent(gu_own, gu_other, both_masks, qkv_rows))
-    down_pieces = {0: down_own, 1: swap_frames(after(down_own, qkv_rows), 1)}
-    probs, mixed_quarter = attention_forward(qkv_mixed)
 
     def returned(value):
         _, quarter, width = value.shape
@@ -727,19 +1063,7 @@
             out = lax.dynamic_update_index_in_dim(out, got, there, 0)
         return out.reshape(4 * quarter, width)
 
-    mixed = returned(mixed_quarter)
-    gu_pieces.update(sent(gu_own, gu_other, near_masks, mixed_quarter))
-    gate_up_full = placed_rows(gu_pieces, frame_index, 0, gate_up_weight.shape[3])
-    down_pieces.update(
-        sent(down_own, down_other, far_masks + both_masks + near_masks, mixed_quarter)
-    )
-    down_full = placed_rows(down_pieces, frame_index, 0, down_weight.shape[3])
-    grad_home_rows = (cotangent[:, 0] * valid_mask).astype(bf16)
-    grad_res = transposed(after(grad_home_rows, mixed_quarter))
-    near = frame_index % 2
-    resid_mid = resid_in + own_sum(rows_back(mixed, out_full))
     scale_two = norm_scale(resid_mid)
-    paired_two = paired((resid_mid * scale_two * gain_two).astype(bf16))
     gate_up = rows_times(paired_two, gate_up_full)
     ffn_half = down_full.shape[1]
     gate_part = gate_up[:, :ffn_half]
@@ -748,7 +1072,7 @@
     activated = gate_part * sigmoid_gate
     hidden = (activated * up_part).astype(bf16)
 
-    paired_grad_ffn = paired(grad_res)
+    grad_res = paired_grad_ffn[:frame_count]
     sum_down = scattered(halves(paired_grad_ffn, near), hidden, frame_index, place)
     grad_hidden = rows_times(paired_grad_ffn, down_full)
     grad_gate = grad_hidden * up_part * (sigmoid_gate * (1.0 + gate_part * (1.0 - sigmoid_gate)))
@@ -777,7 +1101,7 @@
         n,
         part_away,
         part_stay,
-        resid_in.astype(bf16),
+        resid_in,
         grad_mid,
         norm_gains,
         grad_gain_two[None],

time: 743 us -> 561 us (0.76); the launches traced: 731 us -> 557 us
  Pallas kernels: 105 us -> 344 us
  waiting for transfers between devices: 290 us -> 66.7 us
  local copies, waits for them, and re-layouts: 161 us -> 36.9 us
  starting transfers between devices: 74.1 us -> 24.1 us
  matrix products: 76.9 us -> 64 us
    pallas_call x1, Pallas kernels: 7.45 us -> 242 us  [front(): pl.pallas_call(functools.partial(front_body, n), in_specs=[ANY, ANY, VMEM...]
    ppermute x33 -> x8, waiting for transfers between devices: 185 us -> 19.2 us  [swap_frames(): return lax.ppermute(value, 'frames', [(d, d ^ mask) for d in range(n)])]
    dynamic_update_slice x40 -> x0, local copies, waits for them, and re-layouts: 109 us -> none  [the longest x8 97.3 us: shards(): lax.dynamic_update_index_in_dim(ctx_full, held[at], frame_index ^ o, 1)]
    ppermute x14 -> x6, waiting for transfers between devices: 105 us -> 47.5 us  [joint(): return lax.ppermute(value, ('stream', 'frames'), pairs)]
    ppermute x33 -> x8, starting transfers between devices: 37.2 us -> 9.58 us  [swap_frames(): return lax.ppermute(value, 'frames', [(d, d ^ mask) for d in range(n)])]
    ppermute x10 -> x3, starting transfers between devices: 20.7 us -> 0.51 us  [swap_stream(): return lax.ppermute(value, 'stream', [(d, d ^ mask) for d in range(n)])]
    broadcast_in_dim x17 -> x2, local copies, waits for them, and re-layouts: 16.9 us -> 0.32 us  [the longest x1 0.24 us: returned(): out = jnp.zeros((4, quarter, width), value.dtype)]
    dot_general x5 -> x4, matrix products: 22.3 us -> 15.6 us  [rows_back(): lax.dot_general(left, right, (((1,), (1,)), ((), ())), preferred_element_...]
  transfers between devices with their start and end apart: 57 -> 17, of which waited for: 29 -> 8; matrix products, arithmetic and copies ran while one was open for 29% -> 12% of each run, Pallas kernels for 14% -> 18%
where the time goes in v3:
time: 561 us; the launch traced here: 557 us
  Pallas kernels  344 us (61%)
  waiting for transfers between devices  66.7 us (12%)
  matrix products  64 us (11%)
  local copies, waits for them, and re-layouts  36.9 us (7%)
  starting transfers between devices  24.1 us (4%)
  other arithmetic  19.3 us (3%)
    pallas_call x1, Pallas kernels, front(): pl.pallas_call(functools.partial(front_body, n), in_specs=[ANY, ANY, VMEM...  242 us
    pallas_call x1, Pallas kernels, tail(): pl.pallas_call(functools.partial(tail_body, n), in_specs=[ANY, VMEM, VMEM...  93.7 us
    ppermute x6, waiting for transfers between devices, joint(): return lax.ppermute(value, ('stream', 'frames'), pairs)  47.5 us
    unnamed x140, local copies, waits for them, and re-layouts  24 us
    dot_general x3, matrix products, rows_times(): return jnp.dot(left, right, preferred_element_type=f32)  21.6 us
    ppermute x8, waiting for transfers between devices, swap_frames(): return lax.ppermute(value, 'frames', [(d, d ^ mask) for d in range(n)])  19.2 us
    dot_general x4, matrix products, product(): lax.dot_general(part, right, (((0,), (0,)), ((), ())), preferred_element_...  17.7 us
    dot_general x4, matrix products, rows_back(): lax.dot_general(left, right, (((1,), (1,)), ((), ())), preferred_element_...  15.6 us
  transfers between devices with their start and end apart: 17, of which 8 were waited for; matrix products, arithmetic and copies ran while one was open for 12% of the time, Pallas kernels for 18%

profile of v3, /device:TPU:0, one launch (start us, length us, event | category | flops | bytes accessed | tf_op | source)
XLA Modules:
  0.0 557.3 jit_solution(11024314118590815509)
XLA Ops:
  1.4 0.9 fusion.34.fold.fold_ref
  3.0 3.0 fusion.5.grad_rows
  5.9 242.2 %front.1 = (bf16[1024,1536]{1,0:T(8,128)(2,1)}, bf16[1024,512]{1,0:T(8,128)(2,1)}, bf16[1024,2816]{1,0:T(8,128)(2,1)}, bf16[1024,1408]{1,0:T(8,128)(2,1)}, bf16[...) custom-call(bf16[512,4096]{1,0:T(8,128)(2,1)} %context.3, ...), custom_call_target="tpu_custom_call" | custom-call | tf_op jit(solution)/shard_map/front/pallas_call | solution.py:956
  248.2 1.9 fusion.56
  250.5 11.8 %fusion.59 = f32[1024,2816]{1,0:T(8,128)} fusion(bf16[1024,1024]{1,0:T(8,128)(2,1)S(1)} %copy-done.10, bf16[1024,2816]{1,0:T(8,128)(2,1)} %get-tuple-element.34), kind=kOutput, calls=%fused_computation.150 | convolution fusion | flops 5905580032 | bytes 19398656 | tf_op jit(solution)/shard_map/dot_general | solution.py:1050
  262.3 8.6 %multiply_convert_fusion.2 = (bf16[1024,1408]{1,0:T(8,128)(2,1)S(1)}, bf16[1024,1408]{1,0:T(8,128)(2,1)S(1)}, bf16[1024,1408]{1,0:T(8,128)(2,1)S(1)}) fusion(f32[1024,2816]{1,0:T(8,128)} %fusion.59, bf16[1024,1024]{1,0:T(8,128)(2,1)S(1)} %copy-done.4, bf16[1024,1408]{1,0:T(8,128)(2,1)S(1)} %copy-done.55), kind=kOutput, calls=%fused_computation.4 | convolution fusion | flops 2974416896 | bytes 25165824 | tf_op jit(solution)/shard_map/dot_general | solution.py:1050
  271.0 3.6 convolution_convert_fusion.2
  275.1 6.1 %fusion.6 = f32[1024,1024]{1,0:T(8,128)S(1)} fusion(bf16[1024,2816]{1,0:T(8,128)(2,1)S(1)} %bitcast.138, bf16[1024,1408]{1,0:T(8,128)(2,1)S(1)} %get-tuple-element.61, bf16[1024,1408]{1,0:T(8,128)(2,1)S(1)} %get-tuple-element.60), kind=kOutput, calls=%fused_computation.48 | convolution fusion | flops 5917114368 | bytes 15728640 | tf_op jit(solution)/shard_map/dot_general | solution.py:1053
  281.2 1.3 slice.284
  282.5 3.4 fusion.61
  285.9 1.1 slice.283
  288.6 1.2 copy-done.64
  289.8 1.3 copy-done.61
  291.1 4.8 convolution_convert_fusion
  296.0 1.7 collective-permute-start.9
  298.0 1.3 copy-done.9
  299.4 1.6 copy_bitcast_fusion.ctx_full
  301.0 1.3 copy-done.3
  302.4 4.8 multiply_reduce_fusion
  307.2 2.3 collective-permute-done.13
  309.5 3.2 add_convert_fusion.1
  313.0 3.3 collective-permute-start.15
  316.2 1.1 collective-permute-start.16
  317.3 2.1 fusion.54
  319.4 1.5 fusion.58
  320.9 11.9 %collective-permute-done.14 = bf16[128,1408]{1,0:T(8,128)(2,1)S(1)} collective-permute-done((bf16[128,1408]{1,0:T(8,128)(2,1)S(1)}, bf16[128,1408]{1,0:T(8,128)(2,1)S(1)}, u32[]{:S(2)}, u32[]{:S(2)}) %collective-permute-start.14) | collective-permute-done | bytes 360480 | tf_op jit(solution)/shard_map/ppermute | solution.py:389
  332.8 5.0 collective-permute-done.16
  338.0 1.2 maximum_bitcast_fusion.1
  339.7 1.2 fusion.7
  341.2 1.3 collective-permute-start.2
  342.5 7.3 %collective-permute-start.3 = (bf16[256,512]{1,0:T(8,128)(2,1)S(1)}, bf16[256,512]{1,0:T(8,128)(2,1)S(1)}, u32[]{:S(2)}, u32[]{:S(2)}) collective-permute-start(bf16[256,512]{1,0:T(8,128)(2,1)S(1)} %get-tuple-element.113), channel_id=1, source_target_pairs={{0,2},{1,3},{2,0},{3,1},{4,6},{5,7},{6,4},{7,5},{8,10},{9,11},{10,... | collective-permute-start | bytes 786440 | tf_op jit(solution)/shard_map/ppermute | solution.py:404
  350.2 1.5 convolution_convert_fusion.7
  351.7 1.5 convolution_convert_fusion.8
  353.3 1.8 collective-permute-start.4
  356.0 6.7 %collective-permute-done.4 = bf16[256,512]{1,0:T(8,128)(2,1)S(1)} collective-permute-done((bf16[256,512]{1,0:T(8,128)(2,1)S(1)}, bf16[256,512]{1,0:T(8,128)(2,1)S(1)}, u32[]{:S(2)}, u32[]{:S(2)}) %collective-permute-start.4) | collective-permute-done | bytes 262176 | tf_op jit(solution)/shard_map/ppermute | solution.py:404
  362.7 1.0 copy-done.6
  363.7 8.5 %attention_backward.1 = bf16[4,256,1536]{2,1,0:T(8,128)(2,1)} custom-call(bf16[4,256,1536]{2,1,0:T(8,128)(2,1)} %get-tuple-element.28.qkv_ref, f32[10,256,128]{2,1,0:T(8,128)} %get-tuple-element.29.probs_ref, bf16[4,256,512]{2,1,0:T(8,128)(2,1)} %copy-done.6, bf16[512,128]{1,0:T(8,128)(2,1)} %fusion.34.fold.fold_ref, bf16[128,512]{1,0:T(8,128)(2,1)} %fusion.35.spread.spread_ref), custom_call_target="tpu_custom_call" | custom-call | tf_op jit(solution)/shard_map/attention_backward/pallas_call | solution.py:514
  372.4 1.6 copy-done.1
  374.4 0.9 collective-permute-start.5
  375.3 1.3 collective-permute-start.6
  376.6 1.4 collective-permute-start.7
  378.0 6.0 %add_convert_fusion = bf16[512,2816]{1,0:T(8,128)(2,1)S(1)} fusion(bf16[512,2816]{1,0:T(8,128)(2,1)} %collective-permute-done.9, bf16[1024,1408]{1,0:T(8,128)(2,1)} %copy-done.63, bf16[1024,1408]{1,0:T(8,128)(2,1)S(1)} %copy-done.62, pred[]{:T(512)S(6)} %eq.34, bf16[1024,128]{1,0:T(8,128)(2,1)S(1)} %copy-done.16, bf16[1024,128]{1,0:T(8,128)(2,1)S(1)} %copy-done.18, ...), kind=kOutput, calls=%fused_computation.1 | convolution fusion | flops 2980446208 | bytes 13631489 | tf_op jit(solution)/shard_map/dot_general | solution.py:565
  384.0 1.4 dynamic-slice_bitcast_fusion.5
  385.4 1.5 collective-permute-start.10
  387.3 6.0 %collective-permute-done.5 = bf16[256,1536]{1,0:T(8,128)(2,1)S(1)} collective-permute-done((bf16[256,1536]{1,0:T(8,128)(2,1)S(1)}, bf16[256,1536]{1,0:T(8,128)(2,1)S(1)}, u32[]{:S(2)}, u32[]{:S(2)}) %collective-permute-start.5) | collective-permute-done | bytes 786464 | tf_op jit(solution)/shard_map/ppermute | solution.py:404
  393.2 1.2 collective-permute-start.12
  394.6 16.6 %collective-permute-done.6 = bf16[256,1536]{1,0:T(8,128)(2,1)S(1)} collective-permute-done((bf16[256,1536]{1,0:T(8,128)(2,1)S(1)}, bf16[256,1536]{1,0:T(8,128)(2,1)S(1)}, u32[]{:S(2)}, u32[]{:S(2)}) %collective-permute-start.6) | collective-permute-done | bytes 786464 | tf_op jit(solution)/shard_map/ppermute | solution.py:404
  411.3 17.4 %collective-permute-done.7 = bf16[256,1536]{1,0:T(8,128)(2,1)S(1)} collective-permute-done((bf16[256,1536]{1,0:T(8,128)(2,1)S(1)}, bf16[256,1536]{1,0:T(8,128)(2,1)S(1)}, u32[]{:S(2)}, u32[]{:S(2)}) %collective-permute-start.7) | collective-permute-done | bytes 786464 | tf_op jit(solution)/shard_map/ppermute | solution.py:404
  428.8 3.0 convolution_convert_fusion.4
  431.8 3.0 convolution_convert_fusion.5
  435.1 1.7 copy-done.54
  436.7 3.1 fusion.60.part_own
  439.9 2.9 convolution_convert_fusion.6.part_send
  442.8 93.7 %tail.1 = (f32[2,128,1536]{2,1,0:T(8,128)}, f32[2,128,512]{2,1,0:T(8,128)}, f32[512,1024]{1,0:T(8,128)}, bf16[512,1024]{1,0:T(8,128)(2,1)}, f32[512,1024]{1,0:T(8,128)}, /*index=5*/f32[32,4224]{1,0:T(8,128)}) custom-call(bf16[512,1024]{1,0:T(8,128)(2,1)} %convolution_convert_fusion.6.part_send, f32[512,1024]{1,0:T(8,128)} %fusion.60.part_own, ...), custom_call_target="tpu_custom_call" | custom-call | tf_op jit(solution)/shard_map/tail/pallas_call | solution.py:364
  536.4 1.9 slice.210
  539.0 1.4 multiply_bitcast_fusion
  540.5 3.5 copy.20
  543.9 3.5 copy.21
  548.1 1.9 select_bitcast_fusion.1
  550.0 1.8 maximum_bitcast_fusion
  551.8 0.9 copy-done.11
  552.6 1.3 copy.38
  554.0 0.8 copy-done.13
  554.8 1.1 copy.39
  (167 shorter events, 10.0 us)
Async XLA Ops:
  250.1 20.9 %copy-start.29 = (bf16[1024,128]{1,0:T(8,128)(2,1)}, bf16[1024,128]{1,0:T(8,128)(2,1)S(1)}, u32[]{:S(2)}) copy-start(bf16[1024,128]{1,0:T(8,128)(2,1)S(1)} %get-tuple-element.76) | copy-start | bytes 786436
  250.1 20.9 %copy-start.31 = (bf16[1024,128]{1,0:T(8,128)(2,1)}, bf16[1024,128]{1,0:T(8,128)(2,1)S(1)}, u32[]{:S(2)}) copy-start(bf16[1024,128]{1,0:T(8,128)(2,1)S(1)} %get-tuple-element.77) | copy-start | bytes 786436
  250.1 20.9 %copy-start.33 = (bf16[1024,128]{1,0:T(8,128)(2,1)}, bf16[1024,128]{1,0:T(8,128)(2,1)S(1)}, u32[]{:S(2)}) copy-start(bf16[1024,128]{1,0:T(8,128)(2,1)S(1)} %get-tuple-element.78) | copy-start | bytes 786436
  250.1 20.9 %copy-start.35 = (bf16[1024,128]{1,0:T(8,128)(2,1)}, bf16[1024,128]{1,0:T(8,128)(2,1)S(1)}, u32[]{:S(2)}) copy-start(bf16[1024,128]{1,0:T(8,128)(2,1)S(1)} %get-tuple-element.79) | copy-start | bytes 786436
  250.1 20.8 %copy-start.37 = (bf16[1024,128]{1,0:T(8,128)(2,1)}, bf16[1024,128]{1,0:T(8,128)(2,1)S(1)}, u32[]{:S(2)}) copy-start(bf16[1024,128]{1,0:T(8,128)(2,1)S(1)} %get-tuple-element.80) | copy-start | bytes 786436
  250.1 20.8 %copy-start.39 = (bf16[1024,128]{1,0:T(8,128)(2,1)}, bf16[1024,128]{1,0:T(8,128)(2,1)S(1)}, u32[]{:S(2)}) copy-start(bf16[1024,128]{1,0:T(8,128)(2,1)S(1)} %get-tuple-element.81) | copy-start | bytes 786436
  250.1 20.8 %copy-start.41 = (bf16[1024,128]{1,0:T(8,128)(2,1)}, bf16[1024,128]{1,0:T(8,128)(2,1)S(1)}, u32[]{:S(2)}) copy-start(bf16[1024,128]{1,0:T(8,128)(2,1)S(1)} %get-tuple-element.82) | copy-start | bytes 786436
  250.1 20.8 %copy-start.43 = (bf16[1024,128]{1,0:T(8,128)(2,1)}, bf16[1024,128]{1,0:T(8,128)(2,1)S(1)}, u32[]{:S(2)}) copy-start(bf16[1024,128]{1,0:T(8,128)(2,1)S(1)} %get-tuple-element.83) | copy-start | bytes 786436
  250.5 11.8 %copy-start.4 = (bf16[1024,1024]{1,0:T(8,128)(2,1)S(1)}, bf16[1024,1024]{1,0:T(8,128)(2,1)}, u32[]{:S(2)}) copy-start(bf16[1024,1024]{1,0:T(8,128)(2,1)} %get-tuple-element.30) | copy-start | bytes 6291460
  250.5 11.8 %copy-start.55 = (bf16[1024,1408]{1,0:T(8,128)(2,1)S(1)}, bf16[1024,1408]{1,0:T(8,128)(2,1)}, u32[]{:S(2)}) copy-start(bf16[1024,1408]{1,0:T(8,128)(2,1)} %get-tuple-element.32) | copy-start | bytes 8650756
  250.5 24.6 %slice-start = ((s8[5767168]{0:T(1024)(128)(4,1)}), s8[4194304]{0:T(1024)(128)(4,1)S(1)}, s32[]{:S(2)}) async-start(s8[5767168]{0:T(1024)(128)(4,1)} %bitcast.137), calls=%async_computation | async-start | bytes 8388608
  262.3 12.8 %slice-start.1 = ((s8[5767168]{0:T(1024)(128)(4,1)}), s8[1572864]{0:T(1024)(128)(4,1)S(1)}, s32[]{:S(2)}) async-start(s8[5767168]{0:T(1024)(128)(4,1)} %bitcast.137), calls=%async_computation.1 | async-start | bytes 3145728
  270.9 4.2 copy-start.60
  270.9 4.2 copy-start.63
  270.9 11.6 %copy-start.58 = (bf16[1024,1408]{1,0:T(8,128)(2,1)}, bf16[1024,1408]{1,0:T(8,128)(2,1)S(1)}, u32[]{:S(2)}) copy-start(bf16[1024,1408]{1,0:T(8,128)(2,1)S(1)} %get-tuple-element.62) | copy-start | bytes 8650756
  274.6 34.8 %collective-permute-start.13 = (bf16[512,1408]{1,0:T(8,128)(2,1)}, bf16[512,1408]{1,0:T(8,128)(2,1)}, u32[]{:S(2)}, u32[]{:S(2)}) collective-permute-start(bf16[512,1408]{1,0:T(8,128)(2,1)} %convolution_convert_fusion.2), channel_id=1, source_target_pairs={{0,1},{1,0},{2,3},{3,2},{4,5},{5,4},{6,7},{7,6},{8,9},{9,8},{10,11... | collective-permute-start | bytes 4325384 | tf_op jit(solution)/shard_map/ppermute | solution.py:389
  281.2 4.7 copy-start.2
  282.5 18.6 %collective-permute-start = (bf16[512,1024]{1,0:T(8,128)(2,1)}, bf16[512,1024]{1,0:T(8,128)(2,1)S(1)}, u32[]{:S(2)}, u32[]{:S(2)}) collective-permute-start(bf16[512,1024]{1,0:T(8,128)(2,1)} %slice.284), channel_id=1, source_target_pairs={{0,8},{8,0},{16,24},{24,16},{1,9},{9,1},{17,25},{25,17},{2,10},{10... | collective-permute-start | bytes 3145736 | tf_op jit(solution)/shard_map/ppermute | solution.py:394
  285.9 3.9 copy-start.64
  287.1 4.1 copy-start.61
  287.1 14.0 %collective-permute-start.8 = (bf16[512,1024]{1,0:T(8,128)(2,1)}, bf16[512,1024]{1,0:T(8,128)(2,1)}, u32[]{:S(2)}, u32[]{:S(2)}) collective-permute-start(bf16[512,1024]{1,0:T(8,128)(2,1)} %slice.283), channel_id=1, source_target_pairs={{0,8},{8,0},{16,24},{24,16},{1,9},{9,1},{17,25},{25,17},{2,10},{10... | collective-permute-start | bytes 3145736 | tf_op jit(solution)/shard_map/ppermute | solution.py:394
  288.6 7.4 %copy-start.15 = (bf16[1024,128]{1,0:T(8,128)(2,1)}, bf16[1024,128]{1,0:T(8,128)(2,1)S(1)}, u32[]{:S(2)}) copy-start(bf16[1024,128]{1,0:T(8,128)(2,1)S(1)} %get-tuple-element.85) | copy-start | bytes 786436
  288.6 7.4 %copy-start.17 = (bf16[1024,128]{1,0:T(8,128)(2,1)}, bf16[1024,128]{1,0:T(8,128)(2,1)S(1)}, u32[]{:S(2)}) copy-start(bf16[1024,128]{1,0:T(8,128)(2,1)S(1)} %get-tuple-element.86) | copy-start | bytes 786436
  288.6 7.4 %copy-start.19 = (bf16[1024,128]{1,0:T(8,128)(2,1)}, bf16[1024,128]{1,0:T(8,128)(2,1)S(1)}, u32[]{:S(2)}) copy-start(bf16[1024,128]{1,0:T(8,128)(2,1)S(1)} %get-tuple-element.87) | copy-start | bytes 786436
  288.6 7.4 %copy-start.21 = (bf16[1024,128]{1,0:T(8,128)(2,1)}, bf16[1024,128]{1,0:T(8,128)(2,1)S(1)}, u32[]{:S(2)}) copy-start(bf16[1024,128]{1,0:T(8,128)(2,1)S(1)} %get-tuple-element.88) | copy-start | bytes 786436
  288.6 7.4 %copy-start.23 = (bf16[1024,128]{1,0:T(8,128)(2,1)}, bf16[1024,128]{1,0:T(8,128)(2,1)S(1)}, u32[]{:S(2)}) copy-start(bf16[1024,128]{1,0:T(8,128)(2,1)S(1)} %get-tuple-element.89) | copy-start | bytes 786436
  288.6 7.4 %copy-start.25 = (bf16[1024,128]{1,0:T(8,128)(2,1)}, bf16[1024,128]{1,0:T(8,128)(2,1)S(1)}, u32[]{:S(2)}) copy-start(bf16[1024,128]{1,0:T(8,128)(2,1)S(1)} %get-tuple-element.90) | copy-start | bytes 786436
  288.6 7.4 %copy-start.27 = (bf16[1024,128]{1,0:T(8,128)(2,1)}, bf16[1024,128]{1,0:T(8,128)(2,1)S(1)}, u32[]{:S(2)}) copy-start(bf16[1024,128]{1,0:T(8,128)(2,1)S(1)} %get-tuple-element.91) | copy-start | bytes 786436
  291.1 6.6 %copy-start.53 = (f32[2,1024]{1,0:T(2,128)S(1)}, f32[2,1024]{1,0:T(2,128)}, u32[]{:S(2)}) copy-start(f32[2,1024]{1,0:T(2,128)} %gains.3) | copy-start | bytes 24580
  291.1 6.7 %copy-start = (f32[512,1024]{1,0:T(8,128)S(1)}, f32[512,1024]{1,0:T(8,128)}, u32[]{:S(2)}) copy-start(f32[512,1024]{1,0:T(8,128)} %get-tuple-element.31) | copy-start | bytes 6291460
  296.0 81.9 %collective-permute-start.9 = (bf16[512,2816]{1,0:T(8,128)(2,1)}, bf16[512,2816]{1,0:T(8,128)(2,1)}, u32[]{:S(2)}, u32[]{:S(2)}) collective-permute-start(bf16[512,2816]{1,0:T(8,128)(2,1)} %convolution_convert_fusion), channel_id=1, source_target_pairs={{0,1},{1,0},{2,3},{3,2},{4,5},{5,4},{6,7},{7,6},{8,9},{9,8},{10,11... | collective-permute-start | bytes 8650760 | tf_op jit(solution)/shard_map/ppermute | solution.py:389
  302.3 7.1 %copy-start.30 = (bf16[1024,128]{1,0:T(8,128)(2,1)S(1)}, bf16[1024,128]{1,0:T(8,128)(2,1)}, u32[]{:S(2)}) copy-start(bf16[1024,128]{1,0:T(8,128)(2,1)} %copy-done.29) | copy-start | bytes 786436
  302.3 7.1 %copy-start.32 = (bf16[1024,128]{1,0:T(8,128)(2,1)S(1)}, bf16[1024,128]{1,0:T(8,128)(2,1)}, u32[]{:S(2)}) copy-start(bf16[1024,128]{1,0:T(8,128)(2,1)} %copy-done.31) | copy-start | bytes 786436
  302.3 7.1 %copy-start.34 = (bf16[1024,128]{1,0:T(8,128)(2,1)S(1)}, bf16[1024,128]{1,0:T(8,128)(2,1)}, u32[]{:S(2)}) copy-start(bf16[1024,128]{1,0:T(8,128)(2,1)} %copy-done.33) | copy-start | bytes 786436
  302.3 7.1 %copy-start.36 = (bf16[1024,128]{1,0:T(8,128)(2,1)S(1)}, bf16[1024,128]{1,0:T(8,128)(2,1)}, u32[]{:S(2)}) copy-start(bf16[1024,128]{1,0:T(8,128)(2,1)} %copy-done.35) | copy-start | bytes 786436
  302.3 7.2 %copy-start.38 = (bf16[1024,128]{1,0:T(8,128)(2,1)S(1)}, bf16[1024,128]{1,0:T(8,128)(2,1)}, u32[]{:S(2)}) copy-start(bf16[1024,128]{1,0:T(8,128)(2,1)} %copy-done.37) | copy-start | bytes 786436
  302.3 7.2 %copy-start.40 = (bf16[1024,128]{1,0:T(8,128)(2,1)S(1)}, bf16[1024,128]{1,0:T(8,128)(2,1)}, u32[]{:S(2)}) copy-start(bf16[1024,128]{1,0:T(8,128)(2,1)} %copy-done.39) | copy-start | bytes 786436
  302.4 7.2 %copy-start.42 = (bf16[1024,128]{1,0:T(8,128)(2,1)S(1)}, bf16[1024,128]{1,0:T(8,128)(2,1)}, u32[]{:S(2)}) copy-start(bf16[1024,128]{1,0:T(8,128)(2,1)} %copy-done.41) | copy-start | bytes 786436
  302.4 7.2 %copy-start.44 = (bf16[1024,128]{1,0:T(8,128)(2,1)S(1)}, bf16[1024,128]{1,0:T(8,128)(2,1)}, u32[]{:S(2)}) copy-start(bf16[1024,128]{1,0:T(8,128)(2,1)} %copy-done.43) | copy-start | bytes 786436
  302.4 7.2 %copy-start.59 = (bf16[1024,1408]{1,0:T(8,128)(2,1)S(1)}, bf16[1024,1408]{1,0:T(8,128)(2,1)}, u32[]{:S(2)}) copy-start(bf16[1024,1408]{1,0:T(8,128)(2,1)} %copy-done.58) | copy-start | bytes 8650756
  312.8 4.6 copy-start.5
  312.9 19.9 %collective-permute-start.14 = (bf16[128,1408]{1,0:T(8,128)(2,1)S(1)}, bf16[128,1408]{1,0:T(8,128)(2,1)S(1)}, u32[]{:S(2)}, u32[]{:S(2)}) collective-permute-start(bf16[128,1408]{1,0:T(8,128)(2,1)S(1)} %get-tuple-element.109), channel_id=1, source_target_pairs={{0,4},{1,5},{2,6},{3,7},{4,0},{5,1},{6,2},{7,3},{8,12},{9,13},{10,... | collective-permute-start | bytes 1081352 | tf_op jit(solution)/shard_map/ppermute | solution.py:389
  313.0 19.9 %collective-permute-start.15 = (bf16[128,1408]{1,0:T(8,128)(2,1)S(1)}, bf16[128,1408]{1,0:T(8,128)(2,1)S(1)}, u32[]{:S(2)}, u32[]{:S(2)}) collective-permute-start(bf16[128,1408]{1,0:T(8,128)(2,1)S(1)} %get-tuple-element.111), channel_id=1, source_target_pairs={{0,2},{1,3},{2,0},{3,1},{4,6},{5,7},{6,4},{7,5},{8,10},{9,11},{10,... | collective-permute-start | bytes 1081352 | tf_op jit(solution)/shard_map/ppermute | solution.py:389
  316.2 21.6 %collective-permute-start.16 = (bf16[128,1408]{1,0:T(8,128)(2,1)S(1)}, bf16[128,1408]{1,0:T(8,128)(2,1)S(1)}, u32[]{:S(2)}, u32[]{:S(2)}) collective-permute-start(bf16[128,1408]{1,0:T(8,128)(2,1)S(1)} %get-tuple-element.110), channel_id=1, source_target_pairs={{0,6},{1,7},{2,4},{3,5},{4,2},{5,3},{6,0},{7,1},{8,14},{9,15},{10,... | collective-permute-start | bytes 1081352 | tf_op jit(solution)/shard_map/ppermute | solution.py:389
  319.4 19.8 %collective-permute-start.1 = (bf16[512,1024]{1,0:T(8,128)(2,1)S(1)}, bf16[512,1024]{1,0:T(8,128)(2,1)S(1)}, u32[]{:S(2)}, u32[]{:S(2)}) collective-permute-start(bf16[512,1024]{1,0:T(8,128)(2,1)S(1)} %get-tuple-element.58), channel_id=1, source_target_pairs={{0,8},{8,0},{16,24},{24,16},{1,9},{9,1},{17,25},{25,17},{2,10},{10... | collective-permute-start | bytes 3145736 | tf_op jit(solution)/shard_map/ppermute | solution.py:394
  341.2 13.9 %collective-permute-start.2 = (bf16[256,512]{1,0:T(8,128)(2,1)S(1)}, bf16[256,512]{1,0:T(8,128)(2,1)S(1)}, u32[]{:S(2)}, u32[]{:S(2)}) collective-permute-start(bf16[256,512]{1,0:T(8,128)(2,1)S(1)} %get-tuple-element.114), channel_id=1, source_target_pairs={{0,16},{1,17},{2,18},{3,19},{4,20},{5,21},{6,22},{7,23},{8,24},{9,... | collective-permute-start | bytes 786440 | tf_op jit(solution)/shard_map/ppermute | solution.py:404
  342.5 7.7 %copy-start.56 = (bf16[1024,512]{1,0:T(8,128)(2,1)S(1)}, bf16[1024,512]{1,0:T(8,128)(2,1)}, u32[]{:S(2)}) copy-start(bf16[1024,512]{1,0:T(8,128)(2,1)} %get-tuple-element.39) | copy-start | bytes 3145732
  342.5 13.4 %collective-permute-start.3 = (bf16[256,512]{1,0:T(8,128)(2,1)S(1)}, bf16[256,512]{1,0:T(8,128)(2,1)S(1)}, u32[]{:S(2)}, u32[]{:S(2)}) collective-permute-start(bf16[256,512]{1,0:T(8,128)(2,1)S(1)} %get-tuple-element.113), channel_id=1, source_target_pairs={{0,2},{1,3},{2,0},{3,1},{4,6},{5,7},{6,4},{7,5},{8,10},{9,11},{10,... | collective-permute-start | bytes 786440 | tf_op jit(solution)/shard_map/ppermute | solution.py:404
  353.3 9.4 %collective-permute-start.4 = (bf16[256,512]{1,0:T(8,128)(2,1)S(1)}, bf16[256,512]{1,0:T(8,128)(2,1)S(1)}, u32[]{:S(2)}, u32[]{:S(2)}) collective-permute-start(bf16[256,512]{1,0:T(8,128)(2,1)S(1)} %get-tuple-element.112), channel_id=1, source_target_pairs={{0,18},{1,19},{2,16},{3,17},{4,22},{5,23},{6,20},{7,21},{8,26},{9,... | collective-permute-start | bytes 786440 | tf_op jit(solution)/shard_map/ppermute | solution.py:404
  374.1 3.9 copy-start.24
  374.4 18.8 %collective-permute-start.5 = (bf16[256,1536]{1,0:T(8,128)(2,1)S(1)}, bf16[256,1536]{1,0:T(8,128)(2,1)S(1)}, u32[]{:S(2)}, u32[]{:S(2)}) collective-permute-start(bf16[256,1536]{1,0:T(8,128)(2,1)S(1)} %get-tuple-element.69), channel_id=1, source_target_pairs={{0,16},{1,17},{2,18},{3,19},{4,20},{5,21},{6,22},{7,23},{8,24},{9,... | collective-permute-start | bytes 2359304 | tf_op jit(solution)/shard_map/ppermute | solution.py:404
  375.3 35.9 %collective-permute-start.6 = (bf16[256,1536]{1,0:T(8,128)(2,1)S(1)}, bf16[256,1536]{1,0:T(8,128)(2,1)S(1)}, u32[]{:S(2)}, u32[]{:S(2)}) collective-permute-start(bf16[256,1536]{1,0:T(8,128)(2,1)S(1)} %get-tuple-element.68), channel_id=1, source_target_pairs={{0,2},{1,3},{2,0},{3,1},{4,6},{5,7},{6,4},{7,5},{8,10},{9,11},{10,... | collective-permute-start | bytes 2359304 | tf_op jit(solution)/shard_map/ppermute | solution.py:404
  376.6 52.1 %collective-permute-start.7 = (bf16[256,1536]{1,0:T(8,128)(2,1)S(1)}, bf16[256,1536]{1,0:T(8,128)(2,1)S(1)}, u32[]{:S(2)}, u32[]{:S(2)}) collective-permute-start(bf16[256,1536]{1,0:T(8,128)(2,1)S(1)} %get-tuple-element.67), channel_id=1, source_target_pairs={{0,18},{1,19},{2,16},{3,17},{4,22},{5,23},{6,20},{7,21},{8,26},{9,... | collective-permute-start | bytes 2359304 | tf_op jit(solution)/shard_map/ppermute | solution.py:404
  385.4 162.6 %collective-permute-start.10 = (bf16[128,2816]{1,0:T(8,128)(2,1)}, bf16[128,2816]{1,0:T(8,128)(2,1)}, u32[]{:S(2)}, u32[]{:S(2)}) collective-permute-start(bf16[128,2816]{1,0:T(8,128)(2,1)} %get-tuple-element.71), channel_id=1, source_target_pairs={{0,4},{1,5},{2,6},{3,7},{4,0},{5,1},{6,2},{7,3},{8,12},{9,13},{10,... | collective-permute-start | bytes 2162696 | tf_op jit(solution)/shard_map/ppermute | solution.py:389
  387.0 161.1 %collective-permute-start.11 = (bf16[128,2816]{1,0:T(8,128)(2,1)}, bf16[128,2816]{1,0:T(8,128)(2,1)}, u32[]{:S(2)}, u32[]{:S(2)}) collective-permute-start(bf16[128,2816]{1,0:T(8,128)(2,1)} %get-tuple-element.73), channel_id=1, source_target_pairs={{0,2},{1,3},{2,0},{3,1},{4,6},{5,7},{6,4},{7,5},{8,10},{9,11},{10,... | collective-permute-start | bytes 2162696 | tf_op jit(solution)/shard_map/ppermute | solution.py:389
  393.2 154.8 %collective-permute-start.12 = (bf16[128,2816]{1,0:T(8,128)(2,1)}, bf16[128,2816]{1,0:T(8,128)(2,1)}, u32[]{:S(2)}, u32[]{:S(2)}) collective-permute-start(bf16[128,2816]{1,0:T(8,128)(2,1)} %get-tuple-element.72), channel_id=1, source_target_pairs={{0,6},{1,7},{2,4},{3,5},{4,2},{5,3},{6,0},{7,1},{8,14},{9,15},{10,... | collective-permute-start | bytes 2162696 | tf_op jit(solution)/shard_map/ppermute | solution.py:389
  394.5 34.3 %copy-start.45 = (bf16[1024,128]{1,0:T(8,128)(2,1)S(1)}, bf16[1024,128]{1,0:T(8,128)(2,1)}, u32[]{:S(2)}) copy-start(bf16[1024,128]{1,0:T(8,128)(2,1)} %get-tuple-element.100) | copy-start | bytes 786436
  394.5 34.3 %copy-start.46 = (bf16[1024,128]{1,0:T(8,128)(2,1)S(1)}, bf16[1024,128]{1,0:T(8,128)(2,1)}, u32[]{:S(2)}) copy-start(bf16[1024,128]{1,0:T(8,128)(2,1)} %get-tuple-element.101) | copy-start | bytes 786436
  394.5 34.3 %copy-start.47 = (bf16[1024,128]{1,0:T(8,128)(2,1)S(1)}, bf16[1024,128]{1,0:T(8,128)(2,1)}, u32[]{:S(2)}) copy-start(bf16[1024,128]{1,0:T(8,128)(2,1)} %get-tuple-element.102) | copy-start | bytes 786436
  394.5 34.3 %copy-start.48 = (bf16[1024,128]{1,0:T(8,128)(2,1)S(1)}, bf16[1024,128]{1,0:T(8,128)(2,1)}, u32[]{:S(2)}) copy-start(bf16[1024,128]{1,0:T(8,128)(2,1)} %get-tuple-element.103) | copy-start | bytes 786436
  394.5 34.3 %copy-start.49 = (bf16[1024,128]{1,0:T(8,128)(2,1)S(1)}, bf16[1024,128]{1,0:T(8,128)(2,1)}, u32[]{:S(2)}) copy-start(bf16[1024,128]{1,0:T(8,128)(2,1)} %get-tuple-element.104) | copy-start | bytes 786436
  394.5 34.3 %copy-start.50 = (bf16[1024,128]{1,0:T(8,128)(2,1)S(1)}, bf16[1024,128]{1,0:T(8,128)(2,1)}, u32[]{:S(2)}) copy-start(bf16[1024,128]{1,0:T(8,128)(2,1)} %get-tuple-element.105) | copy-start | bytes 786436
  394.5 34.3 %copy-start.51 = (bf16[1024,128]{1,0:T(8,128)(2,1)S(1)}, bf16[1024,128]{1,0:T(8,128)(2,1)}, u32[]{:S(2)}) copy-start(bf16[1024,128]{1,0:T(8,128)(2,1)} %get-tuple-element.106) | copy-start | bytes 786436
  394.5 34.3 %copy-start.52 = (bf16[1024,128]{1,0:T(8,128)(2,1)S(1)}, bf16[1024,128]{1,0:T(8,128)(2,1)}, u32[]{:S(2)}) copy-start(bf16[1024,128]{1,0:T(8,128)(2,1)} %get-tuple-element.107) | copy-start | bytes 786436
  (20 other events, 54.9 us)

commit v4 on v3

--- a/solution.py
+++ b/solution.py
@@ -1,4 +1,5 @@
 import functools
+import math
 
 import jax
 import jax.numpy as jnp
@@ -62,9 +63,10 @@
     def __init__(self, send, recv):
         self.send, self.recv, self.count, self.started = send, recv, 0, []
 
-    def make(self, src, dst, device):
-        k = self.count
-        self.count += 1
+    def make(self, src, dst, device, index=None):
+        k = self.count if index is None else index
+        if index is None:
+            self.count += 1
         return pltpu.make_async_remote_copy(
             src_ref=src,
             dst_ref=dst,
@@ -134,18 +136,23 @@
     def forward(self, mask):
         block = flip(self.w.at, mask // 2)
         self.first[mask].wait_recv()
+        self.wire.sent(self.first[mask])
         total = self.keep[block].astype(f32) + self.arrived[block].astype(f32)
         self.sums[block] = total.astype(bf16)
         if mask:
             self.second[mask] = self.wire.start(
-                self.sums.at[block], self.landed.at[mask // 2], self.w.along_frames(mask)
+                self.sums.at[block], self.landed.at[mask // 2 - 1], self.w.along_frames(mask)
             )
+
+    def land(self):
+        for copy in self.second.values():
+            copy.wait_recv()
 
     def close(self):
         own, other = self.sums[self.w.at].astype(f32), None
         for mask in self.w.masks:
             self.second[mask].wait_recv()
-            got = self.landed[mask // 2].astype(f32)
+            got = self.landed[mask // 2 - 1].astype(f32)
             if mask & 2:
                 other = got if other is None else other + got
             else:
@@ -384,6 +391,318 @@
     )
 
 
+def ending_body(
+    n, resid, mid, gains, gain_two, result_rows, valid,
+    pair_one, pair_grad, mixed_rows, grad_qkv_rows, qkv_weight, context, ctx_pieces,
+    out_q, out_o, landed_q, landed_o, out_grad, out_result, out_context, out_ctx,
+    one, grad_two, mixed, grad_qkv, qkv_full, left_away, left_stay, part_send, part_own,
+    part_got, low, home, partner_half, half_sum, far_half, whole, result_home,
+    send_q, send_o, kept_q, kept_o, arrived_q, arrived_o,
+    context_held, ctx_held, term, term_got, term_sum, term_landed, gain_sum,
+    send_sem, recv_sem, local_sem,
+):
+    w = Where(n)
+    wire, local = Wire(send_sem, recv_sem), Local(local_sem)
+    rows, depth = resid.shape
+    piece = depth // n
+    crossing = w.core != w.place
+    load_grad = local.start(pair_grad, grad_two)
+    load_mixed = local.start(mixed_rows, mixed)
+    load_qkv = local.start(grad_qkv_rows, grad_qkv)
+    load_weight = local.start(qkv_weight, qkv_full)
+    load_one = local.start(pair_one, one)
+    load_context = local.start(context, context_held)
+    load_ctx = [
+        local.start(ctx_pieces.at[k], ctx_held.at[:, k * piece : (k + 1) * piece])
+        for k in range(n)
+    ]
+    greet(
+        [w.along_stream(1), w.along_stream(2), w.along_frames(1)]
+        + [w.along_frames(m) for m in w.masks]
+        + [w.across()]
+    )
+    cross_result = wire.make(result_rows, result_home, w.across())
+    stay_result = pltpu.make_async_copy(result_rows, result_home, local.sems.at[30])
+    stay = pltpu.make_async_copy(low, home, local.sems.at[31])
+
+    @pl.when(crossing)
+    def _():
+        cross_result.start()
+
+    @pl.when(jnp.logical_not(crossing))
+    def _():
+        stay_result.start()
+
+    def split(source, which, into):
+        for b in range(n // 2):
+            at = pl.ds(pl.multiple_of((2 * b + which) * piece, piece), piece)
+            into[:, b * piece : (b + 1) * piece] = source[:, at]
+
+    def product(left, right, into):
+        wide = right.shape[1]
+        for lo in range(0, wide, 512):
+            value = dot_rows(left[...], right[:, lo : lo + 512]).astype(bf16)
+            for b in range(n // 2):
+                into[b, :, lo : lo + 512] = value[b * piece : (b + 1) * piece]
+
+    def partial(t):
+        at = pl.ds(pl.multiple_of(t * 256, 256), 256)
+        return dot_columns(grad_qkv[at, :], qkv_full[...])
+
+    load_grad.wait()
+    split(grad_two, 1 - w.near, left_away)
+    load_mixed.wait()
+    product(left_away, mixed, send_o)
+    red_o = Reduction(w, wire, send_o, kept_o, arrived_o, send_o, landed_o, out_o)
+    for mask in red_o.order:
+        red_o.begin(mask)
+    load_qkv.wait()
+    load_weight.wait()
+
+    @pl.loop(0, rows // 256)
+    def _(t):
+        to = pl.ds(pl.multiple_of(t * 256, 256), 256)
+        part_send[to, :] = partial(rows // 256 + t).astype(bf16)
+
+    part = wire.start(part_send, part_got, w.along_stream(1))
+    load_one.wait()
+    split(one, 1 - w.near, left_away)
+    product(left_away, grad_qkv, send_q)
+    red_q = Reduction(w, wire, send_q, kept_q, arrived_q, send_q, landed_q, out_q)
+    for mask in red_q.order:
+        red_q.begin(mask)
+
+    @pl.loop(0, rows // 256)
+    def _(t):
+        to = pl.ds(pl.multiple_of(t * 256, 256), 256)
+        part_own[to, :] = partial(t)
+
+    part.wait_recv()
+    gain = gains[0:1, :]
+    gain_sum[...] = jnp.zeros_like(gain_sum)
+    step = 64
+
+    @pl.loop(0, rows // step)
+    def _(t):
+        at = pl.ds(pl.multiple_of(t * step, step), step)
+        grad = part_own[at, :].astype(f32) + part_got[at, :].astype(f32)
+        values = resid[at, :].astype(f32)
+        scale = lax.rsqrt(jnp.mean(values * values, axis=-1, keepdims=True) + norm_eps)
+        weighted = grad * gain
+        inner = jnp.mean(weighted * values, axis=-1, keepdims=True)
+        back = scale * weighted - values * (scale * scale * scale * inner)
+        low[at, :] = (mid[at, :] + back).astype(bf16)
+        gain_sum[...] += jnp.sum(grad * values * scale, axis=0, keepdims=True)
+
+    row = lax.broadcasted_iota(jnp.int32, (EXTRA, depth), 0)
+    low[rows:, :] = jnp.where(
+        row == 0, gain_sum[...], jnp.where(row == 1, gain_two[...], 0.0)
+    ).astype(bf16)
+
+    cross = wire.make(low, home, w.across())
+
+    @pl.when(crossing)
+    def _():
+        cross.start()
+
+    split(grad_two, w.near, left_stay)
+    product(left_stay, mixed, kept_o)
+    for mask in red_o.order:
+        red_o.forward(mask)
+
+    @pl.when(crossing)
+    def _():
+        cross_result.wait_recv()
+
+    @pl.when(jnp.logical_not(crossing))
+    def _():
+        stay.start()
+        stay_result.wait()
+
+    split(one, w.near, left_stay)
+    product(left_stay, grad_qkv, kept_q)
+    out_result[:, 0, :] = result_home[...].astype(f32) * valid[...]
+
+    @pl.when(crossing)
+    def _():
+        cross.wait_recv()
+
+    @pl.when(jnp.logical_not(crossing))
+    def _():
+        stay.wait()
+
+    half = (rows + EXTRA) // 2
+    mine = pl.ds(pl.multiple_of(w.core * half, 16), half)
+    theirs = pl.ds(pl.multiple_of((1 - w.core) * half, 16), half)
+    first = wire.start(home.at[theirs, :], partner_half, w.along_stream(1))
+    out_grad[:, 0, :] = home[:rows, :].astype(f32)
+    first.wait_recv()
+    half_sum[...] = (home[mine, :].astype(f32) + partner_half[...].astype(f32)).astype(bf16)
+    second = wire.start(half_sum, far_half, w.along_stream(2))
+    red_q.forward(red_q.order[0])
+    red_q.forward(red_q.order[1])
+    second.wait_recv()
+    whole[mine, :] = (half_sum[...].astype(f32) + far_half[...].astype(f32)).astype(bf16)
+    third = wire.start(whole.at[mine, :], whole.at[mine, :], w.along_stream(1))
+    load_context.wait()
+    third.wait_recv()
+
+    share = depth // 4
+    columns = pl.ds(pl.multiple_of(w.stream * share, LANES), share)
+    block = share // n
+    wide = context_held.shape[1]
+    pieces = 4
+    grad_share = whole[:rows, columns]
+    firsts, seconds = [], []
+    row = lax.broadcasted_iota(jnp.int32, (EXTRA, LANES), 0)
+    select = (row == lax.broadcasted_iota(jnp.int32, (EXTRA, LANES), 1)).astype(bf16)
+    edges = [wide * p // pieces for p in range(pieces)] + [wide + LANES]
+    for p in range(pieces):
+        lo, hi = edges[p], edges[p + 1]
+        for at in range(lo, min(hi, wide), 1024):
+            to = min(at + 1024, wide)
+            value = dot_rows(grad_share, context_held[:, at:to]).astype(bf16)
+            for k in range(n):
+                term[k // 2, k % 2, :, at:to] = value[k * block : (k + 1) * block]
+        if hi > wide:
+            value = dot_rows(whole[rows:, columns], select).astype(bf16)
+            for k in range(n):
+                term[k // 2, k % 2, :, wide:hi] = value[k * block : (k + 1) * block]
+        firsts.append(
+            wire.start(
+                term.at[:, 1 - w.near, :, lo:hi], term_got.at[:, :, lo:hi], w.along_frames(1)
+            )
+        )
+    for mask in red_q.order[2:]:
+        red_q.forward(mask)
+    for copy in load_ctx:
+        copy.wait()
+
+    def context_rows(t):
+        at = pl.ds(pl.multiple_of(t * LANES, LANES), LANES)
+        out_context[at, :] = dot_columns(whole[at, :], ctx_held[...])
+
+    @pl.loop(0, rows // LANES)
+    def _(t):
+        context_rows(t)
+
+    for p in range(pieces):
+        lo, hi = edges[p], edges[p + 1]
+        firsts[p].wait_recv()
+        for mask in w.masks + [0]:
+            to = flip(w.at, mask // 2)
+            total = term[to, w.near, :, lo:hi].astype(f32) + term_got[to, :, lo:hi].astype(f32)
+            term_sum[to, :, lo:hi] = total.astype(bf16)
+            if mask:
+                seconds.append(
+                    wire.start(
+                        term_sum.at[to, :, lo:hi],
+                        term_landed.at[mask // 2, :, lo:hi],
+                        w.along_frames(mask),
+                    )
+                )
+    red_o.land()
+    red_q.land()
+    kept = [local.start(send_o.at[w.at], out_o), local.start(send_q.at[w.at], out_q)]
+
+    @pl.when(crossing)
+    def _():
+        cross.wait_send()
+        cross_result.wait_send()
+
+    for copy in seconds:
+        copy.wait_recv()
+    total = term_sum[w.at].astype(f32)
+    for mask in w.masks:
+        total = total + term_landed[mask // 2].astype(f32)
+    out_ctx[...] = total
+    for copy in kept:
+        copy.wait()
+    wire.finish()
+
+
+def ending_scratch(n, rows, depth, context_shape, count, wide_q, wide_o):
+    halfn, block, share = n // 2, depth // n, depth // 4 // n
+    wide = context_shape[1] + LANES
+    half = (rows + EXTRA) // 2
+    both = 2 * rows
+    shapes = [
+        ((both, depth), bf16),
+        ((both, depth), bf16),
+        ((both, wide_o), bf16),
+        ((both, wide_q), bf16),
+        ((depth, wide_q), bf16),
+        ((both, depth // 2), bf16),
+        ((both, depth // 2), bf16),
+        ((rows, depth), bf16),
+        ((rows, depth), f32),
+        ((rows, depth), bf16),
+        ((rows + EXTRA, depth), bf16),
+        ((rows + EXTRA, depth), bf16),
+        ((half, depth), bf16),
+        ((half, depth), bf16),
+        ((half, depth), bf16),
+        ((rows + EXTRA, depth), bf16),
+        ((rows, depth), bf16),
+        ((halfn, block, wide_q), bf16),
+        ((halfn, block, wide_o), bf16),
+        ((halfn, block, wide_q), bf16),
+        ((halfn, block, wide_o), bf16),
+        ((halfn, block, wide_q), bf16),
+        ((halfn, block, wide_o), bf16),
+        (context_shape, bf16),
+        ((count, depth), bf16),
+        ((halfn, 2, share, wide), bf16),
+        ((halfn, share, wide), bf16),
+        ((halfn, share, wide), bf16),
+        ((halfn, share, wide), bf16),
+        ((1, depth), f32),
+    ]
+    others = [((rows, depth), f32)] * 4 + [((rows, depth), bf16)] * 2 + [((rows, count), f32)]
+    return shapes, sum(math.prod(dims) * jnp.dtype(kind).itemsize for dims, kind in shapes + others)
+
+
+def ending(
+    n, resid, mid, gains, gain_two, result_rows, valid,
+    pair_one, pair_grad, mixed, grad_qkv, qkv_full, context, ctx_pieces,
+):
+    rows, depth = resid.shape
+    halfn, block = n // 2, depth // n
+    wide_q, wide_o = qkv_full.shape[1], mixed.shape[1]
+    count = ctx_pieces.shape[1]
+    shapes, _ = ending_scratch(n, rows, depth, context.shape, count, wide_q, wide_o)
+    sems = 64 + 2 * n
+    shape = jax.ShapeDtypeStruct
+    return pl.pallas_call(
+        functools.partial(ending_body, n),
+        in_specs=[VMEM] * 6 + [ANY] * 7,
+        out_specs=[ANY] * 4 + [VMEM] * 4,
+        out_shape=[
+            shape((block, wide_q), bf16),
+            shape((block, wide_o), bf16),
+            shape((halfn - 1, block, wide_q), bf16),
+            shape((halfn - 1, block, wide_o), bf16),
+            shape((rows, 1, depth), f32),
+            shape((rows, 1, depth), f32),
+            shape((rows, count), f32),
+            shape((depth // 4 // n, context.shape[1] + LANES), f32),
+        ],
+        scratch_shapes=[pltpu.VMEM(dims, kind) for dims, kind in shapes]
+        + [
+            pltpu.SemaphoreType.DMA((sems,)),
+            pltpu.SemaphoreType.DMA((sems,)),
+            pltpu.SemaphoreType.DMA((32,)),
+        ],
+        compiler_params=pltpu.CompilerParams(
+            collective_id=6, has_side_effects=True, vmem_limit_bytes=67_000_000
+        ),
+        name="ending",
+    )(
+        resid, mid, gains, gain_two, result_rows, valid,
+        pair_one, pair_grad, mixed, grad_qkv, qkv_full, context, ctx_pieces,
+    )
+
+
 def swap_frames(value, mask):
     n = lax.axis_size("frames")
     return lax.ppermute(value, "frames", [(d, d ^ mask) for d in range(n)])
@@ -471,16 +790,15 @@
         out_ref[q, at, :] = mixed.astype(bf16)
 
 
-def attention_backward_body(qkv_ref, probs_ref, grad_ref, fold_ref, spread_ref, out_ref):
+def attention_backward_rows(at, qkv_ref, probs_ref, grad_ref, fold, spread, out_ref):
     width = grad_ref.shape[2]
-    fold, spread = fold_ref[...], spread_ref[...]
     grad_keys, grad_values = [None] * 4, [None] * 4
     for q in range(4):
-        grad = grad_ref[q].astype(f32)
-        query = qkv_ref[q, :, :width].astype(f32)
-        probs = [probs_ref[PAIRS.index((q, k))] for k in range(q + 1)]
+        grad = grad_ref[q, at, :].astype(f32)
+        query = qkv_ref[q, at, :width].astype(f32)
+        probs = [probs_ref[PAIRS.index((q, k)), at, :] for k in range(q + 1)]
         grad_probs = [
-            heads_sum(grad * qkv_ref[k, :, 2 * width :].astype(f32), fold) for k in range(q + 1)
+            heads_sum(grad * qkv_ref[k, at, 2 * width :].astype(f32), fold) for k in range(q + 1)
         ]
         total = functools.reduce(jnp.add, [p * g for p, g in zip(probs, grad_probs)])
         grad_query = None
@@ -490,14 +808,21 @@
             grad_values[k] = term if grad_values[k] is None else grad_values[k] + term
             grad_score = (probs[k] * (grad_probs[k] - total)).astype(bf16)
             wide = jnp.dot(grad_score, spread, preferred_element_type=f32)
-            term = wide * qkv_ref[k, :, width : 2 * width].astype(f32)
+            term = wide * qkv_ref[k, at, width : 2 * width].astype(f32)
             grad_query = term if grad_query is None else grad_query + term
             term = wide * query
             grad_keys[k] = term if grad_keys[k] is None else grad_keys[k] + term
-        out_ref[q, :, :width] = (grad_query * HD ** (-0.5)).astype(bf16)
+        out_ref[q, at, :width] = (grad_query * HD ** (-0.5)).astype(bf16)
     for k in range(4):
-        out_ref[k, :, width : 2 * width] = (grad_keys[k] * HD ** (-0.5)).astype(bf16)
-        out_ref[k, :, 2 * width :] = grad_values[k].astype(bf16)
+        out_ref[k, at, width : 2 * width] = (grad_keys[k] * HD ** (-0.5)).astype(bf16)
+        out_ref[k, at, 2 * width :] = grad_values[k].astype(bf16)
+
+
+def attention_backward_body(qkv_ref, probs_ref, grad_ref, fold_ref, spread_ref, out_ref):
+    everything = slice(None)
+    attention_backward_rows(
+        everything, qkv_ref, probs_ref, grad_ref, fold_ref[...], spread_ref[...], out_ref
+    )
 
 
 def fold_matrices(width):
@@ -983,6 +1308,363 @@
     )
 
 
+def back_body(
+    n, pair_two, pair_grad, resid, gu_weight, down_weight, out_weight, qkv_held, probs_held,
+    gains, fold, spread,
+    out_down, out_gu, landed_down, landed_gu, out_mid, out_gain, out_pair, out_rows, out_qkv,
+    two, grad, gu_full, down_full, out_full, two_away, two_stay, grad_away, grad_stay,
+    hidden, grad_gu, send_down, send_gu, got_down, got_gu,
+    values_mid, away, got, grad_rows, grad_mixed, qkv_mixed, probs, grad_qkv,
+    send_sem, recv_sem, tile_send, tile_recv, local_sem,
+):
+    w = Where(n)
+    wire, local = Wire(send_sem, recv_sem), Local(local_sem)
+    tiled = Wire(tile_send, tile_recv)
+    rows, depth = out_mid.shape
+    both = 2 * rows
+    piece = depth // n
+    halfn = n // 2
+    wide = down_full.shape[1]
+    tile = 2 * LANES
+    whole_tiles = wide // tile
+    tiles = whole_tiles + (1 if wide % tile else 0)
+    step = 64
+    loads = [
+        local.start(pair_two, two),
+        local.start(gu_weight, gu_full),
+        local.start(pair_grad, grad),
+        local.start(down_weight, down_full),
+    ]
+    late = [
+        local.start(resid, values_mid),
+        local.start(out_weight, out_full),
+        local.start(qkv_held, qkv_mixed),
+        local.start(probs_held, probs),
+    ]
+    greet(
+        [w.along_stream(1), w.along_stream(2), w.along_frames(1)]
+        + [w.along_frames(m) for m in w.masks]
+        + [w.with_position(3)]
+    )
+    neighbour = w.along_frames(1)
+
+    def split(source, into_away, into_stay):
+        for b in range(halfn):
+            for ref, which in ((into_away, 1 - w.near), (into_stay, w.near)):
+                at = pl.ds(pl.multiple_of((2 * b + which) * piece, piece), piece)
+                ref[:, b * piece : (b + 1) * piece] = source[:, at]
+
+    loads[0].wait()
+    split(two, two_away, two_stay)
+    loads[2].wait()
+    split(grad, grad_away, grad_stay)
+    loads[1].wait()
+    loads[3].wait()
+
+    def columns(start, size):
+        return pl.ds(pl.multiple_of(start, LANES), size)
+
+    def moves(t, size):
+        lo = t * tile
+        for j, (ref, into, start) in enumerate(
+            ((send_down, got_down, lo), (send_gu, got_gu, lo), (send_gu, got_gu, wide + lo))
+        ):
+            at = columns(start, size)
+            yield tiled.make(ref.at[:, :, at], into.at[:, :, at], neighbour, 3 * t + j)
+
+    def forward(t, size):
+        lo = t * tile
+        here = columns(lo, size)
+        there = columns(wide + lo, size)
+
+        @pl.loop(0, both // 256)
+        def _(r):
+            at = pl.ds(pl.multiple_of(r * 256, 256), 256)
+            left = two[at, :]
+            gate = jnp.dot(left, gu_full[:, here], preferred_element_type=f32)
+            up = jnp.dot(left, gu_full[:, there], preferred_element_type=f32)
+            back = jnp.dot(grad[at, :], down_full[:, here], preferred_element_type=f32)
+            sigma = 1.0 / (1.0 + jnp.exp(-gate))
+            active = gate * sigma
+            hidden[at, here] = (active * up).astype(bf16)
+            grad_gu[at, here] = (back * up * (sigma * (1.0 + gate * (1.0 - sigma)))).astype(bf16)
+            grad_gu[at, there] = (back * active).astype(bf16)
+
+        for ref, left, right, at in (
+            (send_down, grad_away, hidden, here),
+            (send_gu, two_away, grad_gu, here),
+            (send_gu, two_away, grad_gu, there),
+        ):
+            value = dot_rows(left[...], right[:, at]).astype(bf16)
+            for b in range(halfn):
+                ref[b, :, at] = value[b * piece : (b + 1) * piece]
+        for move in moves(t, size):
+            move.start()
+
+    rest = wide - whole_tiles * tile
+
+    @pl.loop(0, whole_tiles)
+    def _(t):
+        forward(t, tile)
+
+    if rest:
+        forward(whole_tiles, rest)
+
+    def landings(t, size):
+        lo = t * tile
+        for j, (ref, into, start) in enumerate(
+            ((send_down, landed_down, lo), (send_gu, landed_gu, lo), (send_gu, landed_gu, wide + lo))
+        ):
+            at = columns(start, size)
+            for k, mask in enumerate(w.masks):
+                yield tiled.make(
+                    ref.at[flip(w.at, mask // 2), :, at],
+                    into.at[mask // 2 - 1, :, at],
+                    w.along_frames(mask),
+                    3 * tiles + (3 * t + j) * len(w.masks) + k,
+                )
+
+    def reduce(t, size):
+        lo = t * tile
+        here = columns(lo, size)
+        there = columns(wide + lo, size)
+        for move in moves(t, size):
+            move.wait()
+        for ref, into, left, right, at in (
+            (send_down, got_down, grad_stay, hidden, here),
+            (send_gu, got_gu, two_stay, grad_gu, here),
+            (send_gu, got_gu, two_stay, grad_gu, there),
+        ):
+            value = dot_rows(left[...], right[:, at])
+            for b in range(halfn):
+                total = value[b * piece : (b + 1) * piece] + into[b, :, at].astype(f32)
+                ref[b, :, at] = total.astype(bf16)
+        for landing in landings(t, size):
+            landing.start()
+
+    def reduce_some(lo, hi):
+        if hi - lo == 1:
+            reduce(lo, tile)
+        elif hi > lo:
+
+            @pl.loop(lo, hi)
+            def _(t):
+                reduce(t, tile)
+
+    def rows_of(position):
+        quarter = both // 4
+        return pl.ds(pl.multiple_of(position * quarter, quarter), quarter)
+
+    def partial(left, right, t):
+        at = pl.ds(pl.multiple_of(t * 256, 256), 256)
+        return dot_columns(left[at, :], right[...])
+
+    @pl.loop(0, rows // 256)
+    def _(t):
+        to = pl.ds(pl.multiple_of(t * 256, 256), 256)
+        away[to, :] = partial(grad_gu, gu_full, rows // 256 + t).astype(bf16)
+
+    first = wire.start(away, got, w.along_stream(1))
+
+    @pl.loop(0, rows // 256)
+    def _(t):
+        to = pl.ds(pl.multiple_of(t * 256, 256), 256)
+        out_mid[to, :] = partial(grad_gu, gu_full, t)
+
+    cuts = [min(c, whole_tiles) for c in (1, 2, 3)]
+    reduce_some(0, cuts[0])
+
+    late[0].wait()
+    first.wait_recv()
+    gain = gains[1:2, :]
+    out_gain[...] = jnp.zeros_like(out_gain)
+
+    @pl.loop(0, rows // step)
+    def _(t):
+        at = pl.ds(pl.multiple_of(t * step, step), step)
+        grad_normed = out_mid[at, :] + got[at, :].astype(f32)
+        values = values_mid[at, :]
+        scale = lax.rsqrt(jnp.mean(values * values, axis=-1, keepdims=True) + norm_eps)
+        weighted = grad_normed * gain
+        inner = jnp.mean(weighted * values, axis=-1, keepdims=True)
+        total = grad[at, :].astype(f32) + scale * weighted
+        total = total - values * (scale * scale * scale * inner)
+        out_mid[at, :] = total
+        two[at, :] = total.astype(bf16)
+        out_gain[...] += jnp.sum(grad_normed * values * scale, axis=0, keepdims=True)
+
+    second = wire.start(two.at[:rows, :], two.at[rows:, :], w.along_stream(1))
+    late[1].wait()
+
+    def back_rows(lo, hi):
+        @pl.loop(lo, hi)
+        def _(t):
+            at = pl.ds(pl.multiple_of(t * 256, 256), 256)
+            value = jnp.dot(two[at, :], out_full[...], preferred_element_type=f32)
+            grad_rows[at, :] = value.astype(bf16)
+
+    back_rows(0, rows // 256)
+    second.wait_recv()
+    back_rows(rows // 256, both // 256)
+    mixing = {}
+    for mask in (3, 1, 2):
+        mixing[mask] = wire.start(
+            grad_rows.at[rows_of(flip(w.position, mask)), :],
+            grad_mixed.at[w.position],
+            w.with_position(mask),
+        )
+    own = local.start(grad_rows.at[rows_of(w.position), :], grad_mixed.at[w.position])
+    store_pair = local.start(two, out_pair)
+
+    reduce_some(cuts[0], cuts[1])
+    own.wait()
+    late[2].wait()
+    late[3].wait()
+    for mask in (2, 1, 3):
+        mixing[mask].wait_recv()
+    fold_held, spread_held = fold[...], spread[...]
+
+    @pl.loop(0, both // 4 // step)
+    def _(t):
+        at = pl.ds(pl.multiple_of(t * step, step), step)
+        attention_backward_rows(
+            at, qkv_mixed, probs, grad_mixed, fold_held, spread_held, grad_qkv
+        )
+
+    returning = {}
+    for mask in (3, 1, 2):
+        returning[mask] = wire.start(
+            grad_qkv.at[flip(w.position, mask)],
+            out_qkv.at[rows_of(w.position), :],
+            w.with_position(mask),
+        )
+    own_back = local.start(grad_qkv.at[w.position], out_qkv.at[rows_of(w.position), :])
+    reduce_some(cuts[1], cuts[2])
+
+    wire.sent(first)
+
+    @pl.loop(0, rows // 256)
+    def _(t):
+        to = pl.ds(pl.multiple_of(t * 256, 256), 256)
+        away[to, :] = partial(hidden, down_full, rows // 256 + t).astype(bf16)
+
+    third = wire.start(away, got, w.along_stream(1))
+
+    @pl.loop(0, rows // 256)
+    def _(t):
+        to = pl.ds(pl.multiple_of(t * 256, 256), 256)
+        values_mid[to, :] = values_mid[to, :] + partial(hidden, down_full, t)
+
+    third.wait_recv()
+
+    @pl.loop(0, rows // step)
+    def _(t):
+        at = pl.ds(pl.multiple_of(t * step, step), step)
+        out_rows[at, :] = (values_mid[at, :] + got[at, :].astype(f32)).astype(bf16)
+
+    reduce_some(cuts[2], whole_tiles)
+    if rest:
+        reduce(whole_tiles, rest)
+    kept = [local.start(send_down.at[w.at], out_down), local.start(send_gu.at[w.at], out_gu)]
+    own_back.wait()
+    store_pair.wait()
+    for mask in (2, 1, 3):
+        returning[mask].wait_recv()
+    for t in range(tiles):
+        for landing in landings(t, tile if t < whole_tiles else rest):
+            landing.wait()
+    for copy in kept:
+        copy.wait()
+    wire.finish()
+
+
+def back_scratch(n, rows, depth, wide, head_width):
+    both, halfn, piece = 2 * rows, n // 2, depth // n
+    pairs = len(PAIRS)
+    quarter = both // 4
+    shapes = [
+        ((both, depth), bf16),
+        ((both, depth), bf16),
+        ((depth, 2 * wide), bf16),
+        ((depth, wide), bf16),
+        ((depth, head_width), bf16),
+        ((both, depth // 2), bf16),
+        ((both, depth // 2), bf16),
+        ((both, depth // 2), bf16),
+        ((both, depth // 2), bf16),
+        ((both, wide), bf16),
+        ((both, 2 * wide), bf16),
+        ((halfn, piece, wide), bf16),
+        ((halfn, piece, 2 * wide), bf16),
+        ((halfn, piece, wide), bf16),
+        ((halfn, piece, 2 * wide), bf16),
+        ((rows, depth), f32),
+        ((rows, depth), bf16),
+        ((rows, depth), bf16),
+        ((both, head_width), bf16),
+        ((4, quarter, head_width), bf16),
+        ((4, quarter, 3 * head_width), bf16),
+        ((pairs, quarter, LANES), f32),
+        ((4, quarter, 3 * head_width), bf16),
+    ]
+    outs = [((rows, depth), f32), ((rows, depth), bf16)]
+    return shapes, sum(math.prod(dims) * jnp.dtype(kind).itemsize for dims, kind in shapes + outs)
+
+
+def back(
+    n, pair_two, pair_grad, resid, gu_full, down_full, out_full, qkv_mixed, probs, gains
+):
+    rows, depth = resid.shape
+    wide, head_width = down_full.shape[1], out_full.shape[1]
+    shapes, _ = back_scratch(n, rows, depth, wide, head_width)
+    tiles = -(-wide // (2 * LANES))
+    fold, spread = fold_matrices(head_width)
+    shape = jax.ShapeDtypeStruct
+    moves = 3 * tiles * (1 + n // 2 - 1)
+    return pl.pallas_call(
+        functools.partial(back_body, n),
+        in_specs=[ANY] * 8 + [VMEM] * 3,
+        out_specs=[ANY, ANY, ANY, ANY, VMEM, VMEM, ANY, VMEM, ANY],
+        out_shape=[
+            shape((depth // n, wide), bf16),
+            shape((depth // n, 2 * wide), bf16),
+            shape((n // 2 - 1, depth // n, wide), bf16),
+            shape((n // 2 - 1, depth // n, 2 * wide), bf16),
+            shape((rows, depth), f32),
+            shape((1, depth), f32),
+            shape((2 * rows, depth), bf16),
+            shape((rows, depth), bf16),
+            shape((2 * rows, 3 * head_width), bf16),
+        ],
+        scratch_shapes=[pltpu.VMEM(dims, kind) for dims, kind in shapes]
+        + [
+            pltpu.SemaphoreType.DMA((12,)),
+            pltpu.SemaphoreType.DMA((12,)),
+            pltpu.SemaphoreType.DMA((moves,)),
+            pltpu.SemaphoreType.DMA((moves,)),
+            pltpu.SemaphoreType.DMA((16,)),
+        ],
+        compiler_params=pltpu.CompilerParams(
+            collective_id=4, has_side_effects=True, vmem_limit_bytes=67_000_000
+        ),
+        name="back",
+    )(
+        pair_two, pair_grad, resid, gu_full, down_full, out_full, qkv_mixed, probs,
+        gains, fold, spread,
+    )
+
+
+def settled(own, landed, place):
+    total, other = own.astype(f32), None
+    for k in range(landed.shape[0]):
+        value = landed[k].astype(f32)
+        if (k + 1) & 1:
+            other = value if other is None else other + value
+        else:
+            total = total + value
+    return jnp.where(place == 0, jnp.stack([total, other]), jnp.stack([other, total]))
+
+
 def shards(
     inputs,
     context,
@@ -1035,7 +1717,6 @@
         gate_up_weight[0],
         down_weight[0],
     )
-    ctx_full = ctx_pieces.transpose(1, 0, 2).reshape(-1, width_model)
     near = frame_index % 2
 
     def paired(mine):
@@ -1063,62 +1744,119 @@
             out = lax.dynamic_update_index_in_dim(out, got, there, 0)
         return out.reshape(4 * quarter, width)
 
-    scale_two = norm_scale(resid_mid)
-    gate_up = rows_times(paired_two, gate_up_full)
-    ffn_half = down_full.shape[1]
-    gate_part = gate_up[:, :ffn_half]
-    up_part = gate_up[:, ffn_half:]
-    sigmoid_gate = jax.nn.sigmoid(gate_part)
-    activated = gate_part * sigmoid_gate
-    hidden = (activated * up_part).astype(bf16)
-
-    grad_res = paired_grad_ffn[:frame_count]
-    sum_down = scattered(halves(paired_grad_ffn, near), hidden, frame_index, place)
-    grad_hidden = rows_times(paired_grad_ffn, down_full)
-    grad_gate = grad_hidden * up_part * (sigmoid_gate * (1.0 + gate_part * (1.0 - sigmoid_gate)))
-    grad_up = grad_hidden * activated
-    grad_gu_low = jnp.concatenate([grad_gate, grad_up], axis=-1).astype(bf16)
-    grad_normed_two = own_sum(rows_back(grad_gu_low, gate_up_full))
-    sum_gate_up = scattered(halves(paired_two, near), grad_gu_low, frame_index, place)
-    back_two, grad_gain_two = norm_back(resid_mid, scale_two, gain_two, grad_normed_two)
-    grad_mid = grad_res.astype(f32) + back_two
-    paired_grad_attn = paired(grad_mid.astype(bf16))
-    grad_mixed = rows_times(paired_grad_attn, out_full).astype(bf16)
-    grad_qkv_mixed = attention_backward(qkv_mixed, probs, exchange_rows(grad_mixed, position))
-    grad_qkv_low = returned(grad_qkv_mixed)
-    def parts(left, right):
-        away, stay = halves(left, near)
-        block = width_model // n
-        return [
-            dot_rows(part, right).astype(bf16).reshape(n // 2, block, right.shape[1])
-            for part in (away, stay)
-        ]
-
-    part_away = rows_back(grad_qkv_low[frame_count:], qkv_full).astype(bf16)
-    part_stay = rows_back(grad_qkv_low[:frame_count], qkv_full)
-    result_rows = (resid_mid + own_sum(rows_back(hidden, down_full))).astype(bf16)
-    sum_qkv, sum_out, grad_home, result, sum_context, ctx_total = tail(
-        n,
-        part_away,
-        part_stay,
-        resid_in,
-        grad_mid,
-        norm_gains,
-        grad_gain_two[None],
-        result_rows,
-        *parts(paired_one, grad_qkv_low),
-        *parts(paired_grad_attn, mixed),
-        context,
-        ctx_full,
+    head_width = out_full.shape[1]
+    _, needed = back_scratch(n, frame_count, width_model, down_full.shape[1], head_width)
+    if needed <= 66_000_000 and (width_model // n) % LANES == 0:
+        (
+            own_down,
+            own_gate_up,
+            landed_down,
+            landed_gate_up,
+            grad_mid,
+            grad_gain_two,
+            paired_grad_attn,
+            result_rows,
+            grad_qkv_low,
+        ) = back(
+            n,
+            paired_two,
+            paired_grad_ffn,
+            resid_mid,
+            gate_up_full,
+            down_full,
+            out_full,
+            qkv_mixed,
+            probs,
+            norm_gains,
+        )
+        sum_down = settled(own_down, landed_down, place)
+        sum_gate_up = settled(own_gate_up, landed_gate_up, place)
+    else:
+        scale_two = norm_scale(resid_mid)
+        gate_up = rows_times(paired_two, gate_up_full)
+        ffn_half = down_full.shape[1]
+        gate_part = gate_up[:, :ffn_half]
+        up_part = gate_up[:, ffn_half:]
+        sigmoid_gate = jax.nn.sigmoid(gate_part)
+        activated = gate_part * sigmoid_gate
+        hidden = (activated * up_part).astype(bf16)
+
+        grad_res = paired_grad_ffn[:frame_count]
+        sum_down = scattered(halves(paired_grad_ffn, near), hidden, frame_index, place)
+        grad_hidden = rows_times(paired_grad_ffn, down_full)
+        grad_gate = grad_hidden * up_part * (sigmoid_gate * (1.0 + gate_part * (1.0 - sigmoid_gate)))
+        grad_up = grad_hidden * activated
+        grad_gu_low = jnp.concatenate([grad_gate, grad_up], axis=-1).astype(bf16)
+        grad_normed_two = own_sum(rows_back(grad_gu_low, gate_up_full))
+        sum_gate_up = scattered(halves(paired_two, near), grad_gu_low, frame_index, place)
+        back_two, grad_gain_two = norm_back(resid_mid, scale_two, gain_two, grad_normed_two)
+        grad_mid = grad_res.astype(f32) + back_two
+        paired_grad_attn = paired(grad_mid.astype(bf16))
+        grad_mixed = rows_times(paired_grad_attn, out_full).astype(bf16)
+        grad_qkv_mixed = attention_backward(qkv_mixed, probs, exchange_rows(grad_mixed, position))
+        grad_qkv_low = returned(grad_qkv_mixed)
+        result_rows = (resid_mid + own_sum(rows_back(hidden, down_full))).astype(bf16)
+        grad_gain_two = grad_gain_two[None]
+
+    wide_q = qkv_full.shape[1]
+    count = ctx_pieces.shape[1]
+    _, needed = ending_scratch(
+        n, frame_count, width_model, context.shape, count, wide_q, head_width
     )
-    result = result.astype(f32) * valid_mask
+    if needed <= 66_000_000 and (width_model // n) % LANES == 0:
+        own_qkv, own_out, landed_qkv, landed_out, grad_home, result, sum_context, ctx_total = ending(
+            n,
+            resid_in,
+            grad_mid,
+            norm_gains,
+            grad_gain_two,
+            result_rows,
+            valid_mask,
+            paired_one,
+            paired_grad_attn,
+            mixed,
+            grad_qkv_low,
+            qkv_full,
+            context,
+            ctx_pieces,
+        )
+        sum_qkv = settled(own_qkv, landed_qkv, place)
+        sum_out = settled(own_out, landed_out, place)
+    else:
+
+        def parts(left, right):
+            away, stay = halves(left, near)
+            block = width_model // n
+            return [
+                dot_rows(part, right).astype(bf16).reshape(n // 2, block, right.shape[1])
+                for part in (away, stay)
+            ]
+
+        part_away = rows_back(grad_qkv_low[frame_count:], qkv_full).astype(bf16)
+        part_stay = rows_back(grad_qkv_low[:frame_count], qkv_full)
+        sum_qkv, sum_out, grad_home, result, sum_context, ctx_total = tail(
+            n,
+            part_away,
+            part_stay,
+            resid_in,
+            grad_mid,
+            norm_gains,
+            grad_gain_two,
+            result_rows,
+            *parts(paired_one, grad_qkv_low),
+            *parts(paired_grad_attn, mixed),
+            context,
+            ctx_pieces.transpose(1, 0, 2).reshape(-1, width_model),
+        )
+        result = (result.astype(f32) * valid_mask)[:, None]
+        grad_home = grad_home[:, None]
     ctx_total = ctx_total.T
     sum_ctx = ctx_total[: ctx_weight.shape[0]]
     sum_gains = ctx_total[ctx_weight.shape[0] : ctx_weight.shape[0] + 2]
 
     return (
-        result[:, None],
-        grad_home[:, None],
+        result,
+        grad_home,
         sum_context,
         sum_ctx,
         sum_gains,

time: 561 us -> 521 us (0.929)
  Pallas kernels: 344 us -> 495 us
  waiting for transfers between devices: 66.7 us -> 0 us
  matrix products: 64 us -> 0 us
  local copies, waits for them, and re-layouts: 36.9 us -> 8.71 us
  starting transfers between devices: 24.1 us -> 0 us
    pallas_call x2, Pallas kernels: 102 us -> 253 us  [the longest x1 154 us: back(): pl.pallas_call(functools.partial(back_body, n), in_specs=[ANY] * 8 + [VME...]
    ppermute x17 -> x0, waiting for transfers between devices: 66.7 us -> none  [the longest x6 47.5 us: joint(): return lax.ppermute(value, ('stream', 'frames'), pairs)]
    dot_general x15 -> x0, matrix products: 64 us -> none  [the longest x3 21.6 us: rows_times(): return jnp.dot(left, right, preferred_element_type=f32)]
    ppermute x17 -> x0, starting transfers between devices: 24.1 us -> none  [the longest x6 14 us: joint(): return lax.ppermute(value, ('stream', 'frames'), pairs)]
    unnamed x140 -> x22, local copies, waits for them, and re-layouts: 24 us -> 7.61 us
    slice x7 -> x0, local copies, waits for them, and re-layouts: 6.28 us -> none  [the longest x3 3.69 us: halves(): left[:, k * block:(k + 1) * block]]
  transfers between devices with their start and end apart: 17 -> 0, of which waited for: 8 -> 0; matrix products, arithmetic and copies ran while one was open for 12% -> 0% of each run, Pallas kernels for 18% -> 0%
where the time goes in v4:
time: 521 us
  Pallas kernels  495 us (95%)
  other arithmetic  16.2 us (3%)
  local copies, waits for them, and re-layouts  8.71 us (2%)
    pallas_call x1, Pallas kernels, front(): pl.pallas_call(functools.partial(front_body, n), in_specs=[ANY, ANY, VMEM...  242 us
    pallas_call x1, Pallas kernels, back(): pl.pallas_call(functools.partial(back_body, n), in_specs=[ANY] * 8 + [VME...  154 us
    pallas_call x1, Pallas kernels, ending(): pl.pallas_call(functools.partial(ending_body, n), in_specs=[VMEM] * 6 + [...  98.8 us

profile of v4, /device:TPU:0, one launch (start us, length us, event | category | flops | bytes accessed | tf_op | source)
XLA Modules:
  0.0 521.0 jit_solution(11382575304575804896)
XLA Ops:
  0.7 0.9 fusion.5.fold
  1.6 0.7 fusion.6.spread
  2.3 0.7 fusion.13
  3.0 3.0 fusion.grad_rows
  6.0 242.0 %front.1 = (bf16[1024,1536]{1,0:T(8,128)(2,1)}, bf16[1024,512]{1,0:T(8,128)(2,1)}, bf16[1024,2816]{1,0:T(8,128)(2,1)}, bf16[1024,1408]{1,0:T(8,128)(2,1)}, bf16[...) custom-call(bf16[512,4096]{1,0:T(8,128)(2,1)} %context.3, ...), custom_call_target="tpu_custom_call" | custom-call | tf_op jit(solution)/shard_map/front/pallas_call | solution.py:1281
  248.0 154.5 %back.1 = (bf16[128,1408]{1,0:T(8,128)(2,1)}, bf16[128,2816]{1,0:T(8,128)(2,1)}, bf16[3,128,1408]{2,1,0:T(8,128)(2,1)}, bf16[3,128,2816]{2,1,0:T(8,128)(2,1)}, f...) custom-call(bf16[1024,1024]{1,0:T(8,128)(2,1)} %get-tuple-element.40, ...), custom_call_target="tpu_custom_call" | custom-call | tf_op jit(solution)/shard_map/back/pallas_call | solution.py:1624
  402.5 1.2 fusion.3
  403.7 0.0 copy-start.5
  403.7 1.2 add_bitcast_fusion.2
  404.9 0.0 copy-start
  404.9 1.2 maximum_select_fusion.2
  406.1 0.0 copy-done.5
  406.1 0.9 copy-done
  407.1 0.2 fusion.1
  407.3 0.1 add_bitcast_fusion
  407.4 0.0 copy-start.8
  407.4 1.8 maximum_select_fusion
  409.2 0.0 copy-done.8
  409.2 0.1 broadcast_in_dim.2
  409.3 0.2 copy.22
  409.5 0.7 convert_element_type.98.valid
  410.2 98.8 %ending.1 = (bf16[128,1536]{1,0:T(8,128)(2,1)}, bf16[128,512]{1,0:T(8,128)(2,1)}, bf16[3,128,1536]{2,1,0:T(8,128)(2,1)}, bf16[3,128,512]{2,1,0:T(8,128)(2,1)}, f...) custom-call(bf16[512,1024]{1,0:T(8,128)(2,1)} %get-tuple-element.39.resid, ...), custom_call_target="tpu_custom_call" | custom-call | tf_op jit(solution)/shard_map/ending/pallas_call | solution.py:676
  509.0 0.0 copy-start.4
  509.0 0.0 copy-start.7
  509.0 1.1 fusion.4
  510.1 1.0 add_bitcast_fusion.3
  511.1 0.8 maximum_select_fusion.3
  512.0 0.0 copy-done.4
  512.0 0.0 copy-done.7
  512.0 0.1 fusion.2
  512.1 0.0 copy-start.6
  512.1 0.1 add_bitcast_fusion.1
  512.2 0.0 copy-start.3
  512.2 1.3 maximum_select_fusion.1
  513.5 0.0 copy-done.6
  513.5 0.8 slice.56
  514.3 0.6 copy.23
  514.9 0.0 copy-done.3
  514.9 0.0 copy-start.2
  514.9 1.3 copy.29
  516.3 1.0 copy-done.2
  517.3 0.0 copy-start.1
  517.3 1.3 copy.30
  518.6 1.0 copy-done.1
  519.6 1.3 copy.31
  (4 shorter events, 0.0 us)
Async XLA Ops:
  403.7 2.5 copy-start.5
  404.9 2.1 copy-start
  407.4 1.8 copy-start.8
  509.0 3.0 copy-start.4
  509.0 3.0 copy-start.7
  512.1 1.4 copy-start.6
  512.2 2.8 copy-start.3
  514.9 2.3 copy-start.2
  517.3 2.3 copy-start.1

commit v5 on v4

--- a/solution.py
+++ b/solution.py
@@ -393,11 +393,11 @@
 
 def ending_body(
     n, resid, mid, gains, gain_two, result_rows, valid,
-    pair_one, pair_grad, mixed_rows, grad_qkv_rows, qkv_weight, context, ctx_pieces,
-    out_q, out_o, landed_q, landed_o, out_grad, out_result, out_context, out_ctx,
+    pair_one, pair_grad, mixed_rows, grad_qkv_rows, qkv_weight, context, ctx_pieces, up_send, up_stay,
+    out_q, out_o, out_up, landed_q, landed_o, landed_up, out_grad, out_result, out_context, out_ctx,
     one, grad_two, mixed, grad_qkv, qkv_full, left_away, left_stay, part_send, part_own,
     part_got, low, home, partner_half, half_sum, far_half, whole, result_home,
-    send_q, send_o, kept_q, kept_o, arrived_q, arrived_o,
+    send_q, send_o, kept_q, kept_o, arrived_q, arrived_o, send_up, kept_up, arrived_up,
     context_held, ctx_held, term, term_got, term_sum, term_landed, gain_sum,
     send_sem, recv_sem, local_sem,
 ):
@@ -406,11 +406,13 @@
     rows, depth = resid.shape
     piece = depth // n
     crossing = w.core != w.place
+    load_up = local.start(up_send, send_up)
     load_grad = local.start(pair_grad, grad_two)
     load_mixed = local.start(mixed_rows, mixed)
     load_qkv = local.start(grad_qkv_rows, grad_qkv)
     load_weight = local.start(qkv_weight, qkv_full)
     load_one = local.start(pair_one, one)
+    load_up_stay = local.start(up_stay, kept_up)
     load_context = local.start(context, context_held)
     load_ctx = [
         local.start(ctx_pieces.at[k], ctx_held.at[:, k * piece : (k + 1) * piece])
@@ -449,6 +451,10 @@
         at = pl.ds(pl.multiple_of(t * 256, 256), 256)
         return dot_columns(grad_qkv[at, :], qkv_full[...])
 
+    load_up.wait()
+    red_up = Reduction(w, wire, send_up, kept_up, arrived_up, send_up, landed_up, out_up)
+    for mask in red_up.order:
+        red_up.begin(mask)
     load_grad.wait()
     split(grad_two, 1 - w.near, left_away)
     load_mixed.wait()
@@ -507,6 +513,9 @@
 
     split(grad_two, w.near, left_stay)
     product(left_stay, mixed, kept_o)
+    load_up_stay.wait()
+    for mask in red_up.order[:2]:
+        red_up.forward(mask)
     for mask in red_o.order:
         red_o.forward(mask)
 
@@ -536,6 +545,8 @@
     theirs = pl.ds(pl.multiple_of((1 - w.core) * half, 16), half)
     first = wire.start(home.at[theirs, :], partner_half, w.along_stream(1))
     out_grad[:, 0, :] = home[:rows, :].astype(f32)
+    for mask in red_up.order[2:]:
+        red_up.forward(mask)
     first.wait_recv()
     half_sum[...] = (home[mine, :].astype(f32) + partner_half[...].astype(f32)).astype(bf16)
     second = wire.start(half_sum, far_half, w.along_stream(2))
@@ -601,9 +612,14 @@
                         w.along_frames(mask),
                     )
                 )
+    red_up.land()
     red_o.land()
     red_q.land()
-    kept = [local.start(send_o.at[w.at], out_o), local.start(send_q.at[w.at], out_q)]
+    kept = [
+        local.start(send_o.at[w.at], out_o),
+        local.start(send_q.at[w.at], out_q),
+        local.start(send_up.at[w.at], out_up),
+    ]
 
     @pl.when(crossing)
     def _():
@@ -621,7 +637,7 @@
     wire.finish()
 
 
-def ending_scratch(n, rows, depth, context_shape, count, wide_q, wide_o):
+def ending_scratch(n, rows, depth, context_shape, count, wide_q, wide_o, wide_up):
     halfn, block, share = n // 2, depth // n, depth // 4 // n
     wide = context_shape[1] + LANES
     half = (rows + EXTRA) // 2
@@ -650,6 +666,9 @@
         ((halfn, block, wide_o), bf16),
         ((halfn, block, wide_q), bf16),
         ((halfn, block, wide_o), bf16),
+        ((halfn, block, wide_up), bf16),
+        ((halfn, block, wide_up), bf16),
+        ((halfn, block, wide_up), bf16),
         (context_shape, bf16),
         ((count, depth), bf16),
         ((halfn, 2, share, wide), bf16),
@@ -664,24 +683,27 @@
 
 def ending(
     n, resid, mid, gains, gain_two, result_rows, valid,
-    pair_one, pair_grad, mixed, grad_qkv, qkv_full, context, ctx_pieces,
+    pair_one, pair_grad, mixed, grad_qkv, qkv_full, context, ctx_pieces, up_send, up_stay,
 ):
     rows, depth = resid.shape
     halfn, block = n // 2, depth // n
     wide_q, wide_o = qkv_full.shape[1], mixed.shape[1]
     count = ctx_pieces.shape[1]
-    shapes, _ = ending_scratch(n, rows, depth, context.shape, count, wide_q, wide_o)
+    wide_up = up_send.shape[2]
+    shapes, _ = ending_scratch(n, rows, depth, context.shape, count, wide_q, wide_o, wide_up)
     sems = 64 + 2 * n
     shape = jax.ShapeDtypeStruct
     return pl.pallas_call(
         functools.partial(ending_body, n),
-        in_specs=[VMEM] * 6 + [ANY] * 7,
-        out_specs=[ANY] * 4 + [VMEM] * 4,
+        in_specs=[VMEM] * 6 + [ANY] * 9,
+        out_specs=[ANY] * 6 + [VMEM] * 4,
         out_shape=[
             shape((block, wide_q), bf16),
             shape((block, wide_o), bf16),
+            shape((block, wide_up), bf16),
             shape((halfn - 1, block, wide_q), bf16),
             shape((halfn - 1, block, wide_o), bf16),
+            shape((halfn - 1, block, wide_up), bf16),
             shape((rows, 1, depth), f32),
             shape((rows, 1, depth), f32),
             shape((rows, count), f32),
@@ -699,7 +721,7 @@
         name="ending",
     )(
         resid, mid, gains, gain_two, result_rows, valid,
-        pair_one, pair_grad, mixed, grad_qkv, qkv_full, context, ctx_pieces,
+        pair_one, pair_grad, mixed, grad_qkv, qkv_full, context, ctx_pieces, up_send, up_stay,
     )
 
 
@@ -928,12 +950,13 @@
             self.weight.at[w.place], self.rows(w.frame), w.along_frames(1)
         )
 
-    def send(self, mask):
+    def send(self, masks):
         w = self.w
-        which = 1 - w.place if mask & 2 else w.place
-        self.far[mask] = self.wire.start(
-            self.weight.at[which], self.rows(w.frame), w.along_frames(mask)
-        )
+        for mask in masks:
+            which = 1 - w.place if mask & 2 else w.place
+            self.far[mask] = self.wire.start(
+                self.weight.at[which], self.rows(w.frame), w.along_frames(mask)
+            )
 
     def relay(self, mask):
         self.far[mask].wait_recv()
@@ -946,12 +969,12 @@
 
 
 def front_body(
-    n, context, ctx_weight, inputs, grad_rows, gains, fold, spread,
+    n, context, ctx_weight, inputs, gains, fold, spread,
     qkv_weight, out_weight, gu_weight, down_weight,
-    out_qkv, out_out, out_gu, out_down, out_ctx, out_resid, out_mid, out_one, out_two, out_grad,
+    out_qkv, out_out, out_gu, out_down, out_ctx, out_resid, out_mid, out_one, out_two,
     out_qkv_mixed, out_probs, out_mixed,
     ctx_held, context_held, total, partner_half, half_sum, far_half, whole, home, resid, pair,
-    qkv_full, out_full, qkv_rows, qkv_mixed, probs, mixed_quarter, mixed, away, got, grad_pair,
+    qkv_full, out_full, qkv_rows, qkv_mixed, probs, mixed_quarter, mixed, away, got,
     send_sem, recv_sem, local_sem,
 ):
     w = Where(n)
@@ -997,8 +1020,8 @@
             out.own_near()
         if bit == 1:
             for mask in w.masks:
-                qkv.send(mask)
-                out.send(mask)
+                qkv.send([mask])
+                out.send([mask])
         for o, copy in copies:
             copy.wait_recv()
             ctx_near(o ^ (1 << bit))
@@ -1012,15 +1035,23 @@
         value = jnp.dot(context_held[...], ctx_held[at], preferred_element_type=f32)
         total[:, columns] = value
 
+    def relay_attention(k):
+        for mask in w.masks[k : k + 1]:
+            qkv.relay(mask)
+            out.relay(mask)
+
     if piece % LANES == 0:
         for o in held:
             project(o)
         for o in held:
+            if o == held[-1]:
+                relay_attention(0)
             near[o].wait_recv()
             project(o ^ 1)
     else:
         for o in held:
             near[o].wait_recv()
+        relay_attention(0)
         total[...] = jnp.zeros_like(total)
 
         @pl.loop(0, n)
@@ -1046,9 +1077,7 @@
     first.wait_recv()
     half_sum[...] = (total[mine, :] + partner_half[...].astype(f32)).astype(bf16)
     second = wire.start(half_sum, far_half, w.along_stream(2))
-    for mask in w.masks[:1]:
-        qkv.relay(mask)
-        out.relay(mask)
+    relay_attention(1)
     second.wait_recv()
     home[mine, :] = (half_sum[...].astype(f32) + far_half[...].astype(f32)).astype(bf16)
     third = wire.start(home.at[mine, :], home.at[mine, :], w.along_stream(1))
@@ -1061,9 +1090,7 @@
         home[at, :] = (home[at, :].astype(f32) + inputs[at, :].astype(f32)).astype(bf16)
 
     cross = wire.make(home, resid, w.across())
-    cross_grad = wire.make(grad_rows, grad_pair.at[:rows, :], w.across())
     stay = pltpu.make_async_copy(home, resid, local_sem.at[22])
-    stay_grad = pltpu.make_async_copy(grad_rows, grad_pair.at[:rows, :], local_sem.at[23])
 
     @pl.when(crossing)
     def _():
@@ -1072,15 +1099,11 @@
     @pl.when(jnp.logical_not(crossing))
     def _():
         stay.start()
-        stay_grad.start()
 
     gu.own_near()
-    for mask in w.far_masks:
-        gu.send(mask)
-    for mask in w.masks[1:]:
-        qkv.relay(mask)
-        out.relay(mask)
-    down.own_near()
+    gu.send(w.far_masks + w.both_masks)
+    for k in range(2, len(w.masks)):
+        relay_attention(k)
 
     @pl.when(crossing)
     def _():
@@ -1133,8 +1156,8 @@
             w.with_position(mask),
         )
     own_quarter = local.start(qkv_rows.at[rows_of(w.position), :], qkv_mixed.at[w.position])
-    for mask in w.both_masks:
-        gu.send(mask)
+    gu.send([2])
+    down.send(w.far_masks)
     stores = [
         local.start(pair, out_one),
         local.start(qkv_full, out_qkv),
@@ -1147,7 +1170,8 @@
     own_quarter.wait()
     for mask in (2, 1, 3):
         mixing[mask].wait_recv()
-
+    for mask in w.both_masks:
+        gu.relay(mask)
     fold_held, spread_held = fold[...], spread[...]
 
     @pl.loop(0, quarter // step)
@@ -1163,17 +1187,9 @@
             w.with_position(mask),
         )
     own_back = local.start(mixed_quarter.at[w.position], mixed.at[rows_of(w.position), :])
-    gu.send(2)
-    for mask in w.masks:
-        down.send(mask)
-
-    @pl.when(crossing)
-    def _():
-        cross_grad.start()
-
+    down.send(w.both_masks + [2])
     stores += [local.start(qkv_mixed, out_qkv_mixed), local.start(probs, out_probs)]
-    for mask in w.both_masks:
-        gu.relay(mask)
+    gu.relay(2)
     own_back.wait()
     for mask in (2, 1, 3):
         returning[mask].wait_recv()
@@ -1207,27 +1223,11 @@
 
     second_pair = wire.start(pair.at[:rows, :], upper, w.along_stream(1))
     stores.append(local.start(total, out_mid))
-    gu.relay(2)
-    for mask in w.masks[:-1]:
-        down.relay(mask)
-
-    @pl.when(crossing)
-    def _():
-        cross_grad.wait_recv()
-
-    @pl.when(jnp.logical_not(crossing))
-    def _():
-        stay_grad.wait()
-
-    grad_copy = wire.start(grad_pair.at[:rows, :], grad_pair.at[rows:, :], w.along_stream(1))
-    for mask in w.masks[-1:]:
-        down.relay(mask)
     second_pair.wait_recv()
     stores.append(local.start(pair, out_two))
-    grad_copy.wait_recv()
-    stores.append(local.start(grad_pair, out_grad))
     gu.close()
-    down.close()
+    for copy in down.far.values():
+        copy.wait_recv()
     for copy in stores[1:]:
         copy.wait()
     for copy in (store_ctx, gu_own, down_own):
@@ -1236,14 +1236,12 @@
     @pl.when(crossing)
     def _():
         cross.wait_send()
-        cross_grad.wait_send()
 
     wire.finish()
 
 
 def front(
-    n, context, ctx_weight, inputs, grad_rows, gains,
-    qkv_weight, out_weight, gu_weight, down_weight,
+    n, context, ctx_weight, inputs, gains, qkv_weight, out_weight, gu_weight, down_weight,
 ):
     rows, depth = inputs.shape
     count = ctx_weight.shape[0] // 4
@@ -1272,7 +1270,6 @@
         pltpu.VMEM((2 * rows, wide_o), bf16),
         pltpu.VMEM((rows, depth), bf16),
         pltpu.VMEM((rows, depth), bf16),
-        pltpu.VMEM((2 * rows, depth), bf16),
         pltpu.SemaphoreType.DMA((24 + 10 * n,)),
         pltpu.SemaphoreType.DMA((24 + 10 * n,)),
         pltpu.SemaphoreType.DMA((24,)),
@@ -1280,8 +1277,8 @@
     shape = jax.ShapeDtypeStruct
     return pl.pallas_call(
         functools.partial(front_body, n),
-        in_specs=[ANY, ANY, VMEM, ANY, VMEM, VMEM, VMEM, ANY, ANY, ANY, ANY],
-        out_specs=[ANY] * 13,
+        in_specs=[ANY, ANY, VMEM, VMEM, VMEM, VMEM, ANY, ANY, ANY, ANY],
+        out_specs=[ANY] * 12,
         out_shape=[
             shape((depth, wide_q), bf16),
             shape((depth, wide_o), bf16),
@@ -1290,7 +1287,6 @@
             shape((n, count, depth // n), bf16),
             shape((rows, depth), bf16),
             shape((rows, depth), f32),
-            shape((2 * rows, depth), bf16),
             shape((2 * rows, depth), bf16),
             shape((2 * rows, depth), bf16),
             shape((4, quarter, wide_q), bf16),
@@ -1303,15 +1299,15 @@
         ),
         name="front",
     )(
-        context, ctx_weight, inputs, grad_rows, gains, fold, spread,
+        context, ctx_weight, inputs, gains, fold, spread,
         qkv_weight, out_weight, gu_weight, down_weight,
     )
 
 
 def back_body(
-    n, pair_two, pair_grad, resid, gu_weight, down_weight, out_weight, qkv_held, probs_held,
+    n, pair_two, home_grad, resid, gu_weight, down_half, out_weight, qkv_held, probs_held,
     gains, fold, spread,
-    out_down, out_gu, landed_down, landed_gu, out_mid, out_gain, out_pair, out_rows, out_qkv,
+    out_down, out_gate, out_up, out_up_stay, landed_down, landed_gate, out_mid, out_gain, out_pair, out_rows, out_qkv,
     two, grad, gu_full, down_full, out_full, two_away, two_stay, grad_away, grad_stay,
     hidden, grad_gu, send_down, send_gu, got_down, got_gu,
     values_mid, away, got, grad_rows, grad_mixed, qkv_mixed, probs, grad_qkv,
@@ -1332,9 +1328,11 @@
     loads = [
         local.start(pair_two, two),
         local.start(gu_weight, gu_full),
-        local.start(pair_grad, grad),
-        local.start(down_weight, down_full),
     ]
+    blocks = [
+        pl.ds(pl.multiple_of((2 * b + w.near) * piece, piece), piece) for b in range(halfn)
+    ]
+    down_own = [local.start(down_half.at[at, :], down_full.at[at, :]) for at in blocks]
     late = [
         local.start(resid, values_mid),
         local.start(out_weight, out_full),
@@ -1344,9 +1342,22 @@
     greet(
         [w.along_stream(1), w.along_stream(2), w.along_frames(1)]
         + [w.along_frames(m) for m in w.masks]
-        + [w.with_position(3)]
+        + [w.with_position(3), w.across()]
     )
+    crossing = w.core != w.place
+    cross = wire.make(home_grad, grad.at[:rows, :], w.across())
+    stay = pltpu.make_async_copy(home_grad, grad.at[:rows, :], local_sem.at[15 + n])
+
+    @pl.when(crossing)
+    def _():
+        cross.start()
+
+    @pl.when(jnp.logical_not(crossing))
+    def _():
+        stay.start()
+
     neighbour = w.along_frames(1)
+    down_near = [wire.start(down_half.at[at, :], down_full.at[at, :], neighbour) for at in blocks]
 
     def split(source, into_away, into_stay):
         for b in range(halfn):
@@ -1356,21 +1367,19 @@
 
     loads[0].wait()
     split(two, two_away, two_stay)
-    loads[2].wait()
-    split(grad, grad_away, grad_stay)
     loads[1].wait()
-    loads[3].wait()
 
     def columns(start, size):
         return pl.ds(pl.multiple_of(start, LANES), size)
 
-    def moves(t, size):
+    def tile_parts(t):
         lo = t * tile
-        for j, (ref, into, start) in enumerate(
-            ((send_down, got_down, lo), (send_gu, got_gu, lo), (send_gu, got_gu, wide + lo))
-        ):
-            at = columns(start, size)
-            yield tiled.make(ref.at[:, :, at], into.at[:, :, at], neighbour, 3 * t + j)
+        return ((send_down, got_down, lo), (send_gu, got_gu, lo), (send_gu, got_gu, wide + lo))
+
+    def move(t, size, j):
+        ref, into, start = tile_parts(t)[j]
+        at = columns(start, size)
+        return tiled.make(ref.at[:, :, at], into.at[:, :, at], neighbour, 3 * t + j)
 
     def forward(t, size):
         lo = t * tile
@@ -1383,73 +1392,117 @@
             left = two[at, :]
             gate = jnp.dot(left, gu_full[:, here], preferred_element_type=f32)
             up = jnp.dot(left, gu_full[:, there], preferred_element_type=f32)
-            back = jnp.dot(grad[at, :], down_full[:, here], preferred_element_type=f32)
-            sigma = 1.0 / (1.0 + jnp.exp(-gate))
-            active = gate * sigma
-            hidden[at, here] = (active * up).astype(bf16)
-            grad_gu[at, here] = (back * up * (sigma * (1.0 + gate * (1.0 - sigma)))).astype(bf16)
-            grad_gu[at, there] = (back * active).astype(bf16)
-
-        for ref, left, right, at in (
-            (send_down, grad_away, hidden, here),
-            (send_gu, two_away, grad_gu, here),
-            (send_gu, two_away, grad_gu, there),
-        ):
-            value = dot_rows(left[...], right[:, at]).astype(bf16)
-            for b in range(halfn):
-                ref[b, :, at] = value[b * piece : (b + 1) * piece]
-        for move in moves(t, size):
-            move.start()
-
-    rest = wide - whole_tiles * tile
-
-    @pl.loop(0, whole_tiles)
-    def _(t):
-        forward(t, tile)
-
-    if rest:
-        forward(whole_tiles, rest)
-
-    def landings(t, size):
-        lo = t * tile
-        for j, (ref, into, start) in enumerate(
-            ((send_down, landed_down, lo), (send_gu, landed_gu, lo), (send_gu, landed_gu, wide + lo))
-        ):
-            at = columns(start, size)
-            for k, mask in enumerate(w.masks):
-                yield tiled.make(
-                    ref.at[flip(w.at, mask // 2), :, at],
-                    into.at[mask // 2 - 1, :, at],
-                    w.along_frames(mask),
-                    3 * tiles + (3 * t + j) * len(w.masks) + k,
-                )
-
-    def reduce(t, size):
+            hidden[at, here] = (gate / (1.0 + jnp.exp(-gate)) * up).astype(bf16)
+            grad_gu[at, here] = gate.astype(bf16)
+            grad_gu[at, there] = up.astype(bf16)
+
+    def store_away(ref, left, right, at):
+        value = dot_rows(left[...], right[:, at]).astype(bf16)
+        for b in range(halfn):
+            ref[b, :, at] = value[b * piece : (b + 1) * piece]
+
+    def away_down(t, size):
+        store_away(send_down, grad_away, hidden, columns(t * tile, size))
+        move(t, size, 0).start()
+
+    def backward(t, size):
         lo = t * tile
         here = columns(lo, size)
         there = columns(wide + lo, size)
-        for move in moves(t, size):
-            move.wait()
-        for ref, into, left, right, at in (
-            (send_down, got_down, grad_stay, hidden, here),
-            (send_gu, got_gu, two_stay, grad_gu, here),
-            (send_gu, got_gu, two_stay, grad_gu, there),
-        ):
-            value = dot_rows(left[...], right[:, at])
-            for b in range(halfn):
-                total = value[b * piece : (b + 1) * piece] + into[b, :, at].astype(f32)
-                ref[b, :, at] = total.astype(bf16)
-        for landing in landings(t, size):
-            landing.start()
-
-    def reduce_some(lo, hi):
-        if hi - lo == 1:
-            reduce(lo, tile)
-        elif hi > lo:
-
-            @pl.loop(lo, hi)
+
+        @pl.loop(0, both // 256)
+        def _(r):
+            at = pl.ds(pl.multiple_of(r * 256, 256), 256)
+            gate = grad_gu[at, here].astype(f32)
+            up = grad_gu[at, there].astype(f32)
+            back = jnp.dot(grad[at, :], down_full[:, here], preferred_element_type=f32)
+            sigma = 1.0 / (1.0 + jnp.exp(-gate))
+            grad_gu[at, here] = (back * up * (sigma * (1.0 + gate * (1.0 - sigma)))).astype(bf16)
+            grad_gu[at, there] = (back * (gate * sigma)).astype(bf16)
+
+        store_away(send_gu, two_away, grad_gu, here)
+        store_away(send_gu, two_away, grad_gu, there)
+        move(t, size, 1).start()
+
+    rest = wide - whole_tiles * tile
+
+    def every(step_of):
+        @pl.loop(0, whole_tiles)
+        def _(t):
+            step_of(t, tile)
+
+        if rest:
+            step_of(whole_tiles, rest)
+
+    every(forward)
+
+    @pl.when(crossing)
+    def _():
+        cross.wait_recv()
+
+    @pl.when(jnp.logical_not(crossing))
+    def _():
+        stay.wait()
+
+    grad_pair = wire.start(grad.at[:rows, :], grad.at[rows:, :], w.along_stream(1))
+    grad_pair.wait_recv()
+    split(grad, grad_away, grad_stay)
+    every(away_down)
+    for copy in down_own:
+        copy.wait()
+    for copy in down_near:
+        copy.wait_recv()
+    every(backward)
+
+    landed = (landed_down, landed_gate)
+
+    def landing(t, size, j, k):
+        ref, _, start = tile_parts(t)[j]
+        mask = w.masks[k]
+        at = columns(start, size)
+        return tiled.make(
+            ref.at[flip(w.at, mask // 2), :, at],
+            landed[j].at[mask // 2 - 1, :, columns(t * tile, size)],
+            w.along_frames(mask),
+            3 * tiles + (3 * t + j) * len(w.masks) + k,
+        )
+
+    lefts = (grad_stay, two_stay, two_stay)
+    rights = (hidden, grad_gu, grad_gu)
+
+    def reduce_part(t, size, j):
+        ref, into, start = tile_parts(t)[j]
+        at = columns(start, size)
+        move(t, size, j).wait()
+        value = dot_rows(lefts[j][...], rights[j][:, at])
+        for b in range(halfn):
+            total = value[b * piece : (b + 1) * piece] + into[b, :, at].astype(f32)
+            ref[b, :, at] = total.astype(bf16)
+        for k in range(len(w.masks)):
+            landing(t, size, j, k).start()
+
+    def reduce_down(t, size):
+        reduce_part(t, size, 0)
+
+    def reduce_gu(t, size):
+        reduce_part(t, size, 1)
+
+    def stay_up(t, size):
+        at = columns(wide + t * tile, size)
+        store_away(got_gu, two_stay, grad_gu, at)
+
+    def some(step_of, lo, hi):
+        top = min(hi, whole_tiles)
+        if top > lo:
+
+            @pl.loop(lo, top)
             def _(t):
-                reduce(t, tile)
+                step_of(t, tile)
+
+        if hi > whole_tiles and rest:
+            step_of(whole_tiles, rest)
+
+    cut = min(3, whole_tiles)
 
     def rows_of(position):
         quarter = both // 4
@@ -1471,8 +1524,7 @@
         to = pl.ds(pl.multiple_of(t * 256, 256), 256)
         out_mid[to, :] = partial(grad_gu, gu_full, t)
 
-    cuts = [min(c, whole_tiles) for c in (1, 2, 3)]
-    reduce_some(0, cuts[0])
+    some(reduce_down, 0, cut)
 
     late[0].wait()
     first.wait_recv()
@@ -1516,7 +1568,7 @@
     own = local.start(grad_rows.at[rows_of(w.position), :], grad_mixed.at[w.position])
     store_pair = local.start(two, out_pair)
 
-    reduce_some(cuts[0], cuts[1])
+    some(reduce_down, cut, tiles)
     own.wait()
     late[2].wait()
     late[3].wait()
@@ -1539,7 +1591,9 @@
             w.with_position(mask),
         )
     own_back = local.start(grad_qkv.at[w.position], out_qkv.at[rows_of(w.position), :])
-    reduce_some(cuts[1], cuts[2])
+    early = min(2, whole_tiles)
+    some(reduce_gu, 0, early)
+    some(stay_up, 0, tiles)
 
     wire.sent(first)
 
@@ -1562,19 +1616,28 @@
         at = pl.ds(pl.multiple_of(t * step, step), step)
         out_rows[at, :] = (values_mid[at, :] + got[at, :].astype(f32)).astype(bf16)
 
-    reduce_some(cuts[2], whole_tiles)
-    if rest:
-        reduce(whole_tiles, rest)
-    kept = [local.start(send_down.at[w.at], out_down), local.start(send_gu.at[w.at], out_gu)]
+    some(reduce_gu, early, tiles)
+    kept = [
+        local.start(send_down.at[w.at], out_down),
+        local.start(send_gu.at[w.at, :, :wide], out_gate),
+        local.start(send_gu.at[:, :, wide:], out_up),
+        local.start(got_gu.at[:, :, wide:], out_up_stay),
+    ]
     own_back.wait()
     store_pair.wait()
     for mask in (2, 1, 3):
         returning[mask].wait_recv()
     for t in range(tiles):
-        for landing in landings(t, tile if t < whole_tiles else rest):
-            landing.wait()
+        for j in range(2):
+            for k in range(len(w.masks)):
+                landing(t, tile if t < whole_tiles else rest, j, k).wait()
     for copy in kept:
         copy.wait()
+
+    @pl.when(crossing)
+    def _():
+        cross.wait_send()
+
     wire.finish()
 
 
@@ -1612,10 +1675,10 @@
 
 
 def back(
-    n, pair_two, pair_grad, resid, gu_full, down_full, out_full, qkv_mixed, probs, gains
+    n, pair_two, home_grad, resid, gu_full, down_half, out_full, qkv_mixed, probs, gains
 ):
     rows, depth = resid.shape
-    wide, head_width = down_full.shape[1], out_full.shape[1]
+    wide, head_width = down_half.shape[1], out_full.shape[1]
     shapes, _ = back_scratch(n, rows, depth, wide, head_width)
     tiles = -(-wide // (2 * LANES))
     fold, spread = fold_matrices(head_width)
@@ -1624,12 +1687,14 @@
     return pl.pallas_call(
         functools.partial(back_body, n),
         in_specs=[ANY] * 8 + [VMEM] * 3,
-        out_specs=[ANY, ANY, ANY, ANY, VMEM, VMEM, ANY, VMEM, ANY],
+        out_specs=[ANY, ANY, ANY, ANY, ANY, ANY, VMEM, VMEM, ANY, VMEM, ANY],
         out_shape=[
             shape((depth // n, wide), bf16),
-            shape((depth // n, 2 * wide), bf16),
+            shape((depth // n, wide), bf16),
+            shape((n // 2, depth // n, wide), bf16),
+            shape((n // 2, depth // n, wide), bf16),
             shape((n // 2 - 1, depth // n, wide), bf16),
-            shape((n // 2 - 1, depth // n, 2 * wide), bf16),
+            shape((n // 2 - 1, depth // n, wide), bf16),
             shape((rows, depth), f32),
             shape((1, depth), f32),
             shape((2 * rows, depth), bf16),
@@ -1638,18 +1703,18 @@
         ],
         scratch_shapes=[pltpu.VMEM(dims, kind) for dims, kind in shapes]
         + [
-            pltpu.SemaphoreType.DMA((12,)),
-            pltpu.SemaphoreType.DMA((12,)),
+            pltpu.SemaphoreType.DMA((16 + 2 * n,)),
+            pltpu.SemaphoreType.DMA((16 + 2 * n,)),
             pltpu.SemaphoreType.DMA((moves,)),
             pltpu.SemaphoreType.DMA((moves,)),
-            pltpu.SemaphoreType.DMA((16,)),
+            pltpu.SemaphoreType.DMA((16 + n,)),
         ],
         compiler_params=pltpu.CompilerParams(
             collective_id=4, has_side_effects=True, vmem_limit_bytes=67_000_000
         ),
         name="back",
     )(
-        pair_two, pair_grad, resid, gu_full, down_full, out_full, qkv_mixed, probs,
+        pair_two, home_grad, resid, gu_full, down_half, out_full, qkv_mixed, probs,
         gains, fold, spread,
     )
 
@@ -1695,13 +1760,12 @@
         qkv_full,
         out_full,
         gate_up_full,
-        down_full,
+        down_half,
         ctx_pieces,
         resid_in,
         resid_mid,
         paired_one,
         paired_two,
-        paired_grad_ffn,
         qkv_mixed,
         probs,
         mixed,
@@ -1710,7 +1774,6 @@
         context,
         ctx_weight,
         inputs[:, 0],
-        grad_rows,
         norm_gains,
         qkv_weight[0],
         out_weight[0],
@@ -1745,13 +1808,15 @@
         return out.reshape(4 * quarter, width)
 
     head_width = out_full.shape[1]
-    _, needed = back_scratch(n, frame_count, width_model, down_full.shape[1], head_width)
+    _, needed = back_scratch(n, frame_count, width_model, down_weight.shape[3], head_width)
     if needed <= 66_000_000 and (width_model // n) % LANES == 0:
         (
             own_down,
-            own_gate_up,
+            own_gate,
+            up_send,
+            up_stay,
             landed_down,
-            landed_gate_up,
+            landed_gate,
             grad_mid,
             grad_gain_two,
             paired_grad_attn,
@@ -1760,18 +1825,23 @@
         ) = back(
             n,
             paired_two,
-            paired_grad_ffn,
+            grad_rows,
             resid_mid,
             gate_up_full,
-            down_full,
+            down_half,
             out_full,
             qkv_mixed,
             probs,
             norm_gains,
         )
         sum_down = settled(own_down, landed_down, place)
-        sum_gate_up = settled(own_gate_up, landed_gate_up, place)
     else:
+        paired_grad_ffn = paired(transposed(grad_rows))
+        blocks = down_half.reshape(n // 2, 2, -1, down_half.shape[1])
+        blocks = lax.dynamic_index_in_dim(blocks, near, 1, keepdims=False)
+        others = swap_frames(blocks, 1)
+        even, odd = jnp.where(near == 0, blocks, others), jnp.where(near == 0, others, blocks)
+        down_full = jnp.stack([even, odd], axis=1).reshape(down_half.shape)
         scale_two = norm_scale(resid_mid)
         gate_up = rows_times(paired_two, gate_up_full)
         ffn_half = down_full.shape[1]
@@ -1801,10 +1871,21 @@
     wide_q = qkv_full.shape[1]
     count = ctx_pieces.shape[1]
     _, needed = ending_scratch(
-        n, frame_count, width_model, context.shape, count, wide_q, head_width
+        n, frame_count, width_model, context.shape, count, wide_q, head_width, down_half.shape[1]
     )
     if needed <= 66_000_000 and (width_model // n) % LANES == 0:
-        own_qkv, own_out, landed_qkv, landed_out, grad_home, result, sum_context, ctx_total = ending(
+        (
+            own_qkv,
+            own_out,
+            own_up,
+            landed_qkv,
+            landed_out,
+            landed_up,
+            grad_home,
+            result,
+            sum_context,
+            ctx_total,
+        ) = ending(
             n,
             resid_in,
             grad_mid,
@@ -1819,6 +1900,11 @@
             qkv_full,
             context,
             ctx_pieces,
+            up_send,
+            up_stay,
+        )
+        sum_gate_up = jnp.concatenate(
+            [settled(own_gate, landed_gate, place), settled(own_up, landed_up, place)], axis=-1
         )
         sum_qkv = settled(own_qkv, landed_qkv, place)
         sum_out = settled(own_out, landed_out, place)

time: 521 us -> 501 us (0.962)
  Pallas kernels: 495 us -> 475 us
    pallas_call x1, Pallas kernels: 242 us -> 201 us  [front(): pl.pallas_call(functools.partial(front_body, n), in_specs=[ANY, ANY, VMEM...]
    pallas_call x1, Pallas kernels: 98.8 us -> 120 us  [ending(): pl.pallas_call(functools.partial(ending_body, n), in_specs=[VMEM] * 6 + [...]
where the time goes in v5:
time: 501 us
  Pallas kernels  475 us (95%)
  other arithmetic  14.8 us (3%)
  local copies, waits for them, and re-layouts  10.6 us (2%)
    pallas_call x1, Pallas kernels, front(): pl.pallas_call(functools.partial(front_body, n), in_specs=[ANY, ANY, VMEM...  201 us
    pallas_call x1, Pallas kernels, back(): pl.pallas_call(functools.partial(back_body, n), in_specs=[ANY] * 8 + [VME...  154 us
    pallas_call x1, Pallas kernels, ending(): pl.pallas_call(functools.partial(ending_body, n), in_specs=[VMEM] * 6 + [...  120 us

profile of v5, /device:TPU:0, one launch (start us, length us, event | category | flops | bytes accessed | tf_op | source)
XLA Modules:
  0.0 500.8 jit_solution(6149005569210856422)
XLA Ops:
  0.7 0.7 fusion.7.spread
  1.4 0.9 fusion.6.fold
  2.3 0.0 copy-start.13
  2.3 200.9 %front.1 = (bf16[1024,1536]{1,0:T(8,128)(2,1)}, bf16[1024,512]{1,0:T(8,128)(2,1)}, bf16[1024,2816]{1,0:T(8,128)(2,1)}, bf16[1024,1408]{1,0:T(8,128)(2,1)}, bf16[...) custom-call(bf16[512,4096]{1,0:T(8,128)(2,1)} %context.3, ...), custom_call_target="tpu_custom_call" | custom-call | tf_op jit(solution)/shard_map/front/pallas_call | solution.py:1278
  203.2 0.0 copy-done.13
  203.2 0.1 fusion.14
  203.3 3.0 fusion.home_grad
  206.2 154.1 %back.1 = (bf16[128,1408]{1,0:T(8,128)(2,1)}, bf16[128,1408]{1,0:T(8,128)(2,1)}, bf16[4,128,1408]{2,1,0:T(8,128)(2,1)}, bf16[4,128,1408]{2,1,0:T(8,128)(2,1)}, b...) custom-call(bf16[1024,1024]{1,0:T(8,128)(2,1)} %get-tuple-element.43, ...), custom_call_target="tpu_custom_call" | custom-call | tf_op jit(solution)/shard_map/back/pallas_call | solution.py:1687
  360.3 0.0 copy-start.7
  360.3 1.3 fusion.2
  361.6 0.2 copy-done.7
  361.7 0.1 add_bitcast_fusion.1
  361.8 0.0 copy-start.5
  361.9 0.0 copy-start.11
  361.9 1.2 maximum_select_fusion.3
  363.1 0.5 copy-done.5
  363.6 0.1 copy-done.11
  363.7 0.1 fusion.4
  363.8 0.1 convert_add_fusion.5
  363.8 1.2 maximum_select_fusion.1
  365.0 0.1 broadcast_in_dim.4
  365.1 0.2 copy.22
  365.3 0.7 convert_element_type.115.valid
  366.0 119.6 %ending.1 = (bf16[128,1536]{1,0:T(8,128)(2,1)}, bf16[128,512]{1,0:T(8,128)(2,1)}, bf16[128,1408]{1,0:T(8,128)(2,1)}, bf16[3,128,1536]{2,1,0:T(8,128)(2,1)}, bf16...) custom-call(bf16[512,1024]{1,0:T(8,128)(2,1)} %get-tuple-element.42., ...), custom_call_target="tpu_custom_call" | custom-call | tf_op jit(solution)/shard_map/ending/pallas_call | solution.py:696
  485.6 0.0 copy-start.6
  485.6 1.3 fusion.3
  486.9 0.2 copy-done.6
  487.1 0.1 convert_add_fusion.4
  487.2 0.0 copy-start
  487.2 0.1 maximum_select_fusion.2
  487.3 1.2 copy-done
  488.5 0.0 copy-start.10
  488.5 0.0 copy-start.12
  488.5 1.8 maximum_bitcast_fusion
  490.3 0.0 copy-start.4
  490.3 0.0 copy-start.9
  490.3 0.0 copy-done.10
  490.3 0.0 copy-done.12
  490.4 0.8 maximum_select_fusion.4
  491.2 0.5 copy-done.4
  491.8 0.1 copy-done.9
  491.8 0.1 fusion.1
  491.9 0.1 add_bitcast_fusion
  492.0 0.0 copy-start.8
  492.0 0.0 copy-start.3
  492.1 1.3 maximum_select_fusion
  493.3 0.0 copy-done.8
  493.3 0.8 slice.68
  494.2 0.6 copy.23
  494.8 0.0 copy-done.3
  494.8 0.0 copy-start.2
  494.8 1.3 copy.29
  496.1 1.0 copy-done.2
  497.1 0.0 copy-start.1
  497.1 1.3 copy.30
  498.5 1.0 copy-done.1
  499.5 1.3 copy.31
  (6 shorter events, 0.1 us)
Async XLA Ops:
  2.3 200.9 %copy-start.13 = (s32[4]{0:T(128)S(1)}, s32[4]{0:T(128)}, u32[]{:S(2)}) copy-start(s32[4]{0:T(128)} %param.13) | copy-start | bytes 52
  360.3 1.5 copy-start.7
  361.8 1.7 copy-start.5
  361.9 1.8 copy-start.11
  485.6 1.5 copy-start.6
  487.2 1.4 copy-start
  488.5 1.8 copy-start.10
  488.5 1.8 copy-start.12
  490.3 1.5 copy-start.4
  490.3 1.5 copy-start.9
  492.0 1.3 copy-start.8
  492.0 2.8 copy-start.3
  494.8 2.3 copy-start.2
  497.1 2.3 copy-start.1

commit v6 on v5

--- a/solution.py
+++ b/solution.py
@@ -3,6 +3,7 @@
 
 import jax
 import jax.numpy as jnp
+import numpy as np
 from jax import lax
 from jax.experimental import pallas as pl
 from jax.experimental.pallas import tpu as pltpu
@@ -392,7 +393,7 @@
 
 
 def ending_body(
-    n, resid, mid, gains, gain_two, result_rows, valid,
+    n, resid, mid, gains, gain_two, result_rows,
     pair_one, pair_grad, mixed_rows, grad_qkv_rows, qkv_weight, context, ctx_pieces, up_send, up_stay,
     out_q, out_o, out_up, landed_q, landed_o, landed_up, out_grad, out_result, out_context, out_ctx,
     one, grad_two, mixed, grad_qkv, qkv_full, left_away, left_stay, part_send, part_own,
@@ -530,7 +531,7 @@
 
     split(one, w.near, left_stay)
     product(left_stay, grad_qkv, kept_q)
-    out_result[:, 0, :] = result_home[...].astype(f32) * valid[...]
+    store_result = local.start(result_home, out_result)
 
     @pl.when(crossing)
     def _():
@@ -544,7 +545,7 @@
     mine = pl.ds(pl.multiple_of(w.core * half, 16), half)
     theirs = pl.ds(pl.multiple_of((1 - w.core) * half, 16), half)
     first = wire.start(home.at[theirs, :], partner_half, w.along_stream(1))
-    out_grad[:, 0, :] = home[:rows, :].astype(f32)
+    store_grad = local.start(home.at[:rows, :], out_grad)
     for mask in red_up.order[2:]:
         red_up.forward(mask)
     first.wait_recv()
@@ -616,6 +617,8 @@
     red_o.land()
     red_q.land()
     kept = [
+        store_result,
+        store_grad,
         local.start(send_o.at[w.at], out_o),
         local.start(send_q.at[w.at], out_q),
         local.start(send_up.at[w.at], out_up),
@@ -682,7 +685,7 @@
 
 
 def ending(
-    n, resid, mid, gains, gain_two, result_rows, valid,
+    n, resid, mid, gains, gain_two, result_rows,
     pair_one, pair_grad, mixed, grad_qkv, qkv_full, context, ctx_pieces, up_send, up_stay,
 ):
     rows, depth = resid.shape
@@ -695,8 +698,8 @@
     shape = jax.ShapeDtypeStruct
     return pl.pallas_call(
         functools.partial(ending_body, n),
-        in_specs=[VMEM] * 6 + [ANY] * 9,
-        out_specs=[ANY] * 6 + [VMEM] * 4,
+        in_specs=[VMEM] * 5 + [ANY] * 9,
+        out_specs=[ANY] * 8 + [VMEM] * 2,
         out_shape=[
             shape((block, wide_q), bf16),
             shape((block, wide_o), bf16),
@@ -704,8 +707,8 @@
             shape((halfn - 1, block, wide_q), bf16),
             shape((halfn - 1, block, wide_o), bf16),
             shape((halfn - 1, block, wide_up), bf16),
-            shape((rows, 1, depth), f32),
-            shape((rows, 1, depth), f32),
+            shape((rows, depth), bf16),
+            shape((rows, depth), bf16),
             shape((rows, count), f32),
             shape((depth // 4 // n, context.shape[1] + LANES), f32),
         ],
@@ -720,9 +723,66 @@
         ),
         name="ending",
     )(
-        resid, mid, gains, gain_two, result_rows, valid,
+        resid, mid, gains, gain_two, result_rows,
         pair_one, pair_grad, mixed, grad_qkv, qkv_full, context, ctx_pieces, up_send, up_stay,
     )
+
+
+def finish_body(
+    own_q, own_o, own_gate, own_up, own_down, far_q, far_o, far_gate, far_up, far_down,
+    grad, result, valid, out_q, out_o, out_gu, out_down, out_grad, out_result,
+):
+    place = (lax.axis_index("frames") // 2) % 2
+
+    def settle(own, far, out, columns):
+        total, other = own[...].astype(f32), None
+        for k in range(far.shape[0]):
+            value = far[k].astype(f32)
+            if (k + 1) & 1:
+                other = value if other is None else other + value
+            else:
+                total = total + value
+        out[place, :, columns] = total
+        out[1 - place, :, columns] = other
+
+    wide = own_gate.shape[1]
+    settle(own_q, far_q, out_q, slice(None))
+    settle(own_o, far_o, out_o, slice(None))
+    settle(own_gate, far_gate, out_gu, slice(0, wide))
+    settle(own_up, far_up, out_gu, slice(wide, 2 * wide))
+    settle(own_down, far_down, out_down, slice(None))
+    out_grad[:, 0, :] = grad[...].astype(f32)
+    out_result[:, 0, :] = result[...].astype(f32) * valid[...]
+
+
+def finish(owns, fars, grad, result, valid, steps=4):
+    block = owns[0].shape[0] // steps
+    rows, depth = grad.shape
+    shape = jax.ShapeDtypeStruct
+    q, o, gate, up, down = [own.shape[1] for own in owns]
+    here = rows // steps
+
+    def own_spec(wide):
+        return pl.BlockSpec((block, wide), lambda t: (t, 0))
+
+    def far_spec(count, wide):
+        return pl.BlockSpec((count, block, wide), lambda t: (0, t, 0))
+
+    widths = (q, o, gate + up, down)
+    row_out = pl.BlockSpec((here, 1, depth), lambda t: (t, 0, 0))
+    return pl.pallas_call(
+        finish_body,
+        grid=(steps,),
+        in_specs=[own_spec(x.shape[1]) for x in owns]
+        + [far_spec(x.shape[0], x.shape[2]) for x in fars]
+        + [pl.BlockSpec((here, depth), lambda t: (t, 0))] * 2
+        + [pl.BlockSpec((here, 1), lambda t: (t, 0))],
+        out_specs=[far_spec(2, wide) for wide in widths] + [row_out, row_out],
+        out_shape=[shape((2, owns[0].shape[0], wide), f32) for wide in widths]
+        + [shape((rows, 1, depth), f32)] * 2,
+        compiler_params=pltpu.CompilerParams(vmem_limit_bytes=60 << 20),
+        name="finish",
+    )(*owns, *fars, grad, result, valid)
 
 
 def swap_frames(value, mask):
@@ -848,10 +908,8 @@
 
 
 def fold_matrices(width):
-    feature = lax.broadcasted_iota(jnp.int32, (width, LANES), 0) // HD
-    head = lax.broadcasted_iota(jnp.int32, (width, LANES), 1)
-    fold = (feature == head).astype(bf16)
-    return fold, fold.T
+    fold = np.arange(width)[:, None] // HD == np.arange(LANES)[None, :]
+    return jnp.asarray(fold, bf16), jnp.asarray(fold.T, bf16)
 
 
 def attention_backward(qkv, probs, grad, step=64):
@@ -969,12 +1027,12 @@
 
 
 def front_body(
-    n, context, ctx_weight, inputs, gains, fold, spread,
+    n, context, ctx_weight, inputs, cotangent, valid, gains, fold, spread,
     qkv_weight, out_weight, gu_weight, down_weight,
-    out_qkv, out_out, out_gu, out_down, out_ctx, out_resid, out_mid, out_one, out_two,
+    out_qkv, out_out, out_gu, out_down, out_ctx, out_resid, out_mid, out_one, out_two, out_grad,
     out_qkv_mixed, out_probs, out_mixed,
     ctx_held, context_held, total, partner_half, half_sum, far_half, whole, home, resid, pair,
-    qkv_full, out_full, qkv_rows, qkv_mixed, probs, mixed_quarter, mixed, away, got,
+    qkv_full, out_full, qkv_rows, qkv_mixed, probs, mixed_quarter, mixed, away, got, grad_low,
     send_sem, recv_sem, local_sem,
 ):
     w = Where(n)
@@ -1158,11 +1216,17 @@
     own_quarter = local.start(qkv_rows.at[rows_of(w.position), :], qkv_mixed.at[w.position])
     gu.send([2])
     down.send(w.far_masks)
+    @pl.loop(0, rows // step)
+    def _(t):
+        at = pl.ds(pl.multiple_of(t * step, step), step)
+        grad_low[at, :] = (cotangent[at, 0, :] * valid[at, :]).astype(bf16)
+
     stores = [
         local.start(pair, out_one),
         local.start(qkv_full, out_qkv),
         local.start(out_full, out_out),
         local.start(resid, out_resid),
+        local.start(grad_low, out_grad),
     ]
     gu_own, down_own = gu.own(local), down.own(local)
     for mask in w.far_masks:
@@ -1241,7 +1305,8 @@
 
 
 def front(
-    n, context, ctx_weight, inputs, gains, qkv_weight, out_weight, gu_weight, down_weight,
+    n, context, ctx_weight, inputs, cotangent, valid, gains,
+    qkv_weight, out_weight, gu_weight, down_weight,
 ):
     rows, depth = inputs.shape
     count = ctx_weight.shape[0] // 4
@@ -1270,6 +1335,7 @@
         pltpu.VMEM((2 * rows, wide_o), bf16),
         pltpu.VMEM((rows, depth), bf16),
         pltpu.VMEM((rows, depth), bf16),
+        pltpu.VMEM((rows, depth), bf16),
         pltpu.SemaphoreType.DMA((24 + 10 * n,)),
         pltpu.SemaphoreType.DMA((24 + 10 * n,)),
         pltpu.SemaphoreType.DMA((24,)),
@@ -1277,8 +1343,8 @@
     shape = jax.ShapeDtypeStruct
     return pl.pallas_call(
         functools.partial(front_body, n),
-        in_specs=[ANY, ANY, VMEM, VMEM, VMEM, VMEM, ANY, ANY, ANY, ANY],
-        out_specs=[ANY] * 12,
+        in_specs=[ANY, ANY, VMEM, VMEM, VMEM, VMEM, VMEM, VMEM, ANY, ANY, ANY, ANY],
+        out_specs=[ANY] * 13,
         out_shape=[
             shape((depth, wide_q), bf16),
             shape((depth, wide_o), bf16),
@@ -1289,6 +1355,7 @@
             shape((rows, depth), f32),
             shape((2 * rows, depth), bf16),
             shape((2 * rows, depth), bf16),
+            shape((rows, depth), bf16),
             shape((4, quarter, wide_q), bf16),
             shape((pairs, quarter, LANES), f32),
             shape((2 * rows, wide_o), bf16),
@@ -1299,7 +1366,7 @@
         ),
         name="front",
     )(
-        context, ctx_weight, inputs, gains, fold, spread,
+        context, ctx_weight, inputs, cotangent, valid, gains, fold, spread,
         qkv_weight, out_weight, gu_weight, down_weight,
     )
 
@@ -1719,17 +1786,6 @@
     )
 
 
-def settled(own, landed, place):
-    total, other = own.astype(f32), None
-    for k in range(landed.shape[0]):
-        value = landed[k].astype(f32)
-        if (k + 1) & 1:
-            other = value if other is None else other + value
-        else:
-            total = total + value
-    return jnp.where(place == 0, jnp.stack([total, other]), jnp.stack([other, total]))
-
-
 def shards(
     inputs,
     context,
@@ -1755,7 +1811,6 @@
     gain_one = norm_gains[0]
     gain_two = norm_gains[1]
 
-    grad_rows = (cotangent[:, 0] * valid_mask).astype(bf16)
     (
         qkv_full,
         out_full,
@@ -1766,6 +1821,7 @@
         resid_mid,
         paired_one,
         paired_two,
+        grad_rows,
         qkv_mixed,
         probs,
         mixed,
@@ -1774,6 +1830,8 @@
         context,
         ctx_weight,
         inputs[:, 0],
+        cotangent,
+        valid_mask,
         norm_gains,
         qkv_weight[0],
         out_weight[0],
@@ -1834,7 +1892,6 @@
             probs,
             norm_gains,
         )
-        sum_down = settled(own_down, landed_down, place)
     else:
         paired_grad_ffn = paired(transposed(grad_rows))
         blocks = down_half.reshape(n // 2, 2, -1, down_half.shape[1])
@@ -1892,7 +1949,6 @@
             norm_gains,
             grad_gain_two,
             result_rows,
-            valid_mask,
             paired_one,
             paired_grad_attn,
             mixed,
@@ -1903,11 +1959,13 @@
             up_send,
             up_stay,
         )
-        sum_gate_up = jnp.concatenate(
-            [settled(own_gate, landed_gate, place), settled(own_up, landed_up, place)], axis=-1
+        sum_qkv, sum_out, sum_gate_up, sum_down, grad_home, result = finish(
+            (own_qkv, own_out, own_gate, own_up, own_down),
+            (landed_qkv, landed_out, landed_gate, landed_up, landed_down),
+            grad_home,
+            result,
+            valid_mask,
         )
-        sum_qkv = settled(own_qkv, landed_qkv, place)
-        sum_out = settled(own_out, landed_out, place)
     else:
 
         def parts(left, right):

time: 501 us -> 489 us (0.976)
  other arithmetic: 14.8 us -> 0.75 us
  Pallas kernels: 475 us -> 482 us
  local copies, waits for them, and re-layouts: 10.6 us -> 5.42 us
    unnamed x32 -> x4, local copies, waits for them, and re-layouts: 9.53 us -> 1.96 us
    pallas_call x1 -> x2, Pallas kernels: 120 us -> 127 us  [the longest x1 118 us: ending(): pl.pallas_call(functools.partial(ending_body, n), in_specs=[VMEM] * 5 + [...]
where the time goes in v6:
time: 489 us
  Pallas kernels  482 us (99%)
  local copies, waits for them, and re-layouts  5.42 us (1%)
    pallas_call x1, Pallas kernels, front(): pl.pallas_call(functools.partial(front_body, n), in_specs=[ANY, ANY, VMEM...  202 us
    pallas_call x1, Pallas kernels, back(): pl.pallas_call(functools.partial(back_body, n), in_specs=[ANY] * 8 + [VME...  154 us
    pallas_call x1, Pallas kernels, ending(): pl.pallas_call(functools.partial(ending_body, n), in_specs=[VMEM] * 5 + [...  118 us

profile of v6, /device:TPU:0, one launch (start us, length us, event | category | flops | bytes accessed | tf_op | source)
XLA Modules:
  0.0 489.1 jit_solution(4981787981927367469)
XLA Ops:
  0.6 0.7 broadcast_in_dim.16
  1.4 0.1 copy.24
  1.5 0.7 fusion.4.valid
  2.3 201.6 %front.1 = (bf16[1024,1536]{1,0:T(8,128)(2,1)}, bf16[1024,512]{1,0:T(8,128)(2,1)}, bf16[1024,2816]{1,0:T(8,128)(2,1)}, bf16[1024,1408]{1,0:T(8,128)(2,1)}, bf16[...) custom-call(bf16[512,4096]{1,0:T(8,128)(2,1)} %context.3, ...), custom_call_target="tpu_custom_call" | custom-call | tf_op jit(solution)/shard_map/front/pallas_call | solution.py:1344
  203.9 154.0 %back.1 = (bf16[128,1408]{1,0:T(8,128)(2,1)}, bf16[128,1408]{1,0:T(8,128)(2,1)}, bf16[4,128,1408]{2,1,0:T(8,128)(2,1)}, bf16[4,128,1408]{2,1,0:T(8,128)(2,1)}, b...) custom-call(bf16[1024,1024]{1,0:T(8,128)(2,1)} %get-tuple-element.50, ...), custom_call_target="tpu_custom_call" | custom-call | tf_op jit(solution)/shard_map/back/pallas_call | solution.py:1754
  357.9 118.3 %ending.1 = (bf16[128,1536]{1,0:T(8,128)(2,1)}, bf16[128,512]{1,0:T(8,128)(2,1)}, bf16[128,1408]{1,0:T(8,128)(2,1)}, bf16[3,128,1536]{2,1,0:T(8,128)(2,1)}, bf16...) custom-call(bf16[512,1024]{1,0:T(8,128)(2,1)} %get-tuple-element.49., ...), custom_call_target="tpu_custom_call" | custom-call | tf_op jit(solution)/shard_map/ending/pallas_call | solution.py:699
  476.2 0.7 slice.9
  477.0 1.9 slice.8
  478.8 0.6 copy.25
  479.5 0.0 copy-start
  479.5 8.3 %finish.1 = (f32[2,128,1536]{2,1,0:T(8,128)}, f32[2,128,512]{2,1,0:T(8,128)}, f32[2,128,2816]{2,1,0:T(8,128)}, f32[2,128,1408]{2,1,0:T(8,128)}, f32[512,1,1024]{2,1,0:T(1,128)}, /*index=5*/f32[512,1,1024]{2,1,0:T(1,128)}) custom-call(bf16[128,1536]{1,0:T(8,128)(2,1)} %get-tuple-element.69.own_q, bf16[128,512]{1,0:T(8,128)(2,1)} %get-tuple-element.70.own_o, ...), custom_call_target="tpu_custom_call" | custom-call | tf_op jit(solution)/shard_map/finish/pallas_call | solution.py:773
  487.8 0.0 copy-done
  487.8 1.3 copy.27
Async XLA Ops:
  479.5 8.3 %copy-start = (f32[512,1024]{1,0:T(8,128)S(1)}, f32[512,1024]{1,0:T(8,128)}, u32[]{:S(2)}) copy-start(f32[512,1024]{1,0:T(8,128)} %get-tuple-element.118) | copy-start | bytes 6291460

commit v7 on v6

--- a/solution.py
+++ b/solution.py
@@ -1424,7 +1424,14 @@
         stay.start()
 
     neighbour = w.along_frames(1)
-    down_near = [wire.start(down_half.at[at, :], down_full.at[at, :], neighbour) for at in blocks]
+    cut = min(3, whole_tiles)
+    down_near = [
+        [
+            wire.start(down_half.at[at, span], down_full.at[at, span], neighbour)
+            for at in blocks
+        ]
+        for span in (slice(0, cut * tile), slice(cut * tile, wide))
+    ]
 
     def split(source, into_away, into_stay):
         for b in range(halfn):
@@ -1493,6 +1500,17 @@
 
     rest = wide - whole_tiles * tile
 
+    def some(step_of, lo, hi):
+        top = min(hi, whole_tiles)
+        if top > lo:
+
+            @pl.loop(lo, top)
+            def _(t):
+                step_of(t, tile)
+
+        if hi > whole_tiles and rest:
+            step_of(whole_tiles, rest)
+
     def every(step_of):
         @pl.loop(0, whole_tiles)
         def _(t):
@@ -1517,9 +1535,12 @@
     every(away_down)
     for copy in down_own:
         copy.wait()
-    for copy in down_near:
+    for copy in down_near[0]:
         copy.wait_recv()
-    every(backward)
+    some(backward, 0, cut)
+    for copy in down_near[1]:
+        copy.wait_recv()
+    some(backward, cut, tiles)
 
     landed = (landed_down, landed_gate)
 
@@ -1558,19 +1579,6 @@
         at = columns(wide + t * tile, size)
         store_away(got_gu, two_stay, grad_gu, at)
 
-    def some(step_of, lo, hi):
-        top = min(hi, whole_tiles)
-        if top > lo:
-
-            @pl.loop(lo, top)
-            def _(t):
-                step_of(t, tile)
-
-        if hi > whole_tiles and rest:
-            step_of(whole_tiles, rest)
-
-    cut = min(3, whole_tiles)
-
     def rows_of(position):
         quarter = both // 4
         return pl.ds(pl.multiple_of(position * quarter, quarter), quarter)
@@ -1591,7 +1599,7 @@
         to = pl.ds(pl.multiple_of(t * 256, 256), 256)
         out_mid[to, :] = partial(grad_gu, gu_full, t)
 
-    some(reduce_down, 0, cut)
+    some(reduce_down, 0, min(2, whole_tiles))
 
     late[0].wait()
     first.wait_recv()
@@ -1635,7 +1643,7 @@
     own = local.start(grad_rows.at[rows_of(w.position), :], grad_mixed.at[w.position])
     store_pair = local.start(two, out_pair)
 
-    some(reduce_down, cut, tiles)
+    some(reduce_down, min(2, whole_tiles), tiles)
     own.wait()
     late[2].wait()
     late[3].wait()

time: 489 us -> 481 us (0.984)
  Pallas kernels: 482 us -> 474 us
    pallas_call x1, Pallas kernels: 154 us -> 144 us  [back(): pl.pallas_call(functools.partial(back_body, n), in_specs=[ANY] * 8 + [VME...]
where the time goes in v7:
time: 481 us
  Pallas kernels  474 us (99%)
  local copies, waits for them, and re-layouts  5.42 us (1%)
    pallas_call x1, Pallas kernels, front(): pl.pallas_call(functools.partial(front_body, n), in_specs=[ANY, ANY, VMEM...  202 us
    pallas_call x1, Pallas kernels, back(): pl.pallas_call(functools.partial(back_body, n), in_specs=[ANY] * 8 + [VME...  144 us
    pallas_call x1, Pallas kernels, ending(): pl.pallas_call(functools.partial(ending_body, n), in_specs=[VMEM] * 5 + [...  120 us

profile of v7, /device:TPU:0, one launch (start us, length us, event | category | flops | bytes accessed | tf_op | source)
XLA Modules:
  0.0 480.7 jit_solution(13786257007048157317)
XLA Ops:
  0.6 0.7 broadcast_in_dim.16
  1.4 0.1 copy.24
  1.5 0.7 fusion.4.valid
  2.3 201.6 %front.1 = (bf16[1024,1536]{1,0:T(8,128)(2,1)}, bf16[1024,512]{1,0:T(8,128)(2,1)}, bf16[1024,2816]{1,0:T(8,128)(2,1)}, bf16[1024,1408]{1,0:T(8,128)(2,1)}, bf16[...) custom-call(bf16[512,4096]{1,0:T(8,128)(2,1)} %context.3, ...), custom_call_target="tpu_custom_call" | custom-call | tf_op jit(solution)/shard_map/front/pallas_call | solution.py:1344
  203.9 144.1 %back.1 = (bf16[128,1408]{1,0:T(8,128)(2,1)}, bf16[128,1408]{1,0:T(8,128)(2,1)}, bf16[4,128,1408]{2,1,0:T(8,128)(2,1)}, bf16[4,128,1408]{2,1,0:T(8,128)(2,1)}, b...) custom-call(bf16[1024,1024]{1,0:T(8,128)(2,1)} %get-tuple-element.50, ...), custom_call_target="tpu_custom_call" | custom-call | tf_op jit(solution)/shard_map/back/pallas_call | solution.py:1762
  348.0 119.8 %ending.1 = (bf16[128,1536]{1,0:T(8,128)(2,1)}, bf16[128,512]{1,0:T(8,128)(2,1)}, bf16[128,1408]{1,0:T(8,128)(2,1)}, bf16[3,128,1536]{2,1,0:T(8,128)(2,1)}, bf16...) custom-call(bf16[512,1024]{1,0:T(8,128)(2,1)} %get-tuple-element.49., ...), custom_call_target="tpu_custom_call" | custom-call | tf_op jit(solution)/shard_map/ending/pallas_call | solution.py:699
  467.8 0.7 slice.9
  468.5 1.9 slice.8
  470.4 0.6 copy.25
  471.0 0.0 copy-start
  471.0 8.3 %finish.1 = (f32[2,128,1536]{2,1,0:T(8,128)}, f32[2,128,512]{2,1,0:T(8,128)}, f32[2,128,2816]{2,1,0:T(8,128)}, f32[2,128,1408]{2,1,0:T(8,128)}, f32[512,1,1024]{2,1,0:T(1,128)}, /*index=5*/f32[512,1,1024]{2,1,0:T(1,128)}) custom-call(bf16[128,1536]{1,0:T(8,128)(2,1)} %get-tuple-element.69.own_q, bf16[128,512]{1,0:T(8,128)(2,1)} %get-tuple-element.70.own_o, ...), custom_call_target="tpu_custom_call" | custom-call | tf_op jit(solution)/shard_map/finish/pallas_call | solution.py:773
  479.3 0.0 copy-done
  479.3 1.3 copy.27
Async XLA Ops:
  471.0 8.3 %copy-start = (f32[512,1024]{1,0:T(8,128)S(1)}, f32[512,1024]{1,0:T(8,128)}, u32[]{:S(2)}) copy-start(f32[512,1024]{1,0:T(8,128)} %get-tuple-element.118) | copy-start | bytes 6291460

commit v8 on v7

--- a/solution.py
+++ b/solution.py
@@ -395,7 +395,7 @@
 def ending_body(
     n, resid, mid, gains, gain_two, result_rows,
     pair_one, pair_grad, mixed_rows, grad_qkv_rows, qkv_weight, context, ctx_pieces, up_send, up_stay,
-    out_q, out_o, out_up, landed_q, landed_o, landed_up, out_grad, out_result, out_context, out_ctx,
+    out_q, out_o, out_up, landed_q, landed_o, landed_up, out_grad, out_result, out_context, out_ctx, out_gains,
     one, grad_two, mixed, grad_qkv, qkv_full, left_away, left_stay, part_send, part_own,
     part_got, low, home, partner_half, half_sum, far_half, whole, result_home,
     send_q, send_o, kept_q, kept_o, arrived_q, arrived_o, send_up, kept_up, arrived_up,
@@ -634,7 +634,8 @@
     total = term_sum[w.at].astype(f32)
     for mask in w.masks:
         total = total + term_landed[mask // 2].astype(f32)
-    out_ctx[...] = total
+    out_ctx[...] = total[:, :wide]
+    out_gains[...] = total[:, wide:]
     for copy in kept:
         copy.wait()
     wire.finish()
@@ -699,7 +700,7 @@
     return pl.pallas_call(
         functools.partial(ending_body, n),
         in_specs=[VMEM] * 5 + [ANY] * 9,
-        out_specs=[ANY] * 8 + [VMEM] * 2,
+        out_specs=[ANY] * 8 + [VMEM] * 3,
         out_shape=[
             shape((block, wide_q), bf16),
             shape((block, wide_o), bf16),
@@ -710,7 +711,8 @@
             shape((rows, depth), bf16),
             shape((rows, depth), bf16),
             shape((rows, count), f32),
-            shape((depth // 4 // n, context.shape[1] + LANES), f32),
+            shape((depth // 4 // n, context.shape[1]), f32),
+            shape((depth // 4 // n, LANES), f32),
         ],
         scratch_shapes=[pltpu.VMEM(dims, kind) for dims, kind in shapes]
         + [
@@ -1949,7 +1951,8 @@
             grad_home,
             result,
             sum_context,
-            ctx_total,
+            sum_ctx,
+            sum_gains,
         ) = ending(
             n,
             resid_in,
@@ -1967,6 +1970,7 @@
             up_send,
             up_stay,
         )
+        sum_ctx, sum_gains = sum_ctx.T, sum_gains[:, :2].T
         sum_qkv, sum_out, sum_gate_up, sum_down, grad_home, result = finish(
             (own_qkv, own_out, own_gate, own_up, own_down),
             (landed_qkv, landed_out, landed_gate, landed_up, landed_down),
@@ -2002,9 +2006,9 @@
         )
         result = (result.astype(f32) * valid_mask)[:, None]
         grad_home = grad_home[:, None]
-    ctx_total = ctx_total.T
-    sum_ctx = ctx_total[: ctx_weight.shape[0]]
-    sum_gains = ctx_total[ctx_weight.shape[0] : ctx_weight.shape[0] + 2]
+        ctx_total = ctx_total.T
+        sum_ctx = ctx_total[: ctx_weight.shape[0]]
+        sum_gains = ctx_total[ctx_weight.shape[0] : ctx_weight.shape[0] + 2]
 
     return (
         result,

time: 481 us -> 480 us (level)
  no operation moved by 1% of the time
where the time goes in v8:
time: 480 us
  Pallas kernels  474 us (99%)
    pallas_call x1, Pallas kernels, front(): pl.pallas_call(functools.partial(front_body, n), in_specs=[ANY, ANY, VMEM...  202 us
    pallas_call x1, Pallas kernels, back(): pl.pallas_call(functools.partial(back_body, n), in_specs=[ANY] * 8 + [VME...  144 us
    pallas_call x1, Pallas kernels, ending(): pl.pallas_call(functools.partial(ending_body, n), in_specs=[VMEM] * 5 + [...  120 us

profile of v8, /device:TPU:0, one launch (start us, length us, event | category | flops | bytes accessed | tf_op | source)
XLA Modules:
  0.0 479.7 jit_solution(10952616216236542854)
XLA Ops:
  0.6 0.7 broadcast_in_dim.16
  1.4 0.1 copy.24
  1.5 0.7 fusion.4.valid
  2.3 201.6 %front.1 = (bf16[1024,1536]{1,0:T(8,128)(2,1)}, bf16[1024,512]{1,0:T(8,128)(2,1)}, bf16[1024,2816]{1,0:T(8,128)(2,1)}, bf16[1024,1408]{1,0:T(8,128)(2,1)}, bf16[...) custom-call(bf16[512,4096]{1,0:T(8,128)(2,1)} %context.3, ...), custom_call_target="tpu_custom_call" | custom-call | tf_op jit(solution)/shard_map/front/pallas_call | solution.py:1346
  203.9 144.2 %back.1 = (bf16[128,1408]{1,0:T(8,128)(2,1)}, bf16[128,1408]{1,0:T(8,128)(2,1)}, bf16[4,128,1408]{2,1,0:T(8,128)(2,1)}, bf16[4,128,1408]{2,1,0:T(8,128)(2,1)}, b...) custom-call(bf16[1024,1024]{1,0:T(8,128)(2,1)} %get-tuple-element.51, ...), custom_call_target="tpu_custom_call" | custom-call | tf_op jit(solution)/shard_map/back/pallas_call | solution.py:1764
  348.0 119.8 %ending.1 = (bf16[128,1536]{1,0:T(8,128)(2,1)}, bf16[128,512]{1,0:T(8,128)(2,1)}, bf16[128,1408]{1,0:T(8,128)(2,1)}, bf16[3,128,1536]{2,1,0:T(8,128)(2,1)}, bf16...) custom-call(bf16[512,1024]{1,0:T(8,128)(2,1)} %get-tuple-element.50., ...), custom_call_target="tpu_custom_call" | custom-call | tf_op jit(solution)/shard_map/ending/pallas_call | solution.py:700
  467.9 0.7 slice_bitcast_fusion
  468.6 0.6 copy.25
  469.2 0.0 copy-start
  469.2 8.3 %finish.1 = (f32[2,128,1536]{2,1,0:T(8,128)}, f32[2,128,512]{2,1,0:T(8,128)}, f32[2,128,2816]{2,1,0:T(8,128)}, f32[2,128,1408]{2,1,0:T(8,128)}, f32[512,1,1024]{2,1,0:T(1,128)}, /*index=5*/f32[512,1,1024]{2,1,0:T(1,128)}) custom-call(bf16[128,1536]{1,0:T(8,128)(2,1)} %get-tuple-element.70.own_q, bf16[128,512]{1,0:T(8,128)(2,1)} %get-tuple-element.71.own_o, ...), custom_call_target="tpu_custom_call" | custom-call | tf_op jit(solution)/shard_map/finish/pallas_call | solution.py:775
  477.5 0.0 copy-done
  477.5 0.0 copy-start.1
  477.5 1.3 copy.28
  478.8 0.0 copy-done.1
  478.9 0.8 copy.29
Async XLA Ops:
  469.2 8.3 %copy-start = (f32[512,1024]{1,0:T(8,128)S(1)}, f32[512,1024]{1,0:T(8,128)}, u32[]{:S(2)}) copy-start(f32[512,1024]{1,0:T(8,128)} %get-tuple-element.120) | copy-start | bytes 6291460
  477.5 1.4 copy-start.1
